TPU v7x, 32 devices: a whole 2x2x4 slice. The times are simulated.
32 devices in a mesh: groups: 2 (over x), seq: 16 (over z, y, core).
Axes of the slice: x: 2, y: 2, z: 4, core: 2. Of those that a mesh axis runs over, the one named last changes fastest.
Arguments:
- query_rows: bfloat16 [8192, 2048], P(('groups', 'seq')), parts along dimension 0, may hold values from -6 to 6
- key_rows: bfloat16 [16384, 2048], P(('groups', 'seq')), parts along dimension 0, may hold values from -6 to 6
- value_rows: bfloat16 [16384, 2048], P(('groups', 'seq')), parts along dimension 0, may hold values from -6 to 6
- write_rate: float32 [16384, 16], P(('groups', 'seq')), parts along dimension 0, may hold values from 0 to 1
- log_gate: float32 [8192, 16], P(('groups', 'seq')), parts along dimension 0, may hold values from -1 to 0
- keep_mask: int32 [256, 4], P(('groups', 'seq')), parts along dimension 0, may hold values 0 or 1
- query_kernel: float32 [4, 2048], replicated, may hold values from -3 to 3
- key_kernel: float32 [4, 2048], replicated, may hold values from -3 to 3
- value_kernel: float32 [4, 2048], replicated, may hold values from -3 to 3
Outputs:
- head_outputs: bfloat16 [8192, 2048], P(('groups', 'seq')), parts along dimension 0
There are 2 independent parts, one for each index of `groups`. A program takes and returns all parts, laid end to end along the dimension named above; an argument that names none is the same for every part. Nothing has to cross between parts.
All inputs are finite; a program needn't handle non-finite values. No bound on the sum of `keep_mask` on one device may be relied on, other than what follows from the above.
Results may differ from a plain program's by a relative error of at most 0.001.
Values may be sent and summed in bfloat16 or wider, within the bound.
No kernel may reach another device: no remote copies, remote signals or barrier semaphores. Data moves between devices by JAX's collectives and lax.ppermute only.
A program may use at most 128 MiB of HBM per device.

v0:
```python
import jax
import jax.numpy as jnp
from jax import lax
from jax.sharding import PartitionSpec as P

NH = 2
SPAN = 64
BLOCK = 16


HIGHEST = lax.Precision.HIGHEST


def shifted(value, axis, steps):
    count = lax.axis_size(axis)
    first, last = (max(0, -steps), min(count, count - steps))
    return lax.ppermute(value, axis, [(source, source + steps) for source in range(first, last)])


def conv_silu(leading, current, kernel):
    joined = jnp.concatenate([leading, current], axis=0).astype(jnp.float32)
    length = current.shape[0]
    total = kernel[0] * joined[0:length]
    for offset in range(1, 4):
        total = total + kernel[offset] * joined[offset : offset + length]
    return jax.nn.silu(total)


def unit_heads(rows_in, heads):
    shaped = rows_in.reshape(rows_in.shape[0], heads, -1)
    return shaped * lax.rsqrt(jnp.sum(shaped * shaped, axis=-1, keepdims=True) + 1e-06)


def to_blocks(rows_in, per_block):
    shaped = rows_in.reshape(
        rows_in.shape[0] // per_block, per_block, rows_in.shape[1], rows_in.shape[2]
    )
    return shaped.transpose(0, 2, 1, 3)


def step_scalars(write_rate, log_gate, keep_mask, heads):
    filler = jnp.zeros((log_gate.shape[0], NH - 1, heads), jnp.float32)
    step_log = jnp.concatenate([log_gate[:, None, :], filler], axis=1).reshape(-1, heads)
    keep_steps = jnp.repeat(keep_mask.astype(jnp.float32), BLOCK, axis=1).reshape(-1)
    rates = write_rate * keep_steps[:, None]
    rate_blocks = rates.reshape(-1, SPAN, heads).transpose(0, 2, 1)
    log_blocks = step_log.reshape(-1, SPAN, heads).transpose(0, 2, 1)
    return (rate_blocks, log_blocks)


def unit_lower_inverse(lower_part, steps_here):
    negated = -lower_part
    inverse = jnp.eye(steps_here, dtype=jnp.float32) + negated
    power = negated
    reach = 2
    while reach < steps_here:
        power = jnp.einsum("...ij,...jk->...ik", power, power, precision=HIGHEST)
        inverse = inverse + jnp.einsum("...ij,...jk->...ik", inverse, power, precision=HIGHEST)
        reach = reach * 2
    return inverse


def span_terms(query_block, key_block, value_block, rate_block, log_block):
    steps_here = key_block.shape[-2]
    head_size = key_block.shape[-1]
    readers = query_block.shape[-2]
    stride = steps_here // readers
    cumlog = jnp.cumsum(log_block, axis=-1)
    index_of_row = lax.broadcasted_iota(jnp.int32, (steps_here, steps_here), 0)
    col_index = lax.broadcasted_iota(jnp.int32, (steps_here, steps_here), 1)
    strictly_below = col_index < index_of_row
    spread = cumlog[..., :, None] - cumlog[..., None, :]
    key_gram = jnp.einsum("...id,...jd->...ij", key_block, key_block, precision=HIGHEST)
    lower_part = jnp.where(
        strictly_below,
        rate_block[..., :, None] * jnp.exp(jnp.where(strictly_below, spread, 0.0)) * key_gram,
        0.0,
    )
    inverse = unit_lower_inverse(lower_part, steps_here)
    targets = jnp.concatenate(
        [
            (rate_block * jnp.exp(cumlog))[..., None] * key_block,
            rate_block[..., None] * value_block,
        ],
        axis=-1,
    )
    solved = jnp.einsum("...ij,...jd->...id", inverse, targets, precision=HIGHEST)
    erase_rows = solved[..., :head_size]
    fresh_rows = solved[..., head_size:]
    final_log = cumlog[..., -1:]
    faded_keys = jnp.exp(final_log - cumlog)[..., None] * key_block
    read_log = cumlog[..., stride - 1 :: stride]
    read_step = lax.broadcasted_iota(jnp.int32, (readers, steps_here), 0) * stride + stride - 1
    read_col = lax.broadcasted_iota(jnp.int32, (readers, steps_here), 1)
    visible = read_col <= read_step
    read_spread = read_log[..., :, None] - cumlog[..., None, :]
    scores = jnp.einsum("...td,...jd->...tj", query_block, key_block, precision=HIGHEST)
    inner = jnp.where(visible, jnp.exp(jnp.where(visible, read_spread, 0.0)) * scores, 0.0)
    return (
        erase_rows,
        fresh_rows,
        faded_keys,
        inner,
        jnp.exp(read_log),
        jnp.exp(final_log[..., 0]),
    )


def span_read(state, pieces):
    erase_rows, fresh_rows, faded_keys, inner, read_scale, fade, query_block = pieces
    pseudo = fresh_rows - jnp.einsum("hcd,hde->hce", erase_rows, state, precision=HIGHEST)
    carried = read_scale[..., None] * jnp.einsum(
        "htd,hde->hte", query_block, state, precision=HIGHEST
    )
    output = carried + jnp.einsum("htc,hce->hte", inner, pseudo, precision=HIGHEST)
    state = fade[:, None, None] * state + jnp.einsum(
        "hcd,hce->hde", faded_keys, pseudo, precision=HIGHEST
    )
    return (state, output)


def compose(mapped, pieces):
    erase_rows, fresh_rows, faded_keys, fade = pieces
    pseudo = jnp.concatenate([jnp.zeros_like(fresh_rows), fresh_rows], axis=-1)
    pseudo = pseudo - jnp.einsum("hcd,hde->hce", erase_rows, mapped, precision=HIGHEST)
    mapped = fade[:, None, None] * mapped + jnp.einsum(
        "hcd,hce->hde", faded_keys, pseudo, precision=HIGHEST
    )
    return (mapped, None)


def local(
    query_rows,
    key_rows,
    value_rows,
    write_rate,
    log_gate,
    keep_mask,
    query_kernel,
    key_kernel,
    value_kernel,
):
    heads = write_rate.shape[1]
    tails = jnp.stack([query_rows[-3:], key_rows[-3:], value_rows[-3:]], axis=0)
    rims = shifted(tails, "seq", 1)
    query_unit = unit_heads(conv_silu(rims[0], query_rows, query_kernel), heads)
    key_unit = unit_heads(conv_silu(rims[1], key_rows, key_kernel), heads)
    value_feat = conv_silu(rims[2], value_rows, value_kernel).reshape(
        value_rows.shape[0], heads, -1
    )
    rate_blocks, log_blocks = step_scalars(write_rate, log_gate, keep_mask, heads)
    query_blocks = to_blocks(query_unit, SPAN // NH)
    key_blocks = to_blocks(key_unit, SPAN)
    value_blocks = to_blocks(value_feat, SPAN)
    erase_rows, fresh_rows, faded_keys, inner, read_scale, fade = span_terms(
        query_blocks, key_blocks, value_blocks, rate_blocks, log_blocks
    )
    head_size = key_blocks.shape[-1]
    identity_map = jnp.broadcast_to(
        jnp.eye(head_size, dtype=jnp.float32), (heads, head_size, head_size)
    )
    zero_state = jnp.zeros((heads, head_size, head_size), jnp.float32)
    start_map = jnp.concatenate([identity_map, zero_state], axis=-1)
    mapped, _ = lax.scan(compose, start_map, (erase_rows, fresh_rows, faded_keys, fade))
    linear_map = mapped[..., :head_size]
    offset_map = mapped[..., head_size:]
    device_count = lax.axis_size("seq")

    def relay(turn_index, incoming):
        ending = jnp.einsum("hde,hef->hdf", linear_map, incoming, precision=HIGHEST) + offset_map
        return shifted(ending, "seq", 1)

    entry_state = lax.fori_loop(0, device_count - 1, relay, zero_state)
    _, outputs = lax.scan(
        span_read,
        entry_state,
        (erase_rows, fresh_rows, faded_keys, inner, read_scale, fade, query_blocks),
    )
    return outputs.transpose(0, 2, 1, 3).reshape(-1, heads * head_size).astype(jnp.bfloat16)


def solution(mesh):
    return jax.shard_map(
        local,
        mesh=mesh,
        in_specs=(
            P(("groups", "seq"), None),
            P(("groups", "seq"), None),
            P(("groups", "seq"), None),
            P(("groups", "seq"), None),
            P(("groups", "seq"), None),
            P(("groups", "seq"), None),
            P(),
            P(),
            P(),
        ),
        out_specs=P(("groups", "seq"), None),
        check_vma=False,
    )
```

profile of v0, /device:TPU:24, one launch (start us, length us, event | category | flops | bytes accessed | tf_op | source)
XLA Modules:
  0.0 590.7 jit_solution(17820267615563124761)
XLA Ops:
  15.4 4.1 multiply_bitcast_fusion.1
  22.4 3.4 reduce_sum.18
  26.0 3.1 copy.51
  29.1 9.4 %fusion.34 = f32[8,16,64,64]{3,2,1,0:T(8,128)S(1)} fusion(f32[8,64,16,128]{3,2,1,0:T(8,128)S(1)} %bitcast.175, f32[8,64,16]{1,2,0:T(8,128)S(1)} %copy.39), kind=kOutput, calls=%fused_computation.55 | convolution fusion | flops 806354944 | bytes 6324224 | tf_op jit(solution)/shard_map/...id,...jd->...ij/dot_general | solution.py:73
  38.5 8.3 %fusion.42 = f32[8,16,64,64]{3,2,1,0:T(8,128)S(1)} fusion(f32[8,16,64,64]{3,2,1,0:T(8,128)S(1)} %fusion.34, f32[8,16,64]{2,1,0:T(8,128)S(1)} %reduce_window_sum.11, f32[8,16,64]{2,1,0:T(8,128)S(1)} %bitcast.188, pred[64,64]{1,0:T(8,128)(4,1)S(1)} %get-tuple-element.213), kind=kOutput, calls=%fused_computation.70 | convolution fusion | flops 405798912 | bytes 4263936 | tf_op jit(solution)/shard_map/...ij,...jk->...ik/dot_general | solution.py:57
  46.9 5.2 fusion.73
  52.1 8.3 %add_add_fusion = f32[8,16,64,64]{3,2,1,0:T(8,128)S(1)} fusion(f32[8,16,64,64]{3,2,1,0:T(8,128)S(1)} %fusion.42, f32[8,16,64,64]{3,2,1,0:T(8,128)S(1)} %fusion.34, f32[8,16,64]{2,1,0:T(8,128)S(1)} %reduce_window_sum.11, f32[8,16,64]{2,1,0:T(8,128)S(1)} %bitcast.189, f32[64,64]{1,0:T(8,128)S(1)} %get-tuple-element.214, pred[64,64]{1,0:T(8,128)(4,1)S(1)} %get-tuple-element.213), kind=kOutput, calls=%fused_computation.64 | convolution fusion | flops 410517504 | bytes 6377472 | tf_op jit(solution)/shard_map/...ij,...jk->...ik/dot_general | solution.py:58
  60.4 5.4 fusion.74
  65.8 5.5 convolution_add_fusion.4
  71.3 5.3 fusion.76
  76.6 6.4 %fusion.75 = f32[8,16,64,64]{3,2,1,0:T(8,128)} fusion(f32[8,16,64,64]{3,2,1,0:T(8,128)S(1)} %convolution_add_fusion.4, f32[8,16,64,64]{3,2,1,0:T(8,128)S(1)} %fusion.74), kind=kOutput, calls=%fused_computation.133 | convolution fusion | flops 402653184 | bytes 6291456 | tf_op jit(solution)/shard_map/...ij,...jk->...ik/dot_general | solution.py:58
  83.0 5.3 fusion.77
  88.3 7.9 %convolution_add_fusion.3 = f32[8,16,64,64]{3,2,1,0:T(8,128)} fusion(f32[8,16,64,64]{3,2,1,0:T(8,128)S(1)} %fusion.76, f32[8,16,64,64]{3,2,1,0:T(8,128)S(1)} %convolution_add_fusion.4, f32[8,16,64,64]{3,2,1,0:T(8,128)} %fusion.75), kind=kOutput, calls=%fused_computation.67 | convolution fusion | flops 403701760 | bytes 8388608 | tf_op jit(solution)/shard_map/...ij,...jk->...ik/dot_general | solution.py:58
  103.9 5.9 %fusion.78 = f32[8,16,64,64]{3,2,1,0:T(8,128)} fusion(f32[8,16,64,64]{3,2,1,0:T(8,128)S(1)} %copy-done.2, f32[8,16,64,64]{3,2,1,0:T(8,128)S(1)} %fusion.77), kind=kOutput, calls=%fused_computation.136 | convolution fusion | flops 402653184 | bytes 6291456 | tf_op jit(solution)/shard_map/...ij,...jk->...ik/dot_general | solution.py:58
  109.8 6.3 %bitcast_multiply_fusion.1 = (f32[8,16,64,128]{3,2,1,0:T(8,128)}, f32[8,16,64,128]{3,2,1,0:T(8,128)}) fusion(f32[8,64,16,128]{3,2,1,0:T(8,128)S(1)} %bitcast.176, f32[8,16,64]{2,1,0:T(8,128)S(1)} %get-tuple-element.194, f32[8,64,16]{1,2,0:T(8,128)S(1)} %copy.39, f32[8,16,64]{2,1,0:T(8,128)S(1)} %get-tuple-element.195), kind=kLoop, calls=%fused_computation.54 | loop fusion | flops 3145728 | bytes 12681216 | tf_op jit(solution)/shard_map/mul | solution.py:82
  116.1 15.7 %fusion.22 = f32[8,16,64,256]{3,2,1,0:T(8,128)} fusion(f32[8,16,64,128]{3,2,1,0:T(8,128)} %bitcast_multiply_fusion, f32[8,16,64,128]{3,2,1,0:T(8,128)} %get-tuple-element.190, f32[8,16,64,64]{3,2,1,0:T(8,128)S(1)} %copy-done.2, f32[8,16,64,64]{3,2,1,0:T(8,128)} %fusion.78), kind=kOutput, calls=%fused_computation.33 | convolution fusion | flops 1613234176 | bytes 20971520 | tf_op jit(solution)/shard_map/...ij,...jd->...id/dot_general | solution.py:87
  131.8 8.3 %fusion.68 = (f32[8,16,64,128]{3,2,1,0:T(8,128)}, f32[8,16,64,128]{3,2,1,0:T(8,128)}) fusion(f32[8,16,64,256]{3,2,1,0:T(8,128)} %fusion.22), kind=kLoop, calls=%fused_computation.126 | loop fusion | bytes 16777216 | tf_op jit(solution)/shard_map/slice | solution.py:88
  140.2 56.1 %while.32 = (s32[]{:T(128)}, f32[16,128,256]{2,1,0:T(8,128)S(1)}, f32[8,16]{1,0:T(8,128)S(1)}, f32[8,16,64,128]{3,2,1,0:T(8,128)}, f32[8,16,64,128]{3,2,1,0:T(8,128)}, /*index=5*/f32[8,16,64,128]{3,2,1,0:T(8,128)}, s32[]{:T(128)}) while((s32[]{:T(128)}, f32[16,128,256]{2,1,0:T(8,128)S(1)}, f32[8,16]{1,0:T(8,128)S(1)}, ...), condition=%wide.region_3.4_spmd, body=%wide.region_2.3_spmd.sunk | while | flops 806617088 | bytes 11011349 | solution.py:164
  143.8 3.5 multiply_add_fusion.3
  150.8 3.5 multiply_add_fusion.3
  157.8 3.5 multiply_add_fusion.3
  164.8 3.5 multiply_add_fusion.3
  171.7 3.5 multiply_add_fusion.3
  178.7 3.5 multiply_add_fusion.3
  185.7 3.5 multiply_add_fusion.3
  192.7 3.5 multiply_add_fusion.3
  207.0 8.6 %multiply_select_fusion = f32[8,16,32,64]{3,2,1,0:T(8,128)} fusion(f32[8,64,16,128]{3,2,1,0:T(8,128)S(1)} %bitcast.177, f32[8,64,16]{1,2,0:T(8,128)S(1)} %copy.39, f32[8,16,64]{2,1,0:T(8,128)S(1)} %reduce_window_sum.11, f32[8,16,32]{2,1,0:T(8,128)S(1)} %slice.134, pred[32,64]{1,0:T(8,128)(4,1)S(1)} %copy-done.9, f32[8,16,32,128]{3,1,2,0:T(8,128)S(1)} %fusion.43), kind=kOutput, calls=%fused_computation.82 | convolution fusion | flops 404750336 | bytes 7424000 | tf_op jit(solution)/shard_map/...td,...jd->...tj/dot_general | solution.py:97
  215.7 290.4 %while.33 = (s32[]{:T(128)}, f32[16,128,128]{2,1,0:T(8,128)S(1)}, f32[16,128,128]{2,1,0:T(8,128)S(1)}, f32[16,128,128]{2,1,0:T(8,128)S(1)}, s32[]{:T(128)}) while((s32[]{:T(128)}, f32[16,128,128]{2,1,0:T(8,128)S(1)}, f32[16,128,128]{2,1,0:T(8,128)S(1)}, f32[16,128,128]{2,1,0:T(8,128)S(1)}, s32[]{:T(128)}) %tuple.75), condition=%wide.region_5.6_spmd, body=%wide.region_4.5_spmd.sunk | while | flops 402915328 | bytes 8388709 | solution.py:173
  218.1 3.5 collective-permute-start
  221.6 13.7 %collective-permute-done = f32[16,128,128]{2,1,0:T(8,128)S(1)} collective-permute-done((f32[16,128,128]{2,1,0:T(8,128)}, f32[16,128,128]{2,1,0:T(8,128)S(1)}, u32[]{:S(2)}, u32[]{:S(2)}) %collective-permute-start) | collective-permute-done | bytes 1048608 | tf_op jit(solution)/shard_map/while/body/eval_jaxpr/ppermute | solution.py:17
  239.3 15.3 %collective-permute-done = f32[16,128,128]{2,1,0:T(8,128)S(1)} collective-permute-done((f32[16,128,128]{2,1,0:T(8,128)}, f32[16,128,128]{2,1,0:T(8,128)S(1)}, u32[]{:S(2)}, u32[]{:S(2)}) %collective-permute-start) | collective-permute-done | bytes 1048608 | tf_op jit(solution)/shard_map/while/body/eval_jaxpr/ppermute | solution.py:17
  258.7 15.3 %collective-permute-done = f32[16,128,128]{2,1,0:T(8,128)S(1)} collective-permute-done((f32[16,128,128]{2,1,0:T(8,128)}, f32[16,128,128]{2,1,0:T(8,128)S(1)}, u32[]{:S(2)}, u32[]{:S(2)}) %collective-permute-start) | collective-permute-done | bytes 1048608 | tf_op jit(solution)/shard_map/while/body/eval_jaxpr/ppermute | solution.py:17
  278.0 15.3 %collective-permute-done = f32[16,128,128]{2,1,0:T(8,128)S(1)} collective-permute-done((f32[16,128,128]{2,1,0:T(8,128)}, f32[16,128,128]{2,1,0:T(8,128)S(1)}, u32[]{:S(2)}, u32[]{:S(2)}) %collective-permute-start) | collective-permute-done | bytes 1048608 | tf_op jit(solution)/shard_map/while/body/eval_jaxpr/ppermute | solution.py:17
  297.4 15.3 %collective-permute-done = f32[16,128,128]{2,1,0:T(8,128)S(1)} collective-permute-done((f32[16,128,128]{2,1,0:T(8,128)}, f32[16,128,128]{2,1,0:T(8,128)S(1)}, u32[]{:S(2)}, u32[]{:S(2)}) %collective-permute-start) | collective-permute-done | bytes 1048608 | tf_op jit(solution)/shard_map/while/body/eval_jaxpr/ppermute | solution.py:17
  316.7 15.3 %collective-permute-done = f32[16,128,128]{2,1,0:T(8,128)S(1)} collective-permute-done((f32[16,128,128]{2,1,0:T(8,128)}, f32[16,128,128]{2,1,0:T(8,128)S(1)}, u32[]{:S(2)}, u32[]{:S(2)}) %collective-permute-start) | collective-permute-done | bytes 1048608 | tf_op jit(solution)/shard_map/while/body/eval_jaxpr/ppermute | solution.py:17
  336.0 15.3 %collective-permute-done = f32[16,128,128]{2,1,0:T(8,128)S(1)} collective-permute-done((f32[16,128,128]{2,1,0:T(8,128)}, f32[16,128,128]{2,1,0:T(8,128)S(1)}, u32[]{:S(2)}, u32[]{:S(2)}) %collective-permute-start) | collective-permute-done | bytes 1048608 | tf_op jit(solution)/shard_map/while/body/eval_jaxpr/ppermute | solution.py:17
  355.4 15.3 %collective-permute-done = f32[16,128,128]{2,1,0:T(8,128)S(1)} collective-permute-done((f32[16,128,128]{2,1,0:T(8,128)}, f32[16,128,128]{2,1,0:T(8,128)S(1)}, u32[]{:S(2)}, u32[]{:S(2)}) %collective-permute-start) | collective-permute-done | bytes 1048608 | tf_op jit(solution)/shard_map/while/body/eval_jaxpr/ppermute | solution.py:17
  374.7 15.3 %collective-permute-done = f32[16,128,128]{2,1,0:T(8,128)S(1)} collective-permute-done((f32[16,128,128]{2,1,0:T(8,128)}, f32[16,128,128]{2,1,0:T(8,128)S(1)}, u32[]{:S(2)}, u32[]{:S(2)}) %collective-permute-start) | collective-permute-done | bytes 1048608 | tf_op jit(solution)/shard_map/while/body/eval_jaxpr/ppermute | solution.py:17
  394.1 15.3 %collective-permute-done = f32[16,128,128]{2,1,0:T(8,128)S(1)} collective-permute-done((f32[16,128,128]{2,1,0:T(8,128)}, f32[16,128,128]{2,1,0:T(8,128)S(1)}, u32[]{:S(2)}, u32[]{:S(2)}) %collective-permute-start) | collective-permute-done | bytes 1048608 | tf_op jit(solution)/shard_map/while/body/eval_jaxpr/ppermute | solution.py:17
  413.4 15.3 %collective-permute-done = f32[16,128,128]{2,1,0:T(8,128)S(1)} collective-permute-done((f32[16,128,128]{2,1,0:T(8,128)}, f32[16,128,128]{2,1,0:T(8,128)S(1)}, u32[]{:S(2)}, u32[]{:S(2)}) %collective-permute-start) | collective-permute-done | bytes 1048608 | tf_op jit(solution)/shard_map/while/body/eval_jaxpr/ppermute | solution.py:17
  432.7 15.3 %collective-permute-done = f32[16,128,128]{2,1,0:T(8,128)S(1)} collective-permute-done((f32[16,128,128]{2,1,0:T(8,128)}, f32[16,128,128]{2,1,0:T(8,128)S(1)}, u32[]{:S(2)}, u32[]{:S(2)}) %collective-permute-start) | collective-permute-done | bytes 1048608 | tf_op jit(solution)/shard_map/while/body/eval_jaxpr/ppermute | solution.py:17
  452.1 15.3 %collective-permute-done = f32[16,128,128]{2,1,0:T(8,128)S(1)} collective-permute-done((f32[16,128,128]{2,1,0:T(8,128)}, f32[16,128,128]{2,1,0:T(8,128)S(1)}, u32[]{:S(2)}, u32[]{:S(2)}) %collective-permute-start) | collective-permute-done | bytes 1048608 | tf_op jit(solution)/shard_map/while/body/eval_jaxpr/ppermute | solution.py:17
  471.4 15.3 %collective-permute-done = f32[16,128,128]{2,1,0:T(8,128)S(1)} collective-permute-done((f32[16,128,128]{2,1,0:T(8,128)}, f32[16,128,128]{2,1,0:T(8,128)S(1)}, u32[]{:S(2)}, u32[]{:S(2)}) %collective-permute-start) | collective-permute-done | bytes 1048608 | tf_op jit(solution)/shard_map/while/body/eval_jaxpr/ppermute | solution.py:17
  490.8 15.3 %collective-permute-done = f32[16,128,128]{2,1,0:T(8,128)S(1)} collective-permute-done((f32[16,128,128]{2,1,0:T(8,128)}, f32[16,128,128]{2,1,0:T(8,128)S(1)}, u32[]{:S(2)}, u32[]{:S(2)}) %collective-permute-start) | collective-permute-done | bytes 1048608 | tf_op jit(solution)/shard_map/while/body/eval_jaxpr/ppermute | solution.py:17
  506.0 81.4 %while.34 = (s32[]{:T(128)}, f32[16,128,128]{2,1,0:T(8,128)S(1)}, bf16[8,16,32,128]{3,2,1,0:T(8,128)(2,1)}, f32[8,16]{1,0:T(8,128)}, f32[8,16,64,128]{3,2,1,0:T(...) while((s32[]{:T(128)}, f32[16,128,128]{2,1,0:T(8,128)S(1)}, ...), condition=%wide.region_8.9_spmd, body=%wide.region_7.8_spmd.sunk | while | flops 554434560 | bytes 8660277 | solution.py:174
  513.2 3.0 convolution_add_fusion.8
  523.3 3.0 convolution_add_fusion.8
  574.2 3.0 convolution_add_fusion.8
  (176 shorter events, 197.5 us)
Async XLA Ops:
  1.6 12.0 %collective-permute-start.1 = (bf16[3,3,2048]{2,1,0:T(4,128)(2,1)S(1)}, bf16[3,3,2048]{2,1,0:T(4,128)(2,1)S(1)}, u32[]{:S(2)}, u32[]{:S(2)}) collective-permute-start(bf16[3,3,2048]{2,1,0:T(4,128)(2,1)S(1)} %pad_maximum_fusion), channel_id=1, source_target_pairs={{0,1},{1,2},{2,3},{3,4},{4,5},{5,6},{6,7},{7,8},{8,9},{9,10},{10,1... | collective-permute-start | bytes 110600 | tf_op jit(solution)/shard_map/ppermute | solution.py:17
  13.2 1.6 copy-start.4
  29.1 80.8 %copy-start = (f32[64,8,16,128]{3,2,1,0:T(8,128)}, f32[64,8,16,128]{3,2,1,0:T(8,128)S(1)}, u32[]{:S(2)}) copy-start(f32[64,8,16,128]{3,2,1,0:T(8,128)S(1)} %copy.51) | copy-start | bytes 12582916
  88.3 8.0 %copy-start.5 = (bf16[512,2048]{1,0:T(8,128)(2,1)S(1)}, bf16[512,2048]{1,0:T(8,128)(2,1)}, u32[]{:S(2)}) copy-start(bf16[512,2048]{1,0:T(8,128)(2,1)} %param.17) | copy-start | bytes 6291460
  100.5 3.4 copy-start.2
  196.2 0.6 copy-start.10
  196.8 1.3 copy-start.6
  196.8 1.7 copy-start.7
  196.8 1.7 copy-start.8
  204.3 2.7 copy-start.1
  204.3 2.7 copy-start.9
  207.0 8.7 %copy-start.3 = (f32[16,128,128]{2,1,0:T(8,128)S(1)}, f32[16,128,128]{2,1,0:T(8,128)}, u32[]{:S(2)}) copy-start(f32[16,128,128]{2,1,0:T(8,128)} %get-tuple-element.361) | copy-start | bytes 3145732
  218.1 17.2 %collective-permute-start = (f32[16,128,128]{2,1,0:T(8,128)}, f32[16,128,128]{2,1,0:T(8,128)S(1)}, u32[]{:S(2)}, u32[]{:S(2)}) collective-permute-start(f32[16,128,128]{2,1,0:T(8,128)} %convolution_add_fusion.7), channel_id=1, source_target_pairs={{0,1},{1,2},{2,3},{3,4},{4,5},{5,6},{6,7},{7,8},{8,9},{9,10},{10,1... | collective-permute-start | bytes 3145736 | tf_op jit(solution)/shard_map/while/body/eval_jaxpr/ppermute | solution.py:17
  237.4 17.2 %collective-permute-start = (f32[16,128,128]{2,1,0:T(8,128)}, f32[16,128,128]{2,1,0:T(8,128)S(1)}, u32[]{:S(2)}, u32[]{:S(2)}) collective-permute-start(f32[16,128,128]{2,1,0:T(8,128)} %convolution_add_fusion.7), channel_id=1, source_target_pairs={{0,1},{1,2},{2,3},{3,4},{4,5},{5,6},{6,7},{7,8},{8,9},{9,10},{10,1... | collective-permute-start | bytes 3145736 | tf_op jit(solution)/shard_map/while/body/eval_jaxpr/ppermute | solution.py:17
  256.8 17.2 %collective-permute-start = (f32[16,128,128]{2,1,0:T(8,128)}, f32[16,128,128]{2,1,0:T(8,128)S(1)}, u32[]{:S(2)}, u32[]{:S(2)}) collective-permute-start(f32[16,128,128]{2,1,0:T(8,128)} %convolution_add_fusion.7), channel_id=1, source_target_pairs={{0,1},{1,2},{2,3},{3,4},{4,5},{5,6},{6,7},{7,8},{8,9},{9,10},{10,1... | collective-permute-start | bytes 3145736 | tf_op jit(solution)/shard_map/while/body/eval_jaxpr/ppermute | solution.py:17
  276.1 17.2 %collective-permute-start = (f32[16,128,128]{2,1,0:T(8,128)}, f32[16,128,128]{2,1,0:T(8,128)S(1)}, u32[]{:S(2)}, u32[]{:S(2)}) collective-permute-start(f32[16,128,128]{2,1,0:T(8,128)} %convolution_add_fusion.7), channel_id=1, source_target_pairs={{0,1},{1,2},{2,3},{3,4},{4,5},{5,6},{6,7},{7,8},{8,9},{9,10},{10,1... | collective-permute-start | bytes 3145736 | tf_op jit(solution)/shard_map/while/body/eval_jaxpr/ppermute | solution.py:17
  295.4 17.2 %collective-permute-start = (f32[16,128,128]{2,1,0:T(8,128)}, f32[16,128,128]{2,1,0:T(8,128)S(1)}, u32[]{:S(2)}, u32[]{:S(2)}) collective-permute-start(f32[16,128,128]{2,1,0:T(8,128)} %convolution_add_fusion.7), channel_id=1, source_target_pairs={{0,1},{1,2},{2,3},{3,4},{4,5},{5,6},{6,7},{7,8},{8,9},{9,10},{10,1... | collective-permute-start | bytes 3145736 | tf_op jit(solution)/shard_map/while/body/eval_jaxpr/ppermute | solution.py:17
  314.8 17.2 %collective-permute-start = (f32[16,128,128]{2,1,0:T(8,128)}, f32[16,128,128]{2,1,0:T(8,128)S(1)}, u32[]{:S(2)}, u32[]{:S(2)}) collective-permute-start(f32[16,128,128]{2,1,0:T(8,128)} %convolution_add_fusion.7), channel_id=1, source_target_pairs={{0,1},{1,2},{2,3},{3,4},{4,5},{5,6},{6,7},{7,8},{8,9},{9,10},{10,1... | collective-permute-start | bytes 3145736 | tf_op jit(solution)/shard_map/while/body/eval_jaxpr/ppermute | solution.py:17
  334.1 17.2 %collective-permute-start = (f32[16,128,128]{2,1,0:T(8,128)}, f32[16,128,128]{2,1,0:T(8,128)S(1)}, u32[]{:S(2)}, u32[]{:S(2)}) collective-permute-start(f32[16,128,128]{2,1,0:T(8,128)} %convolution_add_fusion.7), channel_id=1, source_target_pairs={{0,1},{1,2},{2,3},{3,4},{4,5},{5,6},{6,7},{7,8},{8,9},{9,10},{10,1... | collective-permute-start | bytes 3145736 | tf_op jit(solution)/shard_map/while/body/eval_jaxpr/ppermute | solution.py:17
  353.5 17.2 %collective-permute-start = (f32[16,128,128]{2,1,0:T(8,128)}, f32[16,128,128]{2,1,0:T(8,128)S(1)}, u32[]{:S(2)}, u32[]{:S(2)}) collective-permute-start(f32[16,128,128]{2,1,0:T(8,128)} %convolution_add_fusion.7), channel_id=1, source_target_pairs={{0,1},{1,2},{2,3},{3,4},{4,5},{5,6},{6,7},{7,8},{8,9},{9,10},{10,1... | collective-permute-start | bytes 3145736 | tf_op jit(solution)/shard_map/while/body/eval_jaxpr/ppermute | solution.py:17
  372.8 17.2 %collective-permute-start = (f32[16,128,128]{2,1,0:T(8,128)}, f32[16,128,128]{2,1,0:T(8,128)S(1)}, u32[]{:S(2)}, u32[]{:S(2)}) collective-permute-start(f32[16,128,128]{2,1,0:T(8,128)} %convolution_add_fusion.7), channel_id=1, source_target_pairs={{0,1},{1,2},{2,3},{3,4},{4,5},{5,6},{6,7},{7,8},{8,9},{9,10},{10,1... | collective-permute-start | bytes 3145736 | tf_op jit(solution)/shard_map/while/body/eval_jaxpr/ppermute | solution.py:17
  392.1 17.2 %collective-permute-start = (f32[16,128,128]{2,1,0:T(8,128)}, f32[16,128,128]{2,1,0:T(8,128)S(1)}, u32[]{:S(2)}, u32[]{:S(2)}) collective-permute-start(f32[16,128,128]{2,1,0:T(8,128)} %convolution_add_fusion.7), channel_id=1, source_target_pairs={{0,1},{1,2},{2,3},{3,4},{4,5},{5,6},{6,7},{7,8},{8,9},{9,10},{10,1... | collective-permute-start | bytes 3145736 | tf_op jit(solution)/shard_map/while/body/eval_jaxpr/ppermute | solution.py:17
  411.5 17.2 %collective-permute-start = (f32[16,128,128]{2,1,0:T(8,128)}, f32[16,128,128]{2,1,0:T(8,128)S(1)}, u32[]{:S(2)}, u32[]{:S(2)}) collective-permute-start(f32[16,128,128]{2,1,0:T(8,128)} %convolution_add_fusion.7), channel_id=1, source_target_pairs={{0,1},{1,2},{2,3},{3,4},{4,5},{5,6},{6,7},{7,8},{8,9},{9,10},{10,1... | collective-permute-start | bytes 3145736 | tf_op jit(solution)/shard_map/while/body/eval_jaxpr/ppermute | solution.py:17
  430.8 17.2 %collective-permute-start = (f32[16,128,128]{2,1,0:T(8,128)}, f32[16,128,128]{2,1,0:T(8,128)S(1)}, u32[]{:S(2)}, u32[]{:S(2)}) collective-permute-start(f32[16,128,128]{2,1,0:T(8,128)} %convolution_add_fusion.7), channel_id=1, source_target_pairs={{0,1},{1,2},{2,3},{3,4},{4,5},{5,6},{6,7},{7,8},{8,9},{9,10},{10,1... | collective-permute-start | bytes 3145736 | tf_op jit(solution)/shard_map/while/body/eval_jaxpr/ppermute | solution.py:17
  450.2 17.2 %collective-permute-start = (f32[16,128,128]{2,1,0:T(8,128)}, f32[16,128,128]{2,1,0:T(8,128)S(1)}, u32[]{:S(2)}, u32[]{:S(2)}) collective-permute-start(f32[16,128,128]{2,1,0:T(8,128)} %convolution_add_fusion.7), channel_id=1, source_target_pairs={{0,1},{1,2},{2,3},{3,4},{4,5},{5,6},{6,7},{7,8},{8,9},{9,10},{10,1... | collective-permute-start | bytes 3145736 | tf_op jit(solution)/shard_map/while/body/eval_jaxpr/ppermute | solution.py:17
  469.5 17.2 %collective-permute-start = (f32[16,128,128]{2,1,0:T(8,128)}, f32[16,128,128]{2,1,0:T(8,128)S(1)}, u32[]{:S(2)}, u32[]{:S(2)}) collective-permute-start(f32[16,128,128]{2,1,0:T(8,128)} %convolution_add_fusion.7), channel_id=1, source_target_pairs={{0,1},{1,2},{2,3},{3,4},{4,5},{5,6},{6,7},{7,8},{8,9},{9,10},{10,1... | collective-permute-start | bytes 3145736 | tf_op jit(solution)/shard_map/while/body/eval_jaxpr/ppermute | solution.py:17
  488.8 17.2 %collective-permute-start = (f32[16,128,128]{2,1,0:T(8,128)}, f32[16,128,128]{2,1,0:T(8,128)S(1)}, u32[]{:S(2)}, u32[]{:S(2)}) collective-permute-start(f32[16,128,128]{2,1,0:T(8,128)} %convolution_add_fusion.7), channel_id=1, source_target_pairs={{0,1},{1,2},{2,3},{3,4},{4,5},{5,6},{6,7},{7,8},{8,9},{9,10},{10,1... | collective-permute-start | bytes 3145736 | tf_op jit(solution)/shard_map/while/body/eval_jaxpr/ppermute | solution.py:17
where the time goes:
time: 600 us; the launch traced here: 591 us
  matrix products  251 us (42%)
  waiting for transfers between devices  228 us (38%)
  local copies, waits for them, and re-layouts  48.4 us (8%)
  starting transfers between devices  32.1 us (5%)
  other arithmetic  28.7 us (5%)
    ppermute x16, waiting for transfers between devices, shifted(): lax.ppermute(value, axis, [(source, source + steps) for source in range(f...  228 us
    dot_general x5, matrix products, unit_lower_inverse(): jnp.einsum('...ij,...jk->...ik', inverse, power, precision=HIGHEST)  34 us
    ppermute x16, starting transfers between devices, shifted(): lax.ppermute(value, axis, [(source, source + steps) for source in range(f...  32.1 us
    dot_general x15, matrix products, relay(): jnp.einsum('hde,hef->hdf', linear_map, incoming, precision=HIGHEST)  31.9 us
    dot_general x5, matrix products, unit_lower_inverse(): power = jnp.einsum('...ij,...jk->...ik', power, power, precision=HIGHEST)  29.6 us
    dot_general x8, matrix products, compose(): jnp.einsum('hcd,hce->hde', faded_keys, pseudo, precision=HIGHEST)  28.2 us
    dot_general x8, matrix products, span_read(): jnp.einsum('hcd,hce->hde', faded_keys, pseudo, precision=HIGHEST)  24.2 us
    dot_general x8, matrix products, compose(): jnp.einsum('hcd,hde->hce', erase_rows, mapped, precision=HIGHEST)  18.6 us
  transfers between devices with their start and end apart: 16, of which 15 were waited for; matrix products, arithmetic and copies ran while one was open for 2% of the time, Pallas kernels for 0%

commit v1 on v0

v1 whole, which is shorter than its diff:
```python
import functools

import jax
import jax.numpy as jnp
from jax import lax
from jax.experimental import pallas as pl
from jax.experimental.pallas import tpu as pltpu
from jax.sharding import PartitionSpec as P

NH = 2
BLOCK = 16
SPAN = 64
DK = 128
CHUNK = 128
HALF = 64
PLANE = 4
HB = 2
VMEM = 56 << 20

F32 = jnp.float32
BF16 = jnp.bfloat16
NN = (((1,), (0,)), ((), ()))
NT = (((1,), (1,)), ((), ()))


def split(x):
    high = x.astype(BF16)
    low = (x - high.astype(F32)).astype(BF16)
    return high, low


def mm(a, b, dims=NN):
    return lax.dot_general(a, b, dims, preferred_element_type=F32)


def mm3(a, b):
    ah, al = a
    bh, bl = b
    return mm(jnp.concatenate([ah, al], axis=1), jnp.concatenate([bh, bh], axis=0)) + mm(ah, bl)


def mm3_nt(a, b):
    ah, al = a
    bh, bl = b
    return mm(jnp.concatenate([ah, al], axis=1), jnp.concatenate([bh, bh], axis=1), NT) + mm(ah, bl, NT)


def lhs_of(x):
    high, low = x
    return jnp.concatenate([high, low], axis=1)


def rhs_of(x):
    high, low = x
    return jnp.concatenate([high, low, high, low], axis=0)


def silu(v):
    return v / (1.0 + jnp.exp(-v))


def conv(scratch, rows_ref, tail, kernel_ref):
    count = rows_ref.shape[0]
    scratch[5:8, :] = tail
    scratch[8 : 8 + count, :] = rows_ref[...].astype(F32)
    total = kernel_ref[0:1, :] * scratch[5 : 5 + count, :]
    for tap in range(1, 4):
        total = total + kernel_ref[tap : tap + 1, :] * scratch[5 + tap : 5 + tap + count, :]
    return silu(total)


def unit(x):
    return x * lax.rsqrt(jnp.sum(x * x, axis=-1, keepdims=True) + 1e-06)


def iota(shape, dim):
    return lax.broadcasted_iota(jnp.int32, shape, dim)


def prep_kernel(rate_ref, log_ref, mask_ref, rate_out, cum_out, dup_out, row_out, read_out):
    heads, steps = rate_ref.shape
    tokens = log_ref.shape[1]
    group = heads // PLANE
    subs, blocks = mask_ref.shape
    row_of = (iota((steps, blocks), 0) // SPAN == iota((steps, blocks), 1)).astype(F32)
    picked = mm(row_of, mask_ref[...].astype(F32), NT)
    sub_of = ((iota((steps, subs), 0) % SPAN) // BLOCK == iota((steps, subs), 1)).astype(F32)
    keep = jnp.sum(picked * sub_of, axis=1, keepdims=True)
    rates = rate_ref[...].T * keep
    turned = log_ref[...]
    logs = turned.T
    window = CHUNK // NH

    def upto(token, last):
        return ((token // window == last // window) & (token <= last)).astype(F32)

    high = lax.Precision.HIGHEST
    cum = jnp.dot(
        upto(iota((steps, tokens), 1), iota((steps, tokens), 0) // NH), logs, precision=high, preferred_element_type=F32
    )
    read = jnp.dot(
        upto(iota((tokens, tokens), 1), iota((tokens, tokens), 0)), logs, precision=high, preferred_element_type=F32
    )
    wide = (steps // HALF) * CHUNK
    lane = iota((tokens, wide), 1)
    dup = jnp.dot(
        turned,
        upto(iota((tokens, wide), 0), ((lane // CHUNK) * HALF + lane % HALF) // NH),
        precision=high,
        preferred_element_type=F32,
    )
    row = jnp.dot(
        turned,
        upto(iota((tokens, steps), 0), iota((tokens, steps), 1) // NH),
        precision=high,
        preferred_element_type=F32,
    )
    for g in range(PLANE):
        rate_out[g] = rates[:, g * group : (g + 1) * group]
        cum_out[g] = cum[:, g * group : (g + 1) * group]
        read_out[g] = read[:, g * group : (g + 1) * group]
    for b in range(steps // HALF):
        dup_out[:, b, :] = dup[:, b * CHUNK : (b + 1) * CHUNK]
    for b in range(steps // CHUNK):
        row_out[:, b, :] = row[:, b * CHUNK : (b + 1) * CHUNK]


def last_rows_kernel(query_ref, key_ref, value_ref, out_ref):
    for i, ref in enumerate((query_ref, key_ref, value_ref)):
        out_ref[3 * i : 3 * i + 3, :] = ref[...].astype(F32)[13:16].astype(BF16)


def last_rows(*arrays):
    width = arrays[0].shape[1]
    return pl.pallas_call(
        last_rows_kernel,
        grid=(1,),
        in_specs=[pl.BlockSpec((16, width), functools.partial(lambda at, i: (at, 0), x.shape[0] // 16 - 1)) for x in arrays],
        out_specs=pl.BlockSpec((9, width), lambda i: (0, 0)),
        out_shape=jax.ShapeDtypeStruct((9, width), BF16),
        name="last_rows",
    )(*arrays)


def prep(write_rate, log_gate, keep_mask):
    steps, heads = write_rate.shape
    tokens = log_gate.shape[0]
    group = heads // PLANE
    return pl.pallas_call(
        prep_kernel,
        out_shape=(
            jax.ShapeDtypeStruct((PLANE, steps, group), F32),
            jax.ShapeDtypeStruct((PLANE, steps, group), F32),
            jax.ShapeDtypeStruct((heads, steps // HALF, CHUNK), F32),
            jax.ShapeDtypeStruct((heads, steps // CHUNK, CHUNK), F32),
            jax.ShapeDtypeStruct((PLANE, tokens, group), F32),
        ),
        compiler_params=pltpu.CompilerParams(vmem_limit_bytes=40 << 20),
        name="prep",
    )(write_rate.T, log_gate.T, keep_mask.T)


def block_inverses(lowers):
    row = iota((HALF, CHUNK), 0)
    col = iota((HALF, CHUNK), 1) % HALF
    eye = (row == col).astype(F32)
    near = row // BLOCK == col // BLOCK
    inner = [jnp.where(near, -x, 0.0) for x in lowers]
    outer = [split(jnp.where(near, 0.0, x)) for x in lowers]
    first = [split(x) for x in inner]
    second = [mm(lhs_of(x), rhs_of(x)) for x in first]
    s2 = [split(x) for x in second]
    fourth = [mm(lhs_of(x), rhs_of(x)) for x in s2]
    a = [eye + x for x in inner]
    a = [x + mm(lhs_of(split(x)), rhs_of(y)) for x, y in zip(a, s2)]
    s4 = [split(x) for x in fourth]
    eighth = [mm(lhs_of(x), rhs_of(x)) for x in s4]
    a = [x + mm(lhs_of(split(x)), rhs_of(y)) for x, y in zip(a, s4)]
    s8 = [split(x) for x in eighth]
    a = [x + mm(lhs_of(split(x)), rhs_of(y)) for x, y in zip(a, s8)]
    sa = [split(x) for x in a]
    m = [mm(lhs_of(x), rhs_of(y)) for x, y in zip(sa, outer)]
    sm = [split(x) for x in m]
    m2 = [mm(lhs_of(x), rhs_of(x)) for x in sm]
    t = [x - mm(lhs_of(y), rhs_of(z)) for x, y, z in zip(a, sm, sa)]
    return [x + mm(lhs_of(split(y)), rhs_of(split(x))) for x, y in zip(t, m2)]


def maps_kernel(
    group_ref,
    key_ref,
    value_ref,
    tail_ref,
    key_kernel_ref,
    value_kernel_ref,
    rate_ref,
    cum_ref,
    dup_ref,
    row_ref,
    map_out,
    ph_out,
    pl_out,
    scratch,
):
    steps = key_ref.shape[0]
    chunks = steps // CHUNK
    at = pl.program_id(0)
    keys = conv(scratch, key_ref, tail_ref[3:6, :].astype(F32), key_kernel_ref)
    keys = jnp.concatenate([unit(keys[:, h * DK : (h + 1) * DK]) for h in range(HB)], axis=1)
    values = conv(scratch, value_ref, tail_ref[6:9, :].astype(F32), value_kernel_ref)
    kh, kl = split(keys)
    group = rate_ref.shape[2]
    rates, cums = rate_ref[0], cum_ref[0]

    def column(x, h):
        out = x[:, h : h + 1]
        for turn in range(1, group // HB):
            out = jnp.where(at == turn, x[:, turn * HB + h : turn * HB + h + 1], out)
        return out

    row = iota((HALF, CHUNK), 0)
    col = iota((HALF, CHUNK), 1) % HALF
    below = col < row
    lowers, crosses, sides, faded, ends = [], [], [], [], []
    for h in range(HB):
        lanes = slice(h * DK, (h + 1) * DK)
        k_h, v_h = keys[:, lanes], values[:, lanes]
        rate_h, cum_h = column(rates, h), column(cums, h)
        grown = rate_h * jnp.exp(cum_h)
        side = jnp.concatenate([grown * k_h, rate_h * v_h], axis=1)
        for c in range(chunks):
            for b in range(2):
                at_row = c * CHUNK + b * HALF
                rows = slice(at_row, at_row + HALF)
                mine = (kh[rows, lanes], kl[rows, lanes])
                sides.append(split(side[rows]))
                spread = cum_h[rows] - dup_ref[h, 2 * c + b : 2 * c + b + 1, :]
                twice = tuple(jnp.concatenate([x, x], axis=0) for x in mine)
                gram = mm3_nt(mine, twice)
                lowers.append(
                    jnp.where(below, rate_h[rows] * jnp.exp(jnp.where(below, spread, 0.0)) * gram, 0.0)
                )
                if b == 1:
                    before = slice(at_row - HALF, at_row)
                    earlier = (kh[before, lanes], kl[before, lanes])
                    twice = tuple(jnp.concatenate([x, x], axis=0) for x in earlier)
                    spread = cum_h[rows] - dup_ref[h, 2 * c : 2 * c + 1, :]
                    crosses.append(rate_h[rows] * jnp.exp(spread) * mm3_nt(mine, twice))
            row_c = row_ref[h, c : c + 1, :]
            end = row_c[:, CHUNK - 1 : CHUNK]
            turned = k_h[c * CHUNK : (c + 1) * CHUNK].T
            faded.append(split(turned * jnp.exp(end - row_c)))
            ends.append(jnp.exp(end))
    inverses = [split(x) for x in block_inverses(lowers)]
    solved = []
    for i, cross in enumerate(crosses):
        top, low = inverses[2 * i], inverses[2 * i + 1]
        upper = mm(lhs_of(top), rhs_of(sides[2 * i]))
        down = mm(lhs_of(split(cross)), rhs_of(split(upper)))
        lower = mm(lhs_of(low), rhs_of(sides[2 * i + 1])) - mm(lhs_of(low), rhs_of(split(down)))
        solved.append(jnp.concatenate([upper, lower], axis=0))
    state = [None] * HB
    for c in range(chunks):
        for h in range(HB):
            i = h * chunks + c
            erase, fresh = solved[i][:, :DK], solved[i][:, DK:]
            if c == 0:
                pseudo = jnp.concatenate([-erase, fresh], axis=1)
                eye = (iota((DK, 2 * DK), 0) == iota((DK, 2 * DK), 1)).astype(F32)
                carried = ends[i] * eye
            else:
                pieces = split(state[h])
                taken = mm3(split(erase), pieces)
                pseudo = jnp.concatenate([-taken[:, :DK], fresh - taken[:, DK:]], axis=1)
                carried = ends[i] * state[h]
            pieces = split(pseudo)
            at_p = slice(c * CHUNK, (c + 1) * CHUNK)
            ph_out[h, at_p, :], pl_out[h, at_p, :] = pieces
            state[h] = carried + mm3(faded[i], pieces)
    for h in range(HB):
        map_out[h] = state[h]


def group_maps(which, key_rows, value_rows, tails, key_kernel, value_kernel, scalars):
    rate_cols, cum_cols, dup_rows, chunk_rows, _ = scalars
    steps, width = key_rows.shape
    heads = width // DK
    group = heads // PLANE
    turns = group // HB
    lanes = HB * DK
    chunks = steps // CHUNK

    def wide(i, g):
        return (0, g[0] * turns + i)

    def per_head(i, g):
        return (g[0] * turns + i, 0, 0)

    def local(i, g):
        return (i, 0, 0)

    return pl.pallas_call(
        maps_kernel,
        grid_spec=pltpu.PrefetchScalarGridSpec(
            num_scalar_prefetch=1,
            grid=(turns,),
            in_specs=[
                pl.BlockSpec((steps, lanes), wide),
                pl.BlockSpec((steps, lanes), wide),
                pl.BlockSpec((tails.shape[0], lanes), wide),
                pl.BlockSpec((4, lanes), wide),
                pl.BlockSpec((4, lanes), wide),
                pl.BlockSpec((1, steps, group), lambda i, g: (g[0], 0, 0)),
                pl.BlockSpec((1, steps, group), lambda i, g: (g[0], 0, 0)),
                pl.BlockSpec((HB, steps // HALF, CHUNK), per_head),
                pl.BlockSpec((HB, chunks, CHUNK), per_head),
            ],
            out_specs=[
                pl.BlockSpec((HB, DK, 2 * DK), local),
                pl.BlockSpec((HB, steps, 2 * DK), local),
                pl.BlockSpec((HB, steps, 2 * DK), local),
            ],
            scratch_shapes=[pltpu.VMEM((steps + 8, lanes), F32)],
        ),
        out_shape=(
            jax.ShapeDtypeStruct((group, DK, 2 * DK), F32),
            jax.ShapeDtypeStruct((group, steps, 2 * DK), BF16),
            jax.ShapeDtypeStruct((group, steps, 2 * DK), BF16),
        ),
        compiler_params=pltpu.CompilerParams(vmem_limit_bytes=VMEM),
        name="maps",
    )(which, key_rows, value_rows, tails, key_kernel, value_kernel, rate_cols, cum_cols, dup_rows, chunk_rows)


def reads_kernel(
    group_ref,
    query_ref,
    tail_ref,
    query_kernel_ref,
    key_ref,
    key_kernel_ref,
    read_ref,
    row_ref,
    ph_ref,
    pl_ref,
    qh_out,
    ql_out,
    own_out,
    scratch,
):
    tokens = query_ref.shape[0]
    window = CHUNK // NH
    chunks = tokens // window
    at = pl.program_id(0)
    queries = conv(scratch, query_ref, tail_ref[0:3, :].astype(F32), query_kernel_ref)
    queries = jnp.concatenate([unit(queries[:, h * DK : (h + 1) * DK]) for h in range(HB)], axis=1)
    keys = conv(scratch, key_ref, tail_ref[3:6, :].astype(F32), key_kernel_ref)
    group = read_ref.shape[2]
    reads = read_ref[0]
    visible = iota((window, CHUNK), 1) <= NH * iota((window, CHUNK), 0) + NH - 1
    for h in range(HB):
        lanes = slice(h * DK, (h + 1) * DK)
        q_h = queries[:, lanes]
        k_h = unit(keys[:, lanes])
        kh, kl = split(k_h)
        read_h = reads[:, h : h + 1]
        for turn in range(1, group // HB):
            read_h = jnp.where(at == turn, reads[:, turn * HB + h : turn * HB + h + 1], read_h)
        lifted = jnp.exp(read_h) * q_h
        for c in range(chunks):
            rows = slice(c * window, (c + 1) * window)
            steps = slice(c * CHUNK, (c + 1) * CHUNK)
            scores = mm3_nt(split(q_h[rows]), (kh[steps], kl[steps]))
            spread = read_h[rows] - row_ref[h, c : c + 1, :]
            inner = jnp.where(visible, jnp.exp(jnp.where(visible, spread, 0.0)) * scores, 0.0)
            pieces = (ph_ref[h, steps, :], pl_ref[h, steps, :])
            got = mm3(split(inner), pieces)
            if c == 0:
                eff, own = got[:, :DK] + lifted[rows], got[:, DK:]
            else:
                got = got + mm3(split(lifted[rows]), split(state))
                eff, own = got[:, :DK], got[:, DK:]
            if c < chunks - 1:
                row_c = row_ref[h, c : c + 1, :]
                end = row_c[:, CHUNK - 1 : CHUNK]
                faded = split(k_h[steps].T * jnp.exp(end - row_c))
                start = (iota((DK, 2 * DK), 0) == iota((DK, 2 * DK), 1)).astype(F32) if c == 0 else state
                state = jnp.exp(end) * start + mm3(faded, pieces)
            qh_out[rows, lanes], ql_out[rows, lanes] = split(eff)
            own_out[rows, lanes] = own


def group_reads(which, query_rows, key_rows, tails, query_kernel, key_kernel, scalars, kept):
    _, _, _, chunk_rows, read_cols = scalars
    high, low = kept
    tokens, width = query_rows.shape
    steps = tokens * NH
    heads = width // DK
    group = heads // PLANE
    turns = group // HB
    lanes = HB * DK
    chunks = steps // CHUNK

    def wide(i, g):
        return (0, g[0] * turns + i)

    def here(i, g):
        return (0, i)

    def local(i, g):
        return (i, 0, 0)

    return pl.pallas_call(
        reads_kernel,
        grid_spec=pltpu.PrefetchScalarGridSpec(
            num_scalar_prefetch=1,
            grid=(turns,),
            in_specs=[
                pl.BlockSpec((tokens, lanes), wide),
                pl.BlockSpec((tails.shape[0], lanes), wide),
                pl.BlockSpec((4, lanes), wide),
                pl.BlockSpec((steps, lanes), wide),
                pl.BlockSpec((4, lanes), wide),
                pl.BlockSpec((1, tokens, group), lambda i, g: (g[0], 0, 0)),
                pl.BlockSpec((HB, chunks, CHUNK), lambda i, g: (g[0] * turns + i, 0, 0)),
                pl.BlockSpec((HB, steps, 2 * DK), local),
                pl.BlockSpec((HB, steps, 2 * DK), local),
            ],
            out_specs=[
                pl.BlockSpec((tokens, lanes), here),
                pl.BlockSpec((tokens, lanes), here),
                pl.BlockSpec((tokens, lanes), here),
            ],
            scratch_shapes=[pltpu.VMEM((steps + 8, lanes), F32)],
        ),
        out_shape=(
            jax.ShapeDtypeStruct((tokens, group * DK), BF16),
            jax.ShapeDtypeStruct((tokens, group * DK), BF16),
            jax.ShapeDtypeStruct((tokens, group * DK), F32),
        ),
        compiler_params=pltpu.CompilerParams(vmem_limit_bytes=VMEM),
        name="reads",
    )(which, query_rows, tails, query_kernel, key_rows, key_kernel, read_cols, chunk_rows, high, low)


def compose_kernel(flag_ref, mine_ref, other_ref, out_ref):
    mine_first = flag_ref[0] == 0
    for h in range(mine_ref.shape[0]):
        mine, other = mine_ref[h], other_ref[h]
        early = jnp.where(mine_first, mine, other)
        late = jnp.where(mine_first, other, mine)
        both = mm3(split(late[:, :DK]), split(early))
        out_ref[h, :, :DK] = both[:, :DK]
        out_ref[h, :, DK:] = both[:, DK:] + late[:, DK:]


def composed(flag, mine, other):
    return pl.pallas_call(
        compose_kernel,
        in_specs=[pl.BlockSpec(memory_space=pltpu.SMEM)] + [pl.BlockSpec(memory_space=pltpu.VMEM)] * 2,
        out_specs=pl.BlockSpec(memory_space=pltpu.VMEM),
        out_shape=jax.ShapeDtypeStruct(mine.shape, F32),
        name="compose",
    )(flag, mine, other)


def apply_kernel(map_ref, state_ref, out_ref):
    for h in range(map_ref.shape[0]):
        out_ref[h] = mm3(split(map_ref[h, :, :DK]), split(state_ref[h])) + map_ref[h, :, DK:]


def applied(maps, state):
    return pl.pallas_call(
        apply_kernel,
        in_specs=[pl.BlockSpec(memory_space=pltpu.VMEM)] * 2,
        out_specs=pl.BlockSpec(memory_space=pltpu.VMEM),
        out_shape=jax.ShapeDtypeStruct(state.shape, F32),
        name="apply",
    )(maps, state)


def branch_kernel(flag_ref, mine_ref, other_ref, entry_ref, keep_out, send_out):
    first = flag_ref[0] == 0
    for h in range(mine_ref.shape[0]):
        early = jnp.where(first, mine_ref[h], other_ref[h])
        entry = entry_ref[h]
        later = mm3(split(early[:, :DK]), split(entry)) + early[:, DK:]
        keep_out[h] = jnp.where(first, entry, later)
        send_out[h] = jnp.where(first, later, entry)


def branched(flag, mine, other, entry):
    return pl.pallas_call(
        branch_kernel,
        in_specs=[pl.BlockSpec(memory_space=pltpu.SMEM)] + [pl.BlockSpec(memory_space=pltpu.VMEM)] * 3,
        out_specs=[pl.BlockSpec(memory_space=pltpu.VMEM)] * 2,
        out_shape=(jax.ShapeDtypeStruct(entry.shape, F32),) * 2,
        name="branch",
    )(flag, mine, other, entry)


def finish_kernel(group_ref, *refs):
    count = (len(refs) - 1) // 4
    out_ref = refs[-1]
    which = pl.program_id(0)
    for turn in range(count):
        qh_ref, ql_ref, own_ref, entry_ref = refs[4 * turn : 4 * turn + 4]

        @pl.when(which == turn)
        def _():
            for h in range(entry_ref.shape[0]):
                lanes = slice(h * DK, (h + 1) * DK)
                got = mm3((qh_ref[:, lanes], ql_ref[:, lanes]), split(entry_ref[h]))
                out_ref[:, lanes] = (own_ref[:, lanes] + got).astype(BF16)


def finished(order, reads, entries):
    tokens, lanes = reads[0][0].shape
    operands, specs = [], []
    for (qh, ql, own), entry in zip(reads, entries):
        operands += [qh, ql, own, entry]
        specs += [pl.BlockSpec((tokens, lanes), lambda i, g: (0, 0))] * 3
        specs += [pl.BlockSpec(entry.shape, lambda i, g: (0, 0, 0))]
    return pl.pallas_call(
        finish_kernel,
        grid_spec=pltpu.PrefetchScalarGridSpec(
            num_scalar_prefetch=1,
            grid=(len(reads),),
            in_specs=specs,
            out_specs=pl.BlockSpec((tokens, lanes), lambda i, g: (0, g[i])),
        ),
        out_shape=jax.ShapeDtypeStruct((tokens, lanes * len(reads)), BF16),
        compiler_params=pltpu.CompilerParams(vmem_limit_bytes=VMEM),
        name="finish",
    )(order, *operands)


def local(
    count,
    query_rows,
    key_rows,
    value_rows,
    write_rate,
    log_gate,
    keep_mask,
    query_kernel,
    key_kernel,
    value_kernel,
):
    tails = lax.ppermute(last_rows(query_rows, key_rows, value_rows), "seq", [(s, s + 1) for s in range(count - 1)])
    scalars = prep(write_rate, log_gate, keep_mask)
    place = lax.axis_index("seq") % PLANE
    core = (place % 2)[None]
    chip = (place // 2)[None]
    pair = [(s, s ^ 1) for s in range(count)]
    across = [(s, s ^ 2) for s in range(count)]
    onward = [(s, s + PLANE) for s in range(count - PLANE)]
    groups = [(place ^ x)[None] for x in (3, 1, 2, 0)]
    made = [group_maps(g, key_rows, value_rows, tails, key_kernel, value_kernel, scalars) for g in groups]
    maps = [m[0] for m in made]
    from_pair = [lax.ppermute(m, "seq", pair) for m in maps[:2]]
    chip_maps = [composed(core, mine, other) for mine, other in zip(maps[2:], from_pair)]
    from_chip = lax.ppermute(chip_maps[0], "seq", across)
    plane_map = composed(chip, chip_maps[1], from_chip)
    plane_map, kept = lax.optimization_barrier((plane_map, [m[1:] for m in made]))

    def read(i):
        return group_reads(
            groups[i], query_rows, key_rows, tails, query_kernel, key_kernel, scalars, kept[i]
        )

    reads = []
    entry = lax.ppermute(plane_map[:, :, DK:], "seq", onward)
    for i in range(count // PLANE - 1):
        if i > 0:
            entry = lax.ppermute(applied(plane_map, entry), "seq", onward)
        if len(reads) < PLANE - 1:
            reads.append(read(i))
            entry, reads[-1] = lax.optimization_barrier((entry, reads[-1]))
    mine, send = branched(chip, chip_maps[1], from_chip, entry)
    theirs = lax.ppermute(send, "seq", across)
    own_entry, own_send = branched(core, maps[3], from_pair[1], mine)
    reads += [read(i) for i in range(len(reads), PLANE)]
    theirs, reads = lax.optimization_barrier((theirs, reads))
    next_entry, next_send = branched(core, maps[2], from_pair[0], theirs)
    far_own = lax.ppermute(own_send, "seq", pair)
    far_next = lax.ppermute(next_send, "seq", pair)
    return finished(jnp.concatenate(groups), reads, [far_next, far_own, next_entry, own_entry])


def solution(mesh):
    rows = P(("groups", "seq"), None)
    return jax.shard_map(
        functools.partial(local, mesh.shape["seq"]),
        mesh=mesh,
        in_specs=(rows, rows, rows, rows, rows, rows, P(), P(), P()),
        out_specs=rows,
        check_vma=False,
    )
```

time: 600 us -> 146 us (0.24)
  the two profiles are of different devices: /device:TPU:24 before, /device:TPU:9 now
where the time goes in v1:
time: 146 us; the launch traced here: 144 us
  Pallas kernels  114 us (78%)
  starting transfers between devices  16.6 us (11%)
  local copies, waits for them, and re-layouts  11.5 us (8%)
    pallas_call x4, Pallas kernels, group_maps(): pl.pallas_call(maps_kernel, grid_spec=pltpu.PrefetchScalarGridSpec(num_sc...  59.6 us
    pallas_call x4, Pallas kernels, group_reads(): pl.pallas_call(reads_kernel, grid_spec=pltpu.PrefetchScalarGridSpec(num_s...  27.2 us
    unnamed x36, local copies, waits for them, and re-layouts  10.5 us
    pallas_call x3, Pallas kernels, branched(): pl.pallas_call(branch_kernel, in_specs=[pl.BlockSpec(memory_space=pltpu.S...  7 us
    pallas_call x3, Pallas kernels, composed(): pl.pallas_call(compose_kernel, in_specs=[pl.BlockSpec(memory_space=pltpu....  6.97 us
    pallas_call x1, Pallas kernels, finished(): pl.pallas_call(finish_kernel, grid_spec=pltpu.PrefetchScalarGridSpec(num_...  5.76 us
    ppermute x2, starting transfers between devices, local(): entry = lax.ppermute(applied(plane_map, entry), 'seq', onward)  4.22 us
    pallas_call x2, Pallas kernels, applied(): pl.pallas_call(apply_kernel, in_specs=[pl.BlockSpec(memory_space=pltpu.VM...  4.13 us
  transfers between devices with their start and end apart: 10, of which 2 were waited for; matrix products, arithmetic and copies ran while one was open for 0% of the time, Pallas kernels for 58%

profile of v1, /device:TPU:9, one launch (start us, length us, event | category | flops | bytes accessed | tf_op | source)
XLA Modules:
  0.0 144.1 jit_solution(13088490142946156959)
XLA Ops:
  0.0 1.6 %last_rows.1 = bf16[9,2048]{1,0:T(8,128)(2,1)} custom-call(bf16[256,2048]{1,0:T(8,128)(2,1)} %query_ref.9, bf16[512,2048]{1,0:T(8,128)(2,1)} %key_ref.17, bf16[512,2048]{1,0:T(8,128)(2,1)} %value_ref.9), custom_call_target="tpu_custom_call" | custom-call | tf_op jit(solution)/shard_map/last_rows/pallas_call | solution.py:135
  1.6 3.7 %collective-permute-start = (bf16[9,2048]{1,0:T(8,128)(2,1)}, bf16[9,2048]{1,0:T(8,128)(2,1)S(1)}, u32[]{:S(2)}, u32[]{:S(2)}) collective-permute-start(bf16[9,2048]{1,0:T(8,128)(2,1)} %last_rows.1), channel_id=1, source_target_pairs={{0,1},{1,2},{2,3},{3,4},{4,5},{5,6},{6,7},{7,8},{8,9},{9,10},{10,1... | collective-permute-start | bytes 110600 | tf_op jit(solution)/shard_map/ppermute | solution.py:550
  5.3 1.7 %prep.1 = (f32[4,512,4]{2,1,0:T(8,128)S(1)}, f32[4,512,4]{2,1,0:T(8,128)S(1)}, f32[16,8,128]{2,1,0:T(8,128)S(1)}, f32[16,4,128]{2,1,0:T(4,128)S(1)}, f32[4,256,4]{2,1,0:T(8,128)S(1)}) custom-call(f32[16,512]{1,0:T(8,128)S(1)} %bitcast.9, f32[16,256]{1,0:T(8,128)S(1)} %bitcast.10, s32[4,8]{1,0:T(4,128)S(1)} %bitcast.11), custom_call_target="tpu_custom_call" | custom-call | tf_op jit(solution)/shard_map/prep/pallas_call | solution.py:149
  7.0 0.0 copy-start
  7.0 1.0 copy-done
  8.0 1.0 copy-done.1
  9.0 0.8 copy-done.2
  9.8 0.6 copy-done.3
  10.4 0.6 copy-done.4
  11.0 0.6 copy-done.8
  11.6 14.9 %maps.7 = (f32[4,128,256]{2,1,0:T(8,128)}, bf16[4,512,256]{2,1,0:T(8,128)(2,1)}, bf16[4,512,256]{2,1,0:T(8,128)(2,1)}) custom-call(s32[1]{0:T(128)} %bitcast.group_ref, bf16[512,2048]{1,0:T(8,128)(2,1)} %key_ref.17, bf16[512,2048]{1,0:T(8,128)(2,1)} %value_ref.9, bf16[9,2048]{1,0:T(8,128)(2,1)} %copy-done.8, f32[4,2048]{1,0:T(4,128)} %key_kernel_ref.15, ...), custom_call_target="tpu_custom_call" | custom-call | tf_op jit(solution)/shard_map/maps/pallas_call | solution.py:302
  26.5 0.1 collective-permute-start.2
  26.6 14.9 %maps.5 = (f32[4,128,256]{2,1,0:T(8,128)}, bf16[4,512,256]{2,1,0:T(8,128)(2,1)}, bf16[4,512,256]{2,1,0:T(8,128)(2,1)}) custom-call(s32[1]{0:T(128)} %bitcast.1.group_ref, bf16[512,2048]{1,0:T(8,128)(2,1)} %key_ref.17, bf16[512,2048]{1,0:T(8,128)(2,1)} %value_ref.9, bf16[9,2048]{1,0:T(8,128)(2,1)} %copy-done.8, f32[4,2048]{1,0:T(4,128)} %key_kernel_ref.15, ...), custom_call_target="tpu_custom_call" | custom-call | tf_op jit(solution)/shard_map/maps/pallas_call | solution.py:302
  41.5 0.5 collective-permute-start.1
  42.0 15.0 %maps.6 = (f32[4,128,256]{2,1,0:T(8,128)}, bf16[4,512,256]{2,1,0:T(8,128)(2,1)}, bf16[4,512,256]{2,1,0:T(8,128)(2,1)}) custom-call(s32[1]{0:T(128)} %bitcast.2.group_ref, bf16[512,2048]{1,0:T(8,128)(2,1)} %key_ref.17, bf16[512,2048]{1,0:T(8,128)(2,1)} %value_ref.9, bf16[9,2048]{1,0:T(8,128)(2,1)} %copy-done.8, f32[4,2048]{1,0:T(4,128)} %key_kernel_ref.15, ...), custom_call_target="tpu_custom_call" | custom-call | tf_op jit(solution)/shard_map/maps/pallas_call | solution.py:302
  57.0 0.8 copy-done.9
  57.8 2.3 %compose.4 = f32[4,128,256]{2,1,0:T(8,128)} custom-call(s32[1]{0:T(128)} %bitcast.5.flag_ref, f32[4,128,256]{2,1,0:T(8,128)} %get-tuple-element.80.mine_ref, f32[4,128,256]{2,1,0:T(8,128)} %copy-done.9), custom_call_target="tpu_custom_call" | custom-call | tf_op jit(solution)/shard_map/compose/pallas_call | solution.py:458
  60.1 1.2 collective-permute-start.3
  61.3 14.8 %maps.4 = (f32[4,128,256]{2,1,0:T(8,128)}, bf16[4,512,256]{2,1,0:T(8,128)(2,1)}, bf16[4,512,256]{2,1,0:T(8,128)(2,1)}) custom-call(s32[1]{0:T(128)} %bitcast.3.group_ref, bf16[512,2048]{1,0:T(8,128)(2,1)} %key_ref.17, bf16[512,2048]{1,0:T(8,128)(2,1)} %value_ref.9, bf16[9,2048]{1,0:T(8,128)(2,1)} %copy-done.8, f32[4,2048]{1,0:T(4,128)} %key_kernel_ref.15, ...), custom_call_target="tpu_custom_call" | custom-call | tf_op jit(solution)/shard_map/maps/pallas_call | solution.py:302
  76.2 0.0 copy-start.10
  76.2 0.8 copy-done.10
  77.0 2.3 %compose.3.mine_ref = f32[4,128,256]{2,1,0:T(8,128)} custom-call(s32[1]{0:T(128)} %bitcast.5.flag_ref, f32[4,128,256]{2,1,0:T(8,128)} %get-tuple-element.78.mine_ref, f32[4,128,256]{2,1,0:T(8,128)} %copy-done.10), custom_call_target="tpu_custom_call" | custom-call | tf_op jit(solution)/shard_map/compose/pallas_call | solution.py:458
  79.3 0.8 copy-done.11
  80.1 2.3 %compose.5.map_ref = f32[4,128,256]{2,1,0:T(8,128)} custom-call(s32[1]{0:T(128)} %bitcast.4.flag_ref, f32[4,128,256]{2,1,0:T(8,128)} %compose.3.mine_ref, f32[4,128,256]{2,1,0:T(8,128)} %copy-done.11), custom_call_target="tpu_custom_call" | custom-call | tf_op jit(solution)/shard_map/compose/pallas_call | solution.py:458
  82.4 1.0 slice.3
  83.4 3.2 %collective-permute-start.4 = (f32[4,128,128]{2,1,0:T(8,128)S(1)}, f32[4,128,128]{2,1,0:T(8,128)S(1)}, u32[]{:S(2)}, u32[]{:S(2)}) collective-permute-start(f32[4,128,128]{2,1,0:T(8,128)S(1)} %slice.3), channel_id=1, source_target_pairs={{0,4},{1,5},{2,6},{3,7},{4,8},{5,9},{6,10},{7,11},{8,12},{9,13},{1... | collective-permute-start | bytes 786440 | tf_op jit(solution)/shard_map/ppermute | solution.py:573
  86.6 7.0 %reads.4 = (bf16[256,512]{1,0:T(8,128)(2,1)}, bf16[256,512]{1,0:T(8,128)(2,1)}, f32[256,512]{1,0:T(8,128)}) custom-call(s32[1]{0:T(128)} %bitcast.group_ref, bf16[256,2048]{1,0:T(8,128)(2,1)} %query_ref.9, bf16[9,2048]{1,0:T(8,128)(2,1)} %copy-done.8, f32[4,2048]{1,0:T(4,128)} %query_kernel_ref.7, bf16[512,2048]{1,0:T(8,128)(2,1)} %key_ref.17, ...), custom_call_target="tpu_custom_call" | custom-call | tf_op jit(solution)/shard_map/reads/pallas_call | solution.py:413
  93.6 0.7 copy-done.16
  94.3 2.1 %apply.2 = f32[4,128,128]{2,1,0:T(8,128)} custom-call(f32[4,128,256]{2,1,0:T(8,128)} %compose.5.map_ref, f32[4,128,128]{2,1,0:T(8,128)} %copy-done.16), custom_call_target="tpu_custom_call" | custom-call | tf_op jit(solution)/shard_map/apply/pallas_call | solution.py:473
  96.4 2.3 %collective-permute-start.5 = (f32[4,128,128]{2,1,0:T(8,128)}, f32[4,128,128]{2,1,0:T(8,128)S(1)}, u32[]{:S(2)}, u32[]{:S(2)}) collective-permute-start(f32[4,128,128]{2,1,0:T(8,128)} %apply.2), channel_id=1, source_target_pairs={{0,4},{1,5},{2,6},{3,7},{4,8},{5,9},{6,10},{7,11},{8,12},{9,13},{1... | collective-permute-start | bytes 786440 | tf_op jit(solution)/shard_map/ppermute | solution.py:576
  98.7 6.7 %reads.5 = (bf16[256,512]{1,0:T(8,128)(2,1)}, bf16[256,512]{1,0:T(8,128)(2,1)}, f32[256,512]{1,0:T(8,128)}) custom-call(s32[1]{0:T(128)} %bitcast.1.group_ref, bf16[256,2048]{1,0:T(8,128)(2,1)} %query_ref.9, bf16[9,2048]{1,0:T(8,128)(2,1)} %copy-done.8, f32[4,2048]{1,0:T(4,128)} %query_kernel_ref.7, bf16[512,2048]{1,0:T(8,128)(2,1)} %key_ref.17, ...), custom_call_target="tpu_custom_call" | custom-call | tf_op jit(solution)/shard_map/reads/pallas_call | solution.py:413
  105.4 0.2 collective-permute-done.5.state_ref
  105.6 0.7 copy-done.17
  106.3 2.1 %apply.3 = f32[4,128,128]{2,1,0:T(8,128)} custom-call(f32[4,128,256]{2,1,0:T(8,128)} %compose.5.map_ref, f32[4,128,128]{2,1,0:T(8,128)} %copy-done.17), custom_call_target="tpu_custom_call" | custom-call | tf_op jit(solution)/shard_map/apply/pallas_call | solution.py:473
  108.4 1.9 %collective-permute-start.6 = (f32[4,128,128]{2,1,0:T(8,128)}, f32[4,128,128]{2,1,0:T(8,128)S(1)}, u32[]{:S(2)}, u32[]{:S(2)}) collective-permute-start(f32[4,128,128]{2,1,0:T(8,128)} %apply.3), channel_id=1, source_target_pairs={{0,4},{1,5},{2,6},{3,7},{4,8},{5,9},{6,10},{7,11},{8,12},{9,13},{1... | collective-permute-start | bytes 786440 | tf_op jit(solution)/shard_map/ppermute | solution.py:576
  110.3 6.7 %reads.6 = (bf16[256,512]{1,0:T(8,128)(2,1)}, bf16[256,512]{1,0:T(8,128)(2,1)}, f32[256,512]{1,0:T(8,128)}) custom-call(s32[1]{0:T(128)} %bitcast.2.group_ref, bf16[256,2048]{1,0:T(8,128)(2,1)} %query_ref.9, bf16[9,2048]{1,0:T(8,128)(2,1)} %copy-done.8, f32[4,2048]{1,0:T(4,128)} %query_kernel_ref.7, bf16[512,2048]{1,0:T(8,128)(2,1)} %key_ref.17, ...), custom_call_target="tpu_custom_call" | custom-call | tf_op jit(solution)/shard_map/reads/pallas_call | solution.py:413
  117.1 0.7 copy-done.15
  117.8 2.3 %branch.3 = (f32[4,128,128]{2,1,0:T(8,128)}, f32[4,128,128]{2,1,0:T(8,128)}) custom-call(s32[1]{0:T(128)} %bitcast.4.flag_ref, f32[4,128,256]{2,1,0:T(8,128)} %compose.3.mine_ref, f32[4,128,256]{2,1,0:T(8,128)} %copy-done.11, f32[4,128,128]{2,1,0:T(8,128)} %copy-done.15), custom_call_target="tpu_custom_call" | custom-call | tf_op jit(solution)/shard_map/branch/pallas_call | solution.py:493
  120.1 1.5 %collective-permute-start.7 = (f32[4,128,128]{2,1,0:T(8,128)}, f32[4,128,128]{2,1,0:T(8,128)S(1)}, u32[]{:S(2)}, u32[]{:S(2)}) collective-permute-start(f32[4,128,128]{2,1,0:T(8,128)} %get-tuple-element.110), channel_id=1, source_target_pairs={{0,2},{1,3},{2,0},{3,1},{4,6},{5,7},{6,4},{7,5},{8,10},{9,11},{10,... | collective-permute-start | bytes 786440 | tf_op jit(solution)/shard_map/ppermute | solution.py:581
  121.6 6.7 %reads.7 = (bf16[256,512]{1,0:T(8,128)(2,1)}, bf16[256,512]{1,0:T(8,128)(2,1)}, f32[256,512]{1,0:T(8,128)}) custom-call(s32[1]{0:T(128)} %bitcast.3.group_ref, bf16[256,2048]{1,0:T(8,128)(2,1)} %query_ref.9, bf16[9,2048]{1,0:T(8,128)(2,1)} %copy-done.8, f32[4,2048]{1,0:T(4,128)} %query_kernel_ref.7, bf16[512,2048]{1,0:T(8,128)(2,1)} %key_ref.17, ...), custom_call_target="tpu_custom_call" | custom-call | tf_op jit(solution)/shard_map/reads/pallas_call | solution.py:413
  128.3 2.3 %branch.5 = (f32[4,128,128]{2,1,0:T(8,128)}, f32[4,128,128]{2,1,0:T(8,128)}) custom-call(s32[1]{0:T(128)} %bitcast.5.flag_ref, f32[4,128,256]{2,1,0:T(8,128)} %get-tuple-element.78.mine_ref, f32[4,128,256]{2,1,0:T(8,128)} %copy-done.10, f32[4,128,128]{2,1,0:T(8,128)} %get-tuple-element.133.entry_ref), custom_call_target="tpu_custom_call" | custom-call | tf_op jit(solution)/shard_map/branch/pallas_call | solution.py:493
  130.6 2.2 %collective-permute-start.9 = (f32[4,128,128]{2,1,0:T(8,128)}, f32[4,128,128]{2,1,0:T(8,128)S(1)}, u32[]{:S(2)}, u32[]{:S(2)}) collective-permute-start(f32[4,128,128]{2,1,0:T(8,128)} %get-tuple-element.134), channel_id=1, source_target_pairs={{0,1},{1,0},{2,3},{3,2},{4,5},{5,4},{6,7},{7,6},{8,9},{9,8},{10,11... | collective-permute-start | bytes 786440 | tf_op jit(solution)/shard_map/ppermute | solution.py:586
  132.8 0.7 copy-done.13
  133.5 2.3 %branch.4 = (f32[4,128,128]{2,1,0:T(8,128)}, f32[4,128,128]{2,1,0:T(8,128)}) custom-call(s32[1]{0:T(128)} %bitcast.5.flag_ref, f32[4,128,256]{2,1,0:T(8,128)} %get-tuple-element.80.mine_ref, f32[4,128,256]{2,1,0:T(8,128)} %copy-done.9, f32[4,128,128]{2,1,0:T(8,128)} %copy-done.13), custom_call_target="tpu_custom_call" | custom-call | tf_op jit(solution)/shard_map/branch/pallas_call | solution.py:493
  135.8 0.6 pad_add_fusion.group_ref
  136.5 1.1 collective-permute-done.8.refs_3_
  137.6 0.7 copy-done.14
  138.3 5.8 %finish.1 = bf16[256,2048]{1,0:T(8,128)(2,1)} custom-call(s32[4]{0:T(128)} %pad_add_fusion.group_ref, bf16[256,512]{1,0:T(8,128)(2,1)} %get-tuple-element.125.refs_0_, bf16[256,512]{1,0:T(8,128)(2,1)} %get-tuple-element.126.refs_1_, f32[256,512]{1,0:T(8,128)} %get-tuple-element.127.refs_2_, f32[4,128,128]{2,1,0:T(8,128)} %copy-done.14, ...), custom_call_target="tpu_custom_call" | custom-call | tf_op jit(solution)/shard_map/finish/pallas_call | solution.py:524
  (29 shorter events, 0.1 us)
Async XLA Ops:
  0.0 5.3 %copy-start.7 = (s32[8,4]{0,1:T(4,128)S(1)}, s32[8,4]{0,1:T(4,128)}, u32[]{:S(2)}) copy-start(s32[8,4]{0,1:T(4,128)} %param.14) | copy-start | bytes 388
  0.0 5.3 %copy-start.6 = (f32[256,16]{0,1:T(8,128)S(1)}, f32[256,16]{0,1:T(8,128)}, u32[]{:S(2)}) copy-start(f32[256,16]{0,1:T(8,128)} %param.13) | copy-start | bytes 49156
  0.0 5.3 %copy-start.5 = (f32[512,16]{0,1:T(8,128)S(1)}, f32[512,16]{0,1:T(8,128)}, u32[]{:S(2)}) copy-start(f32[512,16]{0,1:T(8,128)} %param.12) | copy-start | bytes 98308
  1.6 9.4 %collective-permute-start = (bf16[9,2048]{1,0:T(8,128)(2,1)}, bf16[9,2048]{1,0:T(8,128)(2,1)S(1)}, u32[]{:S(2)}, u32[]{:S(2)}) collective-permute-start(bf16[9,2048]{1,0:T(8,128)(2,1)} %last_rows.1), channel_id=1, source_target_pairs={{0,1},{1,2},{2,3},{3,4},{4,5},{5,6},{6,7},{7,8},{8,9},{9,10},{10,1... | collective-permute-start | bytes 110600 | tf_op jit(solution)/shard_map/ppermute | solution.py:550
  7.0 1.0 copy-start
  8.0 1.0 copy-start.1
  9.0 0.8 copy-start.2
  9.8 0.6 copy-start.3
  10.4 0.6 copy-start.4
  11.0 0.6 copy-start.8
  26.5 30.5 %collective-permute-start.2 = (f32[4,128,256]{2,1,0:T(8,128)}, f32[4,128,256]{2,1,0:T(8,128)S(1)}, u32[]{:S(2)}, u32[]{:S(2)}) collective-permute-start(f32[4,128,256]{2,1,0:T(8,128)} %get-tuple-element.81), channel_id=1, source_target_pairs={{0,1},{1,0},{2,3},{3,2},{4,5},{5,4},{6,7},{7,6},{8,9},{9,8},{10,11... | collective-permute-start | bytes 1572872 | tf_op jit(solution)/shard_map/ppermute | solution.py:561
  41.5 34.7 %collective-permute-start.1 = (f32[4,128,256]{2,1,0:T(8,128)}, f32[4,128,256]{2,1,0:T(8,128)S(1)}, u32[]{:S(2)}, u32[]{:S(2)}) collective-permute-start(f32[4,128,256]{2,1,0:T(8,128)} %get-tuple-element.79), channel_id=1, source_target_pairs={{0,1},{1,0},{2,3},{3,2},{4,5},{5,4},{6,7},{7,6},{8,9},{9,8},{10,11... | collective-permute-start | bytes 1572872 | tf_op jit(solution)/shard_map/ppermute | solution.py:561
  57.0 0.8 copy-start.9
  60.1 19.2 %collective-permute-start.3 = (f32[4,128,256]{2,1,0:T(8,128)}, f32[4,128,256]{2,1,0:T(8,128)S(1)}, u32[]{:S(2)}, u32[]{:S(2)}) collective-permute-start(f32[4,128,256]{2,1,0:T(8,128)} %compose.4), channel_id=1, source_target_pairs={{0,2},{1,3},{2,0},{3,1},{4,6},{5,7},{6,4},{7,5},{8,10},{9,11},{10,... | collective-permute-start | bytes 1572872 | tf_op jit(solution)/shard_map/ppermute | solution.py:563
  76.2 0.8 copy-start.10
  79.3 0.8 copy-start.11
  83.4 10.2 %collective-permute-start.4 = (f32[4,128,128]{2,1,0:T(8,128)S(1)}, f32[4,128,128]{2,1,0:T(8,128)S(1)}, u32[]{:S(2)}, u32[]{:S(2)}) collective-permute-start(f32[4,128,128]{2,1,0:T(8,128)S(1)} %slice.3), channel_id=1, source_target_pairs={{0,4},{1,5},{2,6},{3,7},{4,8},{5,9},{6,10},{7,11},{8,12},{9,13},{1... | collective-permute-start | bytes 786440 | tf_op jit(solution)/shard_map/ppermute | solution.py:573
  93.6 0.7 copy-start.16
  96.4 9.2 %collective-permute-start.5 = (f32[4,128,128]{2,1,0:T(8,128)}, f32[4,128,128]{2,1,0:T(8,128)S(1)}, u32[]{:S(2)}, u32[]{:S(2)}) collective-permute-start(f32[4,128,128]{2,1,0:T(8,128)} %apply.2), channel_id=1, source_target_pairs={{0,4},{1,5},{2,6},{3,7},{4,8},{5,9},{6,10},{7,11},{8,12},{9,13},{1... | collective-permute-start | bytes 786440 | tf_op jit(solution)/shard_map/ppermute | solution.py:576
  105.6 0.7 copy-start.17
  108.4 8.7 %collective-permute-start.6 = (f32[4,128,128]{2,1,0:T(8,128)}, f32[4,128,128]{2,1,0:T(8,128)S(1)}, u32[]{:S(2)}, u32[]{:S(2)}) collective-permute-start(f32[4,128,128]{2,1,0:T(8,128)} %apply.3), channel_id=1, source_target_pairs={{0,4},{1,5},{2,6},{3,7},{4,8},{5,9},{6,10},{7,11},{8,12},{9,13},{1... | collective-permute-start | bytes 786440 | tf_op jit(solution)/shard_map/ppermute | solution.py:576
  117.0 0.7 copy-start.15
  120.1 12.7 %collective-permute-start.7 = (f32[4,128,128]{2,1,0:T(8,128)}, f32[4,128,128]{2,1,0:T(8,128)S(1)}, u32[]{:S(2)}, u32[]{:S(2)}) collective-permute-start(f32[4,128,128]{2,1,0:T(8,128)} %get-tuple-element.110), channel_id=1, source_target_pairs={{0,2},{1,3},{2,0},{3,1},{4,6},{5,7},{6,4},{7,5},{8,10},{9,11},{10,... | collective-permute-start | bytes 786440 | tf_op jit(solution)/shard_map/ppermute | solution.py:581
  130.6 5.9 %collective-permute-start.9 = (f32[4,128,128]{2,1,0:T(8,128)}, f32[4,128,128]{2,1,0:T(8,128)S(1)}, u32[]{:S(2)}, u32[]{:S(2)}) collective-permute-start(f32[4,128,128]{2,1,0:T(8,128)} %get-tuple-element.134), channel_id=1, source_target_pairs={{0,1},{1,0},{2,3},{3,2},{4,5},{5,4},{6,7},{7,6},{8,9},{9,8},{10,11... | collective-permute-start | bytes 786440 | tf_op jit(solution)/shard_map/ppermute | solution.py:586
  132.8 0.7 copy-start.13
  135.8 1.7 %collective-permute-start.8 = (f32[4,128,128]{2,1,0:T(8,128)}, f32[4,128,128]{2,1,0:T(8,128)S(1)}, u32[]{:S(2)}, u32[]{:S(2)}) collective-permute-start(f32[4,128,128]{2,1,0:T(8,128)} %get-tuple-element.129), channel_id=1, source_target_pairs={{0,1},{1,0},{2,3},{3,2},{4,5},{5,4},{6,7},{7,6},{8,9},{9,8},{10,11... | collective-permute-start | bytes 786440 | tf_op jit(solution)/shard_map/ppermute | solution.py:587
  136.5 1.1 copy-start.12
  137.6 0.7 copy-start.14

commit v2 on v1

v2 whole, which is shorter than its diff:
```python
import functools

import jax
import jax.numpy as jnp
from jax import lax
from jax.experimental import pallas as pl
from jax.experimental.pallas import tpu as pltpu
from jax.sharding import PartitionSpec as P

NH = 2
BLOCK = 16
SPAN = 64
DK = 128
CHUNK = 128
HALF = 64
PLANE = 4
HB = 2
VMEM = 56 << 20

F32 = jnp.float32
BF16 = jnp.bfloat16
NN = (((1,), (0,)), ((), ()))
NT = (((1,), (1,)), ((), ()))


def split(x):
    high = x.astype(BF16)
    low = (x - high.astype(F32)).astype(BF16)
    return high, low


def mm(a, b, dims=NN):
    return lax.dot_general(a, b, dims, preferred_element_type=F32)


def mm3(a, b):
    ah, al = a
    bh, bl = b
    return mm(jnp.concatenate([ah, al], axis=1), jnp.concatenate([bh, bh], axis=0)) + mm(ah, bl)


def mm3_nt(a, b):
    ah, al = a
    bh, bl = b
    return mm(jnp.concatenate([ah, al], axis=1), jnp.concatenate([bh, bh], axis=1), NT) + mm(ah, bl, NT)


def halves(x):
    left = iota(x.shape, 1) < HALF
    zero = jnp.zeros_like(x)
    return jnp.concatenate([jnp.where(left, x, zero), jnp.where(left, zero, x)], axis=0)


def pair_product(x, y):
    return mm3(x, (halves(y[0]), halves(y[1])))


def silu(v):
    return v / (1.0 + jnp.exp(-v))


def load_rows(scratch, rows_ref, tail):
    before = jnp.concatenate([jnp.zeros((13, tail.shape[1]), F32), tail.astype(F32)], axis=0)
    scratch[0:16, :] = before.astype(BF16)
    scratch[16 : 16 + rows_ref.shape[0], :] = rows_ref[...]


def shifter():
    shape = (3 * HALF, HALF + 16)
    row, col = iota(shape, 0), iota(shape, 1)
    return (col == 15 + row % HALF - row // HALF).astype(F32).astype(BF16)


def conv(shifts, scratch, kernel_ref, start, count):
    parts = []
    for at in range(start, start + count, HALF):
        moved = mm(shifts, scratch[at : at + HALF + 16, :])
        total = kernel_ref[3:4, :] * scratch[at + 16 : at + 16 + HALF, :].astype(F32)
        for back in range(1, 4):
            total = total + kernel_ref[3 - back : 4 - back, :] * moved[(back - 1) * HALF : back * HALF]
        parts.append(silu(total))
    return jnp.concatenate(parts, axis=0)


def unit(x):
    return x * lax.rsqrt(jnp.sum(x * x, axis=-1, keepdims=True) + 1e-06)


def iota(shape, dim):
    return lax.broadcasted_iota(jnp.int32, shape, dim)


def prep_kernel(rate_ref, log_ref, mask_ref, rate_out, cum_out, row_out, read_out):
    heads, steps = rate_ref.shape
    tokens = log_ref.shape[1]
    group = heads // PLANE
    subs, blocks = mask_ref.shape
    row_of = (iota((steps, blocks), 0) // SPAN == iota((steps, blocks), 1)).astype(F32)
    picked = mm(row_of, mask_ref[...].astype(F32), NT)
    sub_of = ((iota((steps, subs), 0) % SPAN) // BLOCK == iota((steps, subs), 1)).astype(F32)
    keep = jnp.sum(picked * sub_of, axis=1, keepdims=True)
    rates = rate_ref[...].T * keep
    turned = log_ref[...]
    logs = turned.T
    window = CHUNK // NH

    def upto(token, last):
        return ((token // window == last // window) & (token <= last)).astype(F32)

    high = lax.Precision.HIGHEST
    cum = jnp.dot(
        upto(iota((steps, tokens), 1), iota((steps, tokens), 0) // NH), logs, precision=high, preferred_element_type=F32
    )
    read = jnp.dot(
        upto(iota((tokens, tokens), 1), iota((tokens, tokens), 0)), logs, precision=high, preferred_element_type=F32
    )
    row = jnp.dot(
        turned,
        upto(iota((tokens, steps), 0), iota((tokens, steps), 1) // NH),
        precision=high,
        preferred_element_type=F32,
    )
    for g in range(PLANE):
        rate_out[g] = rates[:, g * group : (g + 1) * group]
        cum_out[g] = cum[:, g * group : (g + 1) * group]
        read_out[g] = read[:, g * group : (g + 1) * group]
    for b in range(steps // CHUNK):
        row_out[:, b, :] = row[:, b * CHUNK : (b + 1) * CHUNK]


def last_rows_kernel(query_ref, key_ref, value_ref, out_ref):
    for i, ref in enumerate((query_ref, key_ref, value_ref)):
        out_ref[3 * i : 3 * i + 3, :] = ref[...].astype(F32)[13:16].astype(BF16)


def last_rows(*arrays):
    width = arrays[0].shape[1]
    return pl.pallas_call(
        last_rows_kernel,
        grid=(1,),
        in_specs=[pl.BlockSpec((16, width), functools.partial(lambda at, i: (at, 0), x.shape[0] // 16 - 1)) for x in arrays],
        out_specs=pl.BlockSpec((9, width), lambda i: (0, 0)),
        out_shape=jax.ShapeDtypeStruct((9, width), BF16),
        name="last_rows",
    )(*arrays)


def prep(write_rate, log_gate, keep_mask):
    steps, heads = write_rate.shape
    tokens = log_gate.shape[0]
    group = heads // PLANE
    return pl.pallas_call(
        prep_kernel,
        out_shape=(
            jax.ShapeDtypeStruct((PLANE, steps, group), F32),
            jax.ShapeDtypeStruct((PLANE, steps, group), F32),
            jax.ShapeDtypeStruct((heads, steps // CHUNK, CHUNK), F32),
            jax.ShapeDtypeStruct((PLANE, tokens, group), F32),
        ),
        compiler_params=pltpu.CompilerParams(vmem_limit_bytes=VMEM),
        name="prep",
    )(write_rate.T, log_gate.T, keep_mask.T)


def block_inverses(lowers, fill):
    row = iota((HALF, CHUNK), 0)
    col = iota((HALF, CHUNK), 1) % HALF
    eye = (row == col).astype(F32)
    near = row // BLOCK == col // BLOCK
    inner = [jnp.where(near, -x, 0.0) for x in lowers]
    outer = [split(jnp.where(near, 0.0, x)) for x in lowers]
    power = [split(x) for x in inner]
    a = [eye + x for x in inner]
    for _ in range(3):
        fill()
        power = [split(pair_product(x, x)) for x in power]
        fill()
        a = [x + pair_product(split(x), y) for x, y in zip(a, power)]
    sa = [split(x) for x in a]
    fill()
    m = [split(pair_product(x, y)) for x, y in zip(sa, outer)]
    fill()
    m2 = [split(pair_product(x, x)) for x in m]
    t = [x - pair_product(y, z) for x, y, z in zip(a, m, sa)]
    return [x + pair_product(y, split(x)) for x, y in zip(t, m2)]


def maps_kernel(
    group_ref,
    key_ref,
    value_ref,
    tail_ref,
    key_kernel_ref,
    value_kernel_ref,
    rate_ref,
    cum_ref,
    row_ref,
    map_out,
    wh_out,
    wl_out,
    mh_out,
    ml_out,
    scratch,
    value_scratch,
):
    steps = key_ref.shape[0]
    chunks = steps // CHUNK
    at = pl.program_id(0)
    load_rows(scratch, key_ref, tail_ref[3:6, :])
    load_rows(value_scratch, value_ref, tail_ref[6:9, :])
    shifts = shifter()
    keys = conv(shifts, scratch, key_kernel_ref, 0, steps)
    keys = jnp.concatenate([unit(keys[:, h * DK : (h + 1) * DK]) for h in range(HB)], axis=1)
    kh, kl = split(keys)
    group = rate_ref.shape[2]
    rates, cums = rate_ref[0], cum_ref[0]

    def column(x, h):
        out = x[:, h : h + 1]
        for turn in range(1, group // HB):
            out = jnp.where(at == turn, x[:, turn * HB + h : turn * HB + h + 1], out)
        return out

    below = iota((CHUNK, CHUNK), 1) < iota((CHUNK, CHUNK), 0)
    left = iota((HALF, CHUNK), 1) < HALF
    items = [(h, c) for h in range(HB) for c in range(chunks)]
    columns = [(column(rates, h), column(cums, h)) for h in range(HB)]
    lowers, crosses, sides, faded, ends = [], [], {}, {}, {}
    for h, c in items:
        lanes = slice(h * DK, (h + 1) * DK)
        rows = slice(c * CHUNK, (c + 1) * CHUNK)
        row_c = row_ref[h, c : c + 1, :]
        rate_c, cum_c = (x[rows] for x in columns[h])
        mine = (kh[rows, lanes], kl[rows, lanes])
        decay = jnp.exp(jnp.where(below, cum_c - row_c, 0.0))
        lower = jnp.where(below, rate_c * decay * mm3_nt(mine, mine), 0.0)
        lowers.append(jnp.where(left, lower[:HALF], lower[HALF:]))
        crosses.append(split(jnp.where(left, lower[HALF:], 0.0)))

    def side(c):
        rows = slice(c * CHUNK, (c + 1) * CHUNK)
        values = conv(shifts, value_scratch, value_kernel_ref, c * CHUNK, CHUNK)
        for h in range(HB):
            lanes = slice(h * DK, (h + 1) * DK)
            rate_c, cum_c = (x[rows] for x in columns[h])
            grown = rate_c * jnp.exp(cum_c) * keys[rows, lanes]
            sides[h, c] = split(jnp.concatenate([grown, rate_c * values[:, lanes]], axis=1))

    def fade(c):
        for h in range(HB):
            row_c = row_ref[h, c : c + 1, :]
            end = row_c[:, CHUNK - 1 : CHUNK]
            k_c = keys[c * CHUNK : (c + 1) * CHUNK, h * DK : (h + 1) * DK]
            faded[h, c] = split(k_c.T * jnp.exp(end - row_c))
            ends[h, c] = jnp.exp(end)

    todo = [functools.partial(f, c) for c in range(chunks) for f in (side, fade)]

    def fill():
        if todo:
            todo.pop(0)()

    eye = (iota((DK, DK), 0) == iota((DK, DK), 1)).astype(F32)
    inverses = block_inverses(lowers, fill)
    while todo:
        fill()
    pieces = [split(x) for x in inverses]
    under = [mm3(y, tuple(jnp.concatenate([z, z], axis=0) for z in x)) for x, y in zip(pieces, crosses)]
    under = [split(jnp.where(left, x, 0.0)) for x in under]
    under = [
        mm3(x, tuple(jnp.concatenate([jnp.zeros_like(z), z], axis=0) for z in y)) for x, y in zip(pieces, under)
    ]
    whole = [
        split(jnp.concatenate([jnp.where(left, x, 0.0), jnp.where(left, -y, x)], axis=0))
        for x, y in zip(inverses, under)
    ]
    solved = [split(mm3(x, sides[i])) for i, x in zip(items, whole)]
    for (h, c), x in zip(items, solved):
        at_w = slice(c * CHUNK, (c + 1) * CHUNK)
        wh_out[h, at_w, :], wl_out[h, at_w, :] = x
    made = [mm3(faded[i], x) for i, x in zip(items, solved)]
    made = [jnp.concatenate([ends[i] * eye - x[:, :DK], x[:, DK:]], axis=1) for i, x in zip(items, made)]

    def then(late, early):
        both = mm3(split(late[:, :DK]), early)
        return jnp.concatenate([both[:, :DK], both[:, DK:] + late[:, DK:]], axis=1)

    assert chunks == 4
    heads = range(HB)
    first, third = ([split(made[h * chunks + c]) for h in heads] for c in (0, 2))
    two = [split(then(made[h * chunks + 1], first[h])) for h in heads]
    last = [then(made[h * chunks + 3], third[h]) for h in heads]
    last = [then(last[h], two[h]) for h in heads]
    for h in heads:
        map_out[h] = last[h]
        for i, x in enumerate((first[h], two[h], third[h])):
            mh_out[h, i * DK : (i + 1) * DK, :], ml_out[h, i * DK : (i + 1) * DK, :] = x


def group_maps(which, key_rows, value_rows, tails, key_kernel, value_kernel, scalars):
    rate_cols, cum_cols, chunk_rows, _ = scalars
    steps, width = key_rows.shape
    heads = width // DK
    group = heads // PLANE
    turns = group // HB
    lanes = HB * DK
    chunks = steps // CHUNK

    def wide(i, g):
        return (0, g[0] * turns + i)

    def per_head(i, g):
        return (g[0] * turns + i, 0, 0)

    def local(i, g):
        return (i, 0, 0)

    return pl.pallas_call(
        maps_kernel,
        grid_spec=pltpu.PrefetchScalarGridSpec(
            num_scalar_prefetch=1,
            grid=(turns,),
            in_specs=[
                pl.BlockSpec((steps, lanes), wide),
                pl.BlockSpec((steps, lanes), wide),
                pl.BlockSpec((tails.shape[0], lanes), wide),
                pl.BlockSpec((4, lanes), wide),
                pl.BlockSpec((4, lanes), wide),
                pl.BlockSpec((1, steps, group), lambda i, g: (g[0], 0, 0)),
                pl.BlockSpec((1, steps, group), lambda i, g: (g[0], 0, 0)),
                pl.BlockSpec((HB, chunks, CHUNK), per_head),
            ],
            out_specs=[
                pl.BlockSpec((HB, DK, 2 * DK), local),
                pl.BlockSpec((HB, steps, 2 * DK), local),
                pl.BlockSpec((HB, steps, 2 * DK), local),
                pl.BlockSpec((HB, 3 * DK, 2 * DK), local),
                pl.BlockSpec((HB, 3 * DK, 2 * DK), local),
            ],
            scratch_shapes=[pltpu.VMEM((steps + 16, lanes), BF16)] * 2,
        ),
        out_shape=(
            jax.ShapeDtypeStruct((group, DK, 2 * DK), F32),
            jax.ShapeDtypeStruct((group, steps, 2 * DK), BF16),
            jax.ShapeDtypeStruct((group, steps, 2 * DK), BF16),
            jax.ShapeDtypeStruct((group, 3 * DK, 2 * DK), BF16),
            jax.ShapeDtypeStruct((group, 3 * DK, 2 * DK), BF16),
        ),
        compiler_params=pltpu.CompilerParams(vmem_limit_bytes=VMEM),
        name="maps",
    )(which, key_rows, value_rows, tails, key_kernel, value_kernel, rate_cols, cum_cols, chunk_rows)


def reads_kernel(
    group_ref,
    query_ref,
    tail_ref,
    query_kernel_ref,
    key_ref,
    key_kernel_ref,
    read_ref,
    row_ref,
    wh_ref,
    wl_ref,
    mh_ref,
    ml_ref,
    qh_out,
    ql_out,
    own_out,
    scratch,
    key_scratch,
):
    tokens = query_ref.shape[0]
    window = CHUNK // NH
    chunks = tokens // window
    at = pl.program_id(0)
    load_rows(scratch, query_ref, tail_ref[0:3, :])
    shifts = shifter()
    queries = conv(shifts, scratch, query_kernel_ref, 0, tokens)
    queries = jnp.concatenate([unit(queries[:, h * DK : (h + 1) * DK]) for h in range(HB)], axis=1)
    load_rows(key_scratch, key_ref, tail_ref[3:6, :])
    keys = conv(shifts, key_scratch, key_kernel_ref, 0, NH * tokens)
    group = read_ref.shape[2]
    reads = read_ref[0]
    visible = iota((window, CHUNK), 1) <= NH * iota((window, CHUNK), 0) + NH - 1
    items = [(h, c) for h in range(HB) for c in range(chunks)]
    pieces, columns, lifted = [], [], []
    for h in range(HB):
        lanes = slice(h * DK, (h + 1) * DK)
        read_h = reads[:, h : h + 1]
        for turn in range(1, group // HB):
            read_h = jnp.where(at == turn, reads[:, turn * HB + h : turn * HB + h + 1], read_h)
        columns.append(read_h)
        lifted.append(jnp.exp(read_h) * queries[:, lanes])
        pieces.append((split(queries[:, lanes]), split(unit(keys[:, lanes]))))

    def tokens_of(c):
        return slice(c * window, (c + 1) * window)

    def steps_of(c):
        return slice(c * CHUNK, (c + 1) * CHUNK)

    scores = [
        mm3_nt(tuple(x[tokens_of(c)] for x in pieces[h][0]), tuple(x[steps_of(c)] for x in pieces[h][1]))
        for h, c in items
    ]
    starts = {}
    for h in range(HB):
        kept = [(mh_ref[h, i * DK : (i + 1) * DK, :], ml_ref[h, i * DK : (i + 1) * DK, :]) for i in range(3)]
        first, two, third = kept
        three = mm3(tuple(x[:, :DK] for x in third), two)
        late = third[0][:, DK:].astype(F32) + third[1][:, DK:].astype(F32)
        three = split(jnp.concatenate([three[:, :DK], three[:, DK:] + late], axis=1))
        starts[h] = [None, first, two, three]
    inner = []
    for (h, c), x in zip(items, scores):
        spread = columns[h][tokens_of(c)] - row_ref[h, c : c + 1, :]
        inner.append(split(jnp.where(visible, jnp.exp(jnp.where(visible, spread, 0.0)) * x, 0.0)))
    got = [mm3(x, (wh_ref[h, steps_of(c), :], wl_ref[h, steps_of(c), :])) for (h, c), x in zip(items, inner)]
    eff = [lifted[h][tokens_of(c)] - x[:, :DK] for (h, c), x in zip(items, got)]
    eff_pieces = [split(x) for x in eff]
    taken = [None if c == 0 else mm3(x, starts[h][c]) for (h, c), x in zip(items, eff_pieces)]
    for (h, c), x, y, z in zip(items, eff_pieces, got, taken):
        at_out = (tokens_of(c), slice(h * DK, (h + 1) * DK))
        qh_out[at_out], ql_out[at_out] = x if c == 0 else split(z[:, :DK])
        own_out[at_out] = y[:, DK:] if c == 0 else y[:, DK:] + z[:, DK:]


def group_reads(which, query_rows, key_rows, tails, query_kernel, key_kernel, scalars, kept):
    _, _, chunk_rows, read_cols = scalars
    tokens, width = query_rows.shape
    steps = tokens * NH
    heads = width // DK
    group = heads // PLANE
    turns = group // HB
    lanes = HB * DK
    chunks = steps // CHUNK

    def wide(i, g):
        return (0, g[0] * turns + i)

    def here(i, g):
        return (0, i)

    def local(i, g):
        return (i, 0, 0)

    return pl.pallas_call(
        reads_kernel,
        grid_spec=pltpu.PrefetchScalarGridSpec(
            num_scalar_prefetch=1,
            grid=(turns,),
            in_specs=[
                pl.BlockSpec((tokens, lanes), wide),
                pl.BlockSpec((tails.shape[0], lanes), wide),
                pl.BlockSpec((4, lanes), wide),
                pl.BlockSpec((steps, lanes), wide),
                pl.BlockSpec((4, lanes), wide),
                pl.BlockSpec((1, tokens, group), lambda i, g: (g[0], 0, 0)),
                pl.BlockSpec((HB, chunks, CHUNK), lambda i, g: (g[0] * turns + i, 0, 0)),
                pl.BlockSpec((HB, steps, 2 * DK), local),
                pl.BlockSpec((HB, steps, 2 * DK), local),
                pl.BlockSpec((HB, 3 * DK, 2 * DK), local),
                pl.BlockSpec((HB, 3 * DK, 2 * DK), local),
            ],
            out_specs=[
                pl.BlockSpec((tokens, lanes), here),
                pl.BlockSpec((tokens, lanes), here),
                pl.BlockSpec((tokens, lanes), here),
            ],
            scratch_shapes=[pltpu.VMEM((tokens + 16, lanes), BF16), pltpu.VMEM((steps + 16, lanes), BF16)],
        ),
        out_shape=(
            jax.ShapeDtypeStruct((tokens, group * DK), BF16),
            jax.ShapeDtypeStruct((tokens, group * DK), BF16),
            jax.ShapeDtypeStruct((tokens, group * DK), F32),
        ),
        compiler_params=pltpu.CompilerParams(vmem_limit_bytes=VMEM),
        name="reads",
    )(which, query_rows, tails, query_kernel, key_rows, key_kernel, read_cols, chunk_rows, *kept)


def small(kernel, flags, operands, outs, name):
    def whole(shape):
        return pl.BlockSpec(shape, lambda i, *_: (0,) * len(shape))

    return pl.pallas_call(
        kernel,
        grid_spec=pltpu.PrefetchScalarGridSpec(
            num_scalar_prefetch=len(flags),
            grid=(1,),
            in_specs=[whole(x.shape) for x in operands],
            out_specs=[whole(shape) for shape in outs],
        ),
        out_shape=[jax.ShapeDtypeStruct(shape, F32) for shape in outs],
        name=name,
    )(*flags, *operands)


def after(first, mine, other):
    early = jnp.where(first, mine, other)
    late = jnp.where(first, other, mine)
    both = mm3(split(late[:, :DK]), split(early))
    return jnp.concatenate([both[:, :DK], both[:, DK:] + late[:, DK:]], axis=1)


def compose_kernel(core_ref, mine_ref, other_ref, out_ref):
    heads = range(mine_ref.shape[0])
    for h, x in enumerate([after(core_ref[0] == 0, mine_ref[h], other_ref[h]) for h in heads]):
        out_ref[h] = x


def composed(core, mine, other):
    return small(compose_kernel, [core], [mine, other], [mine.shape], "compose")[0]


def plane_kernel(core_ref, chip_ref, mine_ref, pair_ref, other_ref, chip_out, plane_out, offset_out):
    heads = range(mine_ref.shape[0])
    chips = [after(core_ref[0] == 0, mine_ref[h], pair_ref[h]) for h in heads]
    planes = [after(chip_ref[0] == 0, chips[h], other_ref[h]) for h in heads]
    for h in heads:
        chip_out[h] = chips[h]
        plane_out[h] = planes[h]
        offset_out[h] = planes[h][:, DK:]


def plane_composed(core, chip, mine, pair, other):
    heads = mine.shape[0]
    return small(
        plane_kernel, [core, chip], [mine, pair, other], [mine.shape, mine.shape, (heads, DK, DK)], "plane"
    )


def apply_kernel(map_ref, state_ref, out_ref):
    heads = range(map_ref.shape[0])
    got = [mm3(split(map_ref[h, :, :DK]), split(state_ref[h])) for h in heads]
    for h in heads:
        out_ref[h] = got[h] + map_ref[h, :, DK:]


def applied(maps, state):
    return small(apply_kernel, [], [maps, state], [state.shape], "apply")[0]


def branches(first, mine, other, entry):
    heads = range(len(entry))
    early = [jnp.where(first, mine[h], other[h]) for h in heads]
    later = [mm3(split(early[h][:, :DK]), split(entry[h])) + early[h][:, DK:] for h in heads]
    own = [jnp.where(first, entry[h], later[h]) for h in heads]
    return own, [jnp.where(first, later[h], entry[h]) for h in heads]


def branch_kernel(core_ref, mine_ref, other_ref, entry_ref, keep_out, send_out):
    refs = (mine_ref, other_ref, entry_ref)
    own, send = branches(core_ref[0] == 0, *([x[h] for h in range(x.shape[0])] for x in refs))
    for h in range(len(own)):
        keep_out[h] = own[h]
        send_out[h] = send[h]


def branched(core, mine, other, entry):
    return small(branch_kernel, [core], [mine, other, entry], [entry.shape] * 2, "branch")


def fork_kernel(core_ref, chip_ref, chip_map_ref, from_chip_ref, map_ref, pair_ref, entry_ref, *outs):
    refs = (chip_map_ref, from_chip_ref, map_ref, pair_ref, entry_ref)
    chip_map, from_chip, mine, pair, entry = ([x[h] for h in range(x.shape[0])] for x in refs)
    own, across = branches(chip_ref[0] == 0, chip_map, from_chip, entry)
    for out_ref, states in zip(outs, (across, *branches(core_ref[0] == 0, mine, pair, own))):
        for h, state in enumerate(states):
            out_ref[h] = state


def forked(core, chip, chip_map, from_chip, mine, pair, entry):
    operands = [chip_map, from_chip, mine, pair, entry]
    return small(fork_kernel, [core, chip], operands, [entry.shape] * 3, "fork")


def finish_kernel(group_ref, *refs):
    out_ref = refs[-1]
    count = (len(refs) - 1) // 4
    for turn in range(count):
        qh_ref, ql_ref, own_ref, entry_ref = refs[4 * turn : 4 * turn + 4]

        @pl.when(pl.program_id(0) == turn)
        def _():
            for h in range(entry_ref.shape[0]):
                lanes = slice(h * DK, (h + 1) * DK)
                got = mm3((qh_ref[:, lanes], ql_ref[:, lanes]), split(entry_ref[h]))
                out_ref[:, lanes] = (own_ref[:, lanes] + got).astype(BF16)


def finished(order, reads, entries, out, width):
    tokens, lanes = reads[0][0].shape
    operands, specs = [], []
    for (qh, ql, own), entry in zip(reads, entries):
        operands += [qh, ql, own, entry]
        specs += [pl.BlockSpec((tokens, lanes), lambda i, g: (0, 0))] * 3
        specs += [pl.BlockSpec(entry.shape, lambda i, g: (0, 0, 0))]
    if out is not None:
        operands.append(out)
        specs.append(pl.BlockSpec(memory_space=pl.ANY))
    return pl.pallas_call(
        finish_kernel,
        grid_spec=pltpu.PrefetchScalarGridSpec(
            num_scalar_prefetch=1,
            grid=(len(reads),),
            in_specs=specs,
            out_specs=pl.BlockSpec((tokens, lanes), lambda i, g: (0, g[i])),
        ),
        out_shape=jax.ShapeDtypeStruct((tokens, width), BF16),
        input_output_aliases={} if out is None else {len(operands): 0},
        name="finish",
    )(order, *operands)


def moved(x, pairs):
    return pltpu.with_memory_space_constraint(lax.ppermute(x, "seq", pairs), pltpu.VMEM)


def local(
    count,
    query_rows,
    key_rows,
    value_rows,
    write_rate,
    log_gate,
    keep_mask,
    query_kernel,
    key_kernel,
    value_kernel,
):
    tails = moved(last_rows(query_rows, key_rows, value_rows), [(s, s + 1) for s in range(count - 1)])
    scalars = prep(write_rate, log_gate, keep_mask)
    place = lax.axis_index("seq") % PLANE
    core = (place % 2)[None]
    chip = (place // 2)[None]
    pair = [(s, s ^ 1) for s in range(count)]
    across = [(s, s ^ 2) for s in range(count)]
    onward = [(s, s + PLANE) for s in range(count - PLANE)]
    groups = [(place ^ x)[None] for x in (3, 1, 2, 0)]
    made = [group_maps(g, key_rows, value_rows, tails, key_kernel, value_kernel, scalars) for g in groups]
    maps = [m[0] for m in made]
    from_pair = [moved(m, pair) for m in maps[:2]]
    next_map = composed(core, maps[2], from_pair[0])
    from_chip = moved(next_map, across)
    chip_map, plane_map, offset = plane_composed(core, chip, maps[3], from_pair[1], from_chip)
    plane_map, offset, kept = lax.optimization_barrier((plane_map, offset, [m[1:] for m in made]))

    def read(i):
        return group_reads(
            groups[i], query_rows, key_rows, tails, query_kernel, key_kernel, scalars, kept[i]
        )

    reads = []
    entry = moved(offset, onward)
    for i in range(count // PLANE - 1):
        if i > 0:
            entry = moved(applied(plane_map, entry), onward)
        if len(reads) < PLANE - 1:
            reads.append(read(i))
            entry, reads[-1] = lax.optimization_barrier((entry, reads[-1]))
    send, own_entry, own_send = forked(core, chip, chip_map, from_chip, maps[3], from_pair[1], entry)
    theirs = moved(send, across)
    far_own = moved(own_send, pair)
    reads += [read(i) for i in range(len(reads), PLANE)]
    width = query_rows.shape[1]
    out = finished(groups[3], reads[3:], [own_entry], None, width)
    out = finished(groups[1], reads[1:2], [far_own], out, width)
    theirs, out = lax.optimization_barrier((theirs, out))
    next_entry, next_send = branched(core, maps[2], from_pair[0], theirs)
    far_next = moved(next_send, pair)
    out = finished(groups[2], reads[2:3], [next_entry], out, width)
    far_next, out = lax.optimization_barrier((far_next, out))
    return finished(groups[0], reads[:1], [far_next], out, width)


def solution(mesh):
    rows = P(("groups", "seq"), None)
    return jax.shard_map(
        functools.partial(local, mesh.shape["seq"]),
        mesh=mesh,
        in_specs=(rows, rows, rows, rows, rows, rows, P(), P(), P()),
        out_specs=rows,
        check_vma=False,
    )
```

time: 146 us -> 114 us (0.78)
  Pallas kernels: 114 us -> 91.1 us
  local copies, waits for them, and re-layouts: 11.5 us -> 0 us
  starting transfers between devices: 16.6 us -> 19 us
    pallas_call x4, Pallas kernels: 59.6 us -> 40.9 us  [group_maps(): pl.pallas_call(maps_kernel, grid_spec=pltpu.PrefetchScalarGridSpec(num_sc...]
    unnamed x36 -> x0, local copies, waits for them, and re-layouts: 10.5 us -> none
    pallas_call x8 -> x6, Pallas kernels: 18.1 us -> 13.3 us  [small(): pl.pallas_call(kernel, grid_spec=pltpu.PrefetchScalarGridSpec(num_scalar_...]
    pallas_call x4, Pallas kernels: 27.2 us -> 23 us  [group_reads(): pl.pallas_call(reads_kernel, grid_spec=pltpu.PrefetchScalarGridSpec(num_s...]
    pallas_call x1 -> x4, Pallas kernels: 5.76 us -> 9.2 us  [finished(): pl.pallas_call(finish_kernel, grid_spec=pltpu.PrefetchScalarGridSpec(num_...]
    ppermute x10, starting transfers between devices: 16.6 us -> 19 us  [moved(): lax.ppermute(x, 'seq', pairs)]
    pallas_call x1, Pallas kernels: 1.69 us -> 3.15 us  [prep(): pl.pallas_call(prep_kernel, out_shape=(jax.ShapeDtypeStruct((PLANE, steps...]
  transfers between devices with their start and end apart: 10 -> 10, of which waited for: 2 -> 1; matrix products, arithmetic and copies ran while one was open for 0% -> 0% of each run, Pallas kernels for 58% -> 59%
where the time goes in v2:
time: 114 us; the launch traced here: 112 us
  Pallas kernels  91.1 us (80%)
  starting transfers between devices  19 us (17%)
  waiting for transfers between devices  2.01 us (2%)
    pallas_call x4, Pallas kernels, group_maps(): pl.pallas_call(maps_kernel, grid_spec=pltpu.PrefetchScalarGridSpec(num_sc...  40.9 us
    pallas_call x4, Pallas kernels, group_reads(): pl.pallas_call(reads_kernel, grid_spec=pltpu.PrefetchScalarGridSpec(num_s...  23 us
    ppermute x10, starting transfers between devices, moved(): lax.ppermute(x, 'seq', pairs)  19 us
    pallas_call x6, Pallas kernels, small(): pl.pallas_call(kernel, grid_spec=pltpu.PrefetchScalarGridSpec(num_scalar_...  13.3 us
    pallas_call x4, Pallas kernels, finished(): pl.pallas_call(finish_kernel, grid_spec=pltpu.PrefetchScalarGridSpec(num_...  9.2 us
    pallas_call x1, Pallas kernels, prep(): pl.pallas_call(prep_kernel, out_shape=(jax.ShapeDtypeStruct((PLANE, steps...  3.15 us
  transfers between devices with their start and end apart: 10, of which 1 were waited for; matrix products, arithmetic and copies ran while one was open for 0% of the time, Pallas kernels for 59%

profile of v2, /device:TPU:9, one launch (start us, length us, event | category | flops | bytes accessed | tf_op | source)
XLA Modules:
  0.0 112.3 jit_solution(2118406291253062607)
XLA Ops:
  0.0 1.5 %last_rows.1 = bf16[9,2048]{1,0:T(8,128)(2,1)} custom-call(bf16[256,2048]{1,0:T(8,128)(2,1)} %query_ref.9, bf16[512,2048]{1,0:T(8,128)(2,1)} %key_ref.17, bf16[512,2048]{1,0:T(8,128)(2,1)} %value_ref.9), custom_call_target="tpu_custom_call" | custom-call | tf_op jit(solution)/shard_map/last_rows/pallas_call | solution.py:138
  1.5 3.7 %collective-permute-start = (bf16[9,2048]{1,0:T(8,128)(2,1)}, bf16[9,2048]{1,0:T(8,128)(2,1)S(1)}, u32[]{:S(2)}, u32[]{:S(2)}) collective-permute-start(bf16[9,2048]{1,0:T(8,128)(2,1)} %last_rows.1), channel_id=1, source_target_pairs={{0,1},{1,2},{2,3},{3,4},{4,5},{5,6},{6,7},{7,8},{8,9},{9,10},{10,1... | collective-permute-start | bytes 110600 | tf_op jit(solution)/shard_map/ppermute | solution.py:618
  5.3 3.2 %prep.1 = (f32[4,512,4]{2,1,0:T(8,128)}, f32[4,512,4]{2,1,0:T(8,128)}, f32[16,4,128]{2,1,0:T(4,128)}, f32[4,256,4]{2,1,0:T(8,128)}) custom-call(f32[16,512]{1,0:T(8,128)} %bitcast.9, f32[16,256]{1,0:T(8,128)} %bitcast.10, s32[4,8]{1,0:T(4,128)} %bitcast.11), custom_call_target="tpu_custom_call" | custom-call | tf_op jit(solution)/shard_map/prep/pallas_call | solution.py:152
  8.4 0.0 collective-permute-done.tail_ref
  8.4 10.3 %maps.7 = (f32[4,128,256]{2,1,0:T(8,128)}, bf16[4,512,256]{2,1,0:T(8,128)(2,1)}, bf16[4,512,256]{2,1,0:T(8,128)(2,1)}, bf16[4,384,256]{2,1,0:T(8,128)(2,1)}, bf16[4,384,256]{2,1,0:T(8,128)(2,1)}) custom-call(s32[1]{0:T(128)} %bitcast.group_ref, bf16[512,2048]{1,0:T(8,128)(2,1)} %key_ref.17, bf16[512,2048]{1,0:T(8,128)(2,1)} %value_ref.9, ...), custom_call_target="tpu_custom_call" | custom-call | tf_op jit(solution)/shard_map/maps/pallas_call | solution.py:318
  18.7 0.5 collective-permute-start.2
  19.3 10.2 %maps.5 = (f32[4,128,256]{2,1,0:T(8,128)}, bf16[4,512,256]{2,1,0:T(8,128)(2,1)}, bf16[4,512,256]{2,1,0:T(8,128)(2,1)}, bf16[4,384,256]{2,1,0:T(8,128)(2,1)}, bf16[4,384,256]{2,1,0:T(8,128)(2,1)}) custom-call(s32[1]{0:T(128)} %bitcast.7.group_ref, bf16[512,2048]{1,0:T(8,128)(2,1)} %key_ref.17, bf16[512,2048]{1,0:T(8,128)(2,1)} %value_ref.9, ...), custom_call_target="tpu_custom_call" | custom-call | tf_op jit(solution)/shard_map/maps/pallas_call | solution.py:318
  29.5 0.2 collective-permute-start.1
  29.6 10.2 %maps.6 = (f32[4,128,256]{2,1,0:T(8,128)}, bf16[4,512,256]{2,1,0:T(8,128)(2,1)}, bf16[4,512,256]{2,1,0:T(8,128)(2,1)}, bf16[4,384,256]{2,1,0:T(8,128)(2,1)}, bf16[4,384,256]{2,1,0:T(8,128)(2,1)}) custom-call(s32[1]{0:T(128)} %bitcast.8.group_ref, bf16[512,2048]{1,0:T(8,128)(2,1)} %key_ref.17, bf16[512,2048]{1,0:T(8,128)(2,1)} %value_ref.9, ...), custom_call_target="tpu_custom_call" | custom-call | tf_op jit(solution)/shard_map/maps/pallas_call | solution.py:318
  39.9 0.0 collective-permute-done.2.other_ref
  39.9 2.2 %compose.1 = f32[4,128,256]{2,1,0:T(8,128)} custom-call(s32[1]{0:T(128)} %bitcast.1.core_ref, f32[4,128,256]{2,1,0:T(8,128)} %get-tuple-element.88.mine_ref, f32[4,128,256]{2,1,0:T(8,128)S(1)} %collective-permute-done.2.other_ref), custom_call_target="tpu_custom_call" | custom-call | tf_op jit(solution)/shard_map/compose/pallas_call | solution.py:487
  42.0 1.1 %collective-permute-start.3 = (f32[4,128,256]{2,1,0:T(8,128)}, f32[4,128,256]{2,1,0:T(8,128)S(1)}, u32[]{:S(2)}, u32[]{:S(2)}) collective-permute-start(f32[4,128,256]{2,1,0:T(8,128)} %compose.1), channel_id=1, source_target_pairs={{0,2},{1,3},{2,0},{3,1},{4,6},{5,7},{6,4},{7,5},{8,10},{9,11},{10,... | collective-permute-start | bytes 1572872 | tf_op jit(solution)/shard_map/ppermute | solution.py:618
  43.2 10.2 %maps.4 = (f32[4,128,256]{2,1,0:T(8,128)}, bf16[4,512,256]{2,1,0:T(8,128)(2,1)}, bf16[4,512,256]{2,1,0:T(8,128)(2,1)}, bf16[4,384,256]{2,1,0:T(8,128)(2,1)}, bf16[4,384,256]{2,1,0:T(8,128)(2,1)}) custom-call(s32[1]{0:T(128)} %bitcast.3.group_ref, bf16[512,2048]{1,0:T(8,128)(2,1)} %key_ref.17, bf16[512,2048]{1,0:T(8,128)(2,1)} %value_ref.9, ...), custom_call_target="tpu_custom_call" | custom-call | tf_op jit(solution)/shard_map/maps/pallas_call | solution.py:318
  53.4 0.0 collective-permute-done.1.pair_ref
  53.4 2.0 %collective-permute-done.3.other_ref.from_chip_ref = f32[4,128,256]{2,1,0:T(8,128)S(1)} collective-permute-done((f32[4,128,256]{2,1,0:T(8,128)}, f32[4,128,256]{2,1,0:T(8,128)S(1)}, u32[]{:S(2)}, u32[]{:S(2)}) %collective-permute-start.3) | collective-permute-done | bytes 524320 | tf_op jit(solution)/shard_map/ppermute | solution.py:618
  55.4 2.5 %plane.1 = (f32[4,128,256]{2,1,0:T(8,128)}, f32[4,128,256]{2,1,0:T(8,128)}, f32[4,128,128]{2,1,0:T(8,128)}) custom-call(s32[1]{0:T(128)} %bitcast.1.core_ref, s32[1]{0:T(128)} %bitcast.2.chip_ref, f32[4,128,256]{2,1,0:T(8,128)} %get-tuple-element.86.mine_ref.map_ref, f32[4,128,256]{2,1,0:T(8,128)S(1)} %collective-permute-done.1.pair_ref, ...), custom_call_target="tpu_custom_call" | custom-call | tf_op jit(solution)/shard_map/plane/pallas_call | solution.py:487
  57.9 3.2 %collective-permute-start.4 = (f32[4,128,128]{2,1,0:T(8,128)}, f32[4,128,128]{2,1,0:T(8,128)S(1)}, u32[]{:S(2)}, u32[]{:S(2)}) collective-permute-start(f32[4,128,128]{2,1,0:T(8,128)} %get-tuple-element.108), channel_id=1, source_target_pairs={{0,4},{1,5},{2,6},{3,7},{4,8},{5,9},{6,10},{7,11},{8,12},{9,13},{1... | collective-permute-start | bytes 786440 | tf_op jit(solution)/shard_map/ppermute | solution.py:618
  61.1 5.7 %reads.4 = (bf16[256,512]{1,0:T(8,128)(2,1)}, bf16[256,512]{1,0:T(8,128)(2,1)}, f32[256,512]{1,0:T(8,128)}) custom-call(s32[1]{0:T(128)} %bitcast.group_ref, bf16[256,2048]{1,0:T(8,128)(2,1)} %query_ref.9, bf16[9,2048]{1,0:T(8,128)(2,1)S(1)} %collective-permute-done.tail_ref, f32[4,2048]{1,0:T(4,128)} %query_kernel_ref.7, bf16[512,2048]{1,0:T(8,128)(2,1)} %key_ref.17, ...), custom_call_target="tpu_custom_call" | custom-call | tf_op jit(solution)/shard_map/reads/pallas_call | solution.py:448
  66.8 0.0 collective-permute-done.4.state_ref
  66.8 2.0 %apply.2 = f32[4,128,128]{2,1,0:T(8,128)} custom-call(f32[4,128,256]{2,1,0:T(8,128)} %get-tuple-element.121.map_ref, f32[4,128,128]{2,1,0:T(8,128)S(1)} %collective-permute-done.4.state_ref), custom_call_target="tpu_custom_call" | custom-call | tf_op jit(solution)/shard_map/apply/pallas_call | solution.py:487
  68.8 3.2 %collective-permute-start.5 = (f32[4,128,128]{2,1,0:T(8,128)}, f32[4,128,128]{2,1,0:T(8,128)S(1)}, u32[]{:S(2)}, u32[]{:S(2)}) collective-permute-start(f32[4,128,128]{2,1,0:T(8,128)} %apply.2), channel_id=1, source_target_pairs={{0,4},{1,5},{2,6},{3,7},{4,8},{5,9},{6,10},{7,11},{8,12},{9,13},{1... | collective-permute-start | bytes 786440 | tf_op jit(solution)/shard_map/ppermute | solution.py:618
  72.0 5.7 %reads.5 = (bf16[256,512]{1,0:T(8,128)(2,1)}, bf16[256,512]{1,0:T(8,128)(2,1)}, f32[256,512]{1,0:T(8,128)}) custom-call(s32[1]{0:T(128)} %bitcast.7.group_ref, bf16[256,2048]{1,0:T(8,128)(2,1)} %query_ref.9, bf16[9,2048]{1,0:T(8,128)(2,1)S(1)} %collective-permute-done.tail_ref, f32[4,2048]{1,0:T(4,128)} %query_kernel_ref.7, bf16[512,2048]{1,0:T(8,128)(2,1)} %key_ref.17, ...), custom_call_target="tpu_custom_call" | custom-call | tf_op jit(solution)/shard_map/reads/pallas_call | solution.py:448
  77.7 0.0 collective-permute-done.5.state_ref
  77.7 2.0 %apply.3 = f32[4,128,128]{2,1,0:T(8,128)} custom-call(f32[4,128,256]{2,1,0:T(8,128)} %get-tuple-element.121.map_ref, f32[4,128,128]{2,1,0:T(8,128)S(1)} %collective-permute-done.5.state_ref), custom_call_target="tpu_custom_call" | custom-call | tf_op jit(solution)/shard_map/apply/pallas_call | solution.py:487
  79.7 2.9 %collective-permute-start.6 = (f32[4,128,128]{2,1,0:T(8,128)}, f32[4,128,128]{2,1,0:T(8,128)S(1)}, u32[]{:S(2)}, u32[]{:S(2)}) collective-permute-start(f32[4,128,128]{2,1,0:T(8,128)} %apply.3), channel_id=1, source_target_pairs={{0,4},{1,5},{2,6},{3,7},{4,8},{5,9},{6,10},{7,11},{8,12},{9,13},{1... | collective-permute-start | bytes 786440 | tf_op jit(solution)/shard_map/ppermute | solution.py:618
  82.7 5.9 %reads.6 = (bf16[256,512]{1,0:T(8,128)(2,1)}, bf16[256,512]{1,0:T(8,128)(2,1)}, f32[256,512]{1,0:T(8,128)}) custom-call(s32[1]{0:T(128)} %bitcast.8.group_ref, bf16[256,2048]{1,0:T(8,128)(2,1)} %query_ref.9, bf16[9,2048]{1,0:T(8,128)(2,1)S(1)} %collective-permute-done.tail_ref, f32[4,2048]{1,0:T(4,128)} %query_kernel_ref.7, bf16[512,2048]{1,0:T(8,128)(2,1)} %key_ref.17, ...), custom_call_target="tpu_custom_call" | custom-call | tf_op jit(solution)/shard_map/reads/pallas_call | solution.py:448
  88.6 0.0 collective-permute-done.6.entry_ref
  88.6 2.5 %fork.1 = (f32[4,128,128]{2,1,0:T(8,128)}, f32[4,128,128]{2,1,0:T(8,128)}, f32[4,128,128]{2,1,0:T(8,128)}) custom-call(s32[1]{0:T(128)} %bitcast.1.core_ref, s32[1]{0:T(128)} %bitcast.2.chip_ref, f32[4,128,256]{2,1,0:T(8,128)} %get-tuple-element.120.chip_map_ref, f32[4,128,256]{2,1,0:T(8,128)S(1)} %collective-permute-done.3.other_ref.from_chip_ref, ...), custom_call_target="tpu_custom_call" | custom-call | tf_op jit(solution)/shard_map/fork/pallas_call | solution.py:487
  91.1 2.7 %collective-permute-start.8 = (f32[4,128,128]{2,1,0:T(8,128)}, f32[4,128,128]{2,1,0:T(8,128)S(1)}, u32[]{:S(2)}, u32[]{:S(2)}) collective-permute-start(f32[4,128,128]{2,1,0:T(8,128)} %get-tuple-element.143), channel_id=1, source_target_pairs={{0,1},{1,0},{2,3},{3,2},{4,5},{5,4},{6,7},{7,6},{8,9},{9,8},{10,11... | collective-permute-start | bytes 786440 | tf_op jit(solution)/shard_map/ppermute | solution.py:618
  93.8 1.2 %collective-permute-start.7 = (f32[4,128,128]{2,1,0:T(8,128)}, f32[4,128,128]{2,1,0:T(8,128)S(1)}, u32[]{:S(2)}, u32[]{:S(2)}) collective-permute-start(f32[4,128,128]{2,1,0:T(8,128)} %get-tuple-element.139), channel_id=1, source_target_pairs={{0,2},{1,3},{2,0},{3,1},{4,6},{5,7},{6,4},{7,5},{8,10},{9,11},{10,... | collective-permute-start | bytes 786440 | tf_op jit(solution)/shard_map/ppermute | solution.py:618
  95.0 5.7 %reads.7 = (bf16[256,512]{1,0:T(8,128)(2,1)}, bf16[256,512]{1,0:T(8,128)(2,1)}, f32[256,512]{1,0:T(8,128)}) custom-call(s32[1]{0:T(128)} %bitcast.3.group_ref, bf16[256,2048]{1,0:T(8,128)(2,1)} %query_ref.9, bf16[9,2048]{1,0:T(8,128)(2,1)S(1)} %collective-permute-done.tail_ref, f32[4,2048]{1,0:T(4,128)} %query_kernel_ref.7, bf16[512,2048]{1,0:T(8,128)(2,1)} %key_ref.17, ...), custom_call_target="tpu_custom_call" | custom-call | tf_op jit(solution)/shard_map/reads/pallas_call | solution.py:448
  100.6 2.3 %finish.4.refs_4_ = bf16[256,2048]{1,0:T(8,128)(2,1)} custom-call(s32[1]{0:T(128)} %bitcast.3.group_ref, bf16[256,512]{1,0:T(8,128)(2,1)} %get-tuple-element.148.refs_0_, bf16[256,512]{1,0:T(8,128)(2,1)} %get-tuple-element.149.refs_1_, f32[256,512]{1,0:T(8,128)} %get-tuple-element.150.refs_2_, f32[4,128,128]{2,1,0:T(8,128)} %get-tuple-element.151.refs_3_), custom_call_target="tpu_custom_call" | custom-call | tf_op jit(solution)/shard_map/finish/pallas_call | solution.py:603
  103.0 0.0 collective-permute-done.8.refs_3_
  103.0 2.3 %finish.5.refs_4_ = bf16[256,2048]{1,0:T(8,128)(2,1)} custom-call(s32[1]{0:T(128)} %bitcast.7.group_ref, bf16[256,512]{1,0:T(8,128)(2,1)} %get-tuple-element.140.refs_0_, bf16[256,512]{1,0:T(8,128)(2,1)} %get-tuple-element.141.refs_1_, f32[256,512]{1,0:T(8,128)} %get-tuple-element.142.refs_2_, ...), custom_call_target="tpu_custom_call", output_to_operand_aliasing={{}: (5, {})} | custom-call | tf_op jit(solution)/shard_map/finish/pallas_call | solution.py:603
  105.2 0.0 collective-permute-done.7.entry_ref
  105.2 2.1 %branch.1 = (f32[4,128,128]{2,1,0:T(8,128)}, f32[4,128,128]{2,1,0:T(8,128)}) custom-call(s32[1]{0:T(128)} %bitcast.1.core_ref, f32[4,128,256]{2,1,0:T(8,128)} %get-tuple-element.88.mine_ref, f32[4,128,256]{2,1,0:T(8,128)S(1)} %collective-permute-done.2.other_ref, f32[4,128,128]{2,1,0:T(8,128)S(1)} %collective-permute-done.7.entry_ref), custom_call_target="tpu_custom_call" | custom-call | tf_op jit(solution)/shard_map/branch/pallas_call | solution.py:487
  107.4 0.3 collective-permute-start.9
  107.6 2.3 %finish.6.refs_4_ = bf16[256,2048]{1,0:T(8,128)(2,1)} custom-call(s32[1]{0:T(128)} %bitcast.8.group_ref, bf16[256,512]{1,0:T(8,128)(2,1)} %get-tuple-element.154.refs_0_, bf16[256,512]{1,0:T(8,128)(2,1)} %get-tuple-element.155.refs_1_, f32[256,512]{1,0:T(8,128)} %get-tuple-element.156.refs_2_, ...), custom_call_target="tpu_custom_call", output_to_operand_aliasing={{}: (5, {})} | custom-call | tf_op jit(solution)/shard_map/finish/pallas_call | solution.py:603
  110.0 0.0 collective-permute-done.9.refs_3_
  110.0 2.3 %finish.7 = bf16[256,2048]{1,0:T(8,128)(2,1)} custom-call(s32[1]{0:T(128)} %bitcast.group_ref, bf16[256,512]{1,0:T(8,128)(2,1)} %get-tuple-element.117.refs_0_, bf16[256,512]{1,0:T(8,128)(2,1)} %get-tuple-element.118.refs_1_, f32[256,512]{1,0:T(8,128)} %get-tuple-element.119.refs_2_, ...), custom_call_target="tpu_custom_call", output_to_operand_aliasing={{}: (5, {})} | custom-call | tf_op jit(solution)/shard_map/finish/pallas_call | solution.py:603
Async XLA Ops:
  1.5 6.9 %collective-permute-start = (bf16[9,2048]{1,0:T(8,128)(2,1)}, bf16[9,2048]{1,0:T(8,128)(2,1)S(1)}, u32[]{:S(2)}, u32[]{:S(2)}) collective-permute-start(bf16[9,2048]{1,0:T(8,128)(2,1)} %last_rows.1), channel_id=1, source_target_pairs={{0,1},{1,2},{2,3},{3,4},{4,5},{5,6},{6,7},{7,8},{8,9},{9,10},{10,1... | collective-permute-start | bytes 110600 | tf_op jit(solution)/shard_map/ppermute | solution.py:618
  18.7 21.1 %collective-permute-start.2 = (f32[4,128,256]{2,1,0:T(8,128)}, f32[4,128,256]{2,1,0:T(8,128)S(1)}, u32[]{:S(2)}, u32[]{:S(2)}) collective-permute-start(f32[4,128,256]{2,1,0:T(8,128)} %get-tuple-element.89), channel_id=1, source_target_pairs={{0,1},{1,0},{2,3},{3,2},{4,5},{5,4},{6,7},{7,6},{8,9},{9,8},{10,11... | collective-permute-start | bytes 1572872 | tf_op jit(solution)/shard_map/ppermute | solution.py:618
  29.5 23.9 %collective-permute-start.1 = (f32[4,128,256]{2,1,0:T(8,128)}, f32[4,128,256]{2,1,0:T(8,128)S(1)}, u32[]{:S(2)}, u32[]{:S(2)}) collective-permute-start(f32[4,128,256]{2,1,0:T(8,128)} %get-tuple-element.87), channel_id=1, source_target_pairs={{0,1},{1,0},{2,3},{3,2},{4,5},{5,4},{6,7},{7,6},{8,9},{9,8},{10,11... | collective-permute-start | bytes 1572872 | tf_op jit(solution)/shard_map/ppermute | solution.py:618
  42.0 13.3 %collective-permute-start.3 = (f32[4,128,256]{2,1,0:T(8,128)}, f32[4,128,256]{2,1,0:T(8,128)S(1)}, u32[]{:S(2)}, u32[]{:S(2)}) collective-permute-start(f32[4,128,256]{2,1,0:T(8,128)} %compose.1), channel_id=1, source_target_pairs={{0,2},{1,3},{2,0},{3,1},{4,6},{5,7},{6,4},{7,5},{8,10},{9,11},{10,... | collective-permute-start | bytes 1572872 | tf_op jit(solution)/shard_map/ppermute | solution.py:618
  57.9 8.9 %collective-permute-start.4 = (f32[4,128,128]{2,1,0:T(8,128)}, f32[4,128,128]{2,1,0:T(8,128)S(1)}, u32[]{:S(2)}, u32[]{:S(2)}) collective-permute-start(f32[4,128,128]{2,1,0:T(8,128)} %get-tuple-element.108), channel_id=1, source_target_pairs={{0,4},{1,5},{2,6},{3,7},{4,8},{5,9},{6,10},{7,11},{8,12},{9,13},{1... | collective-permute-start | bytes 786440 | tf_op jit(solution)/shard_map/ppermute | solution.py:618
  68.8 8.9 %collective-permute-start.5 = (f32[4,128,128]{2,1,0:T(8,128)}, f32[4,128,128]{2,1,0:T(8,128)S(1)}, u32[]{:S(2)}, u32[]{:S(2)}) collective-permute-start(f32[4,128,128]{2,1,0:T(8,128)} %apply.2), channel_id=1, source_target_pairs={{0,4},{1,5},{2,6},{3,7},{4,8},{5,9},{6,10},{7,11},{8,12},{9,13},{1... | collective-permute-start | bytes 786440 | tf_op jit(solution)/shard_map/ppermute | solution.py:618
  79.7 8.9 %collective-permute-start.6 = (f32[4,128,128]{2,1,0:T(8,128)}, f32[4,128,128]{2,1,0:T(8,128)S(1)}, u32[]{:S(2)}, u32[]{:S(2)}) collective-permute-start(f32[4,128,128]{2,1,0:T(8,128)} %apply.3), channel_id=1, source_target_pairs={{0,4},{1,5},{2,6},{3,7},{4,8},{5,9},{6,10},{7,11},{8,12},{9,13},{1... | collective-permute-start | bytes 786440 | tf_op jit(solution)/shard_map/ppermute | solution.py:618
  91.1 11.9 %collective-permute-start.8 = (f32[4,128,128]{2,1,0:T(8,128)}, f32[4,128,128]{2,1,0:T(8,128)S(1)}, u32[]{:S(2)}, u32[]{:S(2)}) collective-permute-start(f32[4,128,128]{2,1,0:T(8,128)} %get-tuple-element.143), channel_id=1, source_target_pairs={{0,1},{1,0},{2,3},{3,2},{4,5},{5,4},{6,7},{7,6},{8,9},{9,8},{10,11... | collective-permute-start | bytes 786440 | tf_op jit(solution)/shard_map/ppermute | solution.py:618
  93.8 11.5 %collective-permute-start.7 = (f32[4,128,128]{2,1,0:T(8,128)}, f32[4,128,128]{2,1,0:T(8,128)S(1)}, u32[]{:S(2)}, u32[]{:S(2)}) collective-permute-start(f32[4,128,128]{2,1,0:T(8,128)} %get-tuple-element.139), channel_id=1, source_target_pairs={{0,2},{1,3},{2,0},{3,1},{4,6},{5,7},{6,4},{7,5},{8,10},{9,11},{10,... | collective-permute-start | bytes 786440 | tf_op jit(solution)/shard_map/ppermute | solution.py:618
  107.4 2.6 %collective-permute-start.9 = (f32[4,128,128]{2,1,0:T(8,128)}, f32[4,128,128]{2,1,0:T(8,128)S(1)}, u32[]{:S(2)}, u32[]{:S(2)}) collective-permute-start(f32[4,128,128]{2,1,0:T(8,128)} %get-tuple-element.153), channel_id=1, source_target_pairs={{0,1},{1,0},{2,3},{3,2},{4,5},{5,4},{6,7},{7,6},{8,9},{9,8},{10,11... | collective-permute-start | bytes 786440 | tf_op jit(solution)/shard_map/ppermute | solution.py:618

commit v3 on v2

--- a/solution.py
+++ b/solution.py
@@ -15,7 +15,10 @@
 HALF = 64
 PLANE = 4
 HB = 2
-VMEM = 56 << 20
+VMEM = 24 << 20
+SMALL = pltpu.CompilerParams(vmem_limit_bytes=8 << 20)
+
+WHOLE = pl.BlockSpec(memory_space=pltpu.VMEM)
 
 F32 = jnp.float32
 BF16 = jnp.bfloat16
@@ -59,10 +62,10 @@
     return v / (1.0 + jnp.exp(-v))
 
 
-def load_rows(scratch, rows_ref, tail):
+def load_rows(scratch, rows_ref, lanes, tail):
     before = jnp.concatenate([jnp.zeros((13, tail.shape[1]), F32), tail.astype(F32)], axis=0)
     scratch[0:16, :] = before.astype(BF16)
-    scratch[16 : 16 + rows_ref.shape[0], :] = rows_ref[...]
+    scratch[16 : 16 + rows_ref.shape[0], :] = rows_ref[:, lanes]
 
 
 def shifter():
@@ -86,11 +89,42 @@
     return x * lax.rsqrt(jnp.sum(x * x, axis=-1, keepdims=True) + 1e-06)
 
 
+CORE, CHIP, GROUPS = 0, 1, 2
+FLAGS = jax.ShapeDtypeStruct((8,), jnp.int32)
+FLAGS_SPEC = pl.BlockSpec(memory_space=pltpu.SMEM)
+TOKEN = pltpu.VMEM((8, 128), jnp.int32)
+
+
+def hand_on(token_ref, token_out):
+    token_out[...] = token_ref[...]
+
+
+def lanes_at(flags_ref, which, at, group):
+    first = flags_ref[GROUPS + which] * group + at * HB
+    return pl.ds(pl.multiple_of(first * DK, HB * DK), HB * DK)
+
+
+def in_hbm(x):
+    return pltpu.with_memory_space_constraint(x, pltpu.HBM)
+
+
+def held(x):
+    return pltpu.with_memory_space_constraint(x, pltpu.VMEM)
+
+
 def iota(shape, dim):
     return lax.broadcasted_iota(jnp.int32, shape, dim)
 
 
-def prep_kernel(rate_ref, log_ref, mask_ref, rate_out, cum_out, row_out, read_out):
+def prep_kernel(at_ref, rate_ref, log_ref, mask_ref, rate_out, cum_out, row_out, read_out, flags_out, token_out):
+    token_out[...] = jnp.zeros_like(token_out)
+    place = lax.rem(at_ref[0], PLANE)
+    flags_out[CORE] = lax.rem(place, 2)
+    flags_out[CHIP] = lax.div(place, 2)
+    for i, other in enumerate((3, 1, 2, 0)):
+        flags_out[GROUPS + i] = place ^ other
+    for i in range(GROUPS + PLANE, FLAGS.shape[0]):
+        flags_out[i] = 0
     heads, steps = rate_ref.shape
     tokens = log_ref.shape[1]
     group = heads // PLANE
@@ -141,11 +175,12 @@
         in_specs=[pl.BlockSpec((16, width), functools.partial(lambda at, i: (at, 0), x.shape[0] // 16 - 1)) for x in arrays],
         out_specs=pl.BlockSpec((9, width), lambda i: (0, 0)),
         out_shape=jax.ShapeDtypeStruct((9, width), BF16),
+        compiler_params=SMALL,
         name="last_rows",
-    )(*arrays)
-
-
-def prep(write_rate, log_gate, keep_mask):
+    )(*map(in_hbm, arrays))
+
+
+def prep(at, write_rate, log_gate, keep_mask):
     steps, heads = write_rate.shape
     tokens = log_gate.shape[0]
     group = heads // PLANE
@@ -156,10 +191,14 @@
             jax.ShapeDtypeStruct((PLANE, steps, group), F32),
             jax.ShapeDtypeStruct((heads, steps // CHUNK, CHUNK), F32),
             jax.ShapeDtypeStruct((PLANE, tokens, group), F32),
+            FLAGS,
+            TOKEN,
         ),
+        in_specs=[FLAGS_SPEC] + [WHOLE] * 3,
+        out_specs=[WHOLE] * 4 + [FLAGS_SPEC, WHOLE],
         compiler_params=pltpu.CompilerParams(vmem_limit_bytes=VMEM),
         name="prep",
-    )(write_rate.T, log_gate.T, keep_mask.T)
+    )(at, write_rate.T, log_gate.T, keep_mask.T)
 
 
 def block_inverses(lowers, fill):
@@ -186,7 +225,8 @@
 
 
 def maps_kernel(
-    group_ref,
+    which,
+    flags_ref,
     key_ref,
     value_ref,
     tail_ref,
@@ -195,19 +235,23 @@
     rate_ref,
     cum_ref,
     row_ref,
+    token_ref,
     map_out,
     wh_out,
     wl_out,
     mh_out,
     ml_out,
+    token_out,
     scratch,
     value_scratch,
 ):
+    hand_on(token_ref, token_out)
     steps = key_ref.shape[0]
     chunks = steps // CHUNK
     at = pl.program_id(0)
-    load_rows(scratch, key_ref, tail_ref[3:6, :])
-    load_rows(value_scratch, value_ref, tail_ref[6:9, :])
+    lanes = lanes_at(flags_ref, which, at, rate_ref.shape[2])
+    load_rows(scratch, key_ref, lanes, tail_ref[3:6, :])
+    load_rows(value_scratch, value_ref, lanes, tail_ref[6:9, :])
     shifts = shifter()
     keys = conv(shifts, scratch, key_kernel_ref, 0, steps)
     keys = jnp.concatenate([unit(keys[:, h * DK : (h + 1) * DK]) for h in range(HB)], axis=1)
@@ -277,7 +321,7 @@
     solved = [split(mm3(x, sides[i])) for i, x in zip(items, whole)]
     for (h, c), x in zip(items, solved):
         at_w = slice(c * CHUNK, (c + 1) * CHUNK)
-        wh_out[h, at_w, :], wl_out[h, at_w, :] = x
+        wh_out[at * HB + h, at_w, :], wl_out[at * HB + h, at_w, :] = x
     made = [mm3(faded[i], x) for i, x in zip(items, solved)]
     made = [jnp.concatenate([ends[i] * eye - x[:, :DK], x[:, DK:]], axis=1) for i, x in zip(items, made)]
 
@@ -292,12 +336,13 @@
     last = [then(made[h * chunks + 3], third[h]) for h in heads]
     last = [then(last[h], two[h]) for h in heads]
     for h in heads:
-        map_out[h] = last[h]
+        map_out[at * HB + h] = last[h]
         for i, x in enumerate((first[h], two[h], third[h])):
-            mh_out[h, i * DK : (i + 1) * DK, :], ml_out[h, i * DK : (i + 1) * DK, :] = x
-
-
-def group_maps(which, key_rows, value_rows, tails, key_kernel, value_kernel, scalars):
+            at_m = slice(i * DK, (i + 1) * DK)
+            mh_out[at * HB + h, at_m, :], ml_out[at * HB + h, at_m, :] = x
+
+
+def group_maps(flags, token, which, key_rows, value_rows, tails, key_kernel, value_kernel, scalars):
     rate_cols, cum_cols, chunk_rows, _ = scalars
     steps, width = key_rows.shape
     heads = width // DK
@@ -307,52 +352,53 @@
     chunks = steps // CHUNK
 
     def wide(i, g):
-        return (0, g[0] * turns + i)
+        return (0, g[GROUPS + which] * turns + i)
 
     def per_head(i, g):
-        return (g[0] * turns + i, 0, 0)
-
-    def local(i, g):
-        return (i, 0, 0)
+        return (g[GROUPS + which] * turns + i, 0, 0)
 
     return pl.pallas_call(
-        maps_kernel,
+        functools.partial(maps_kernel, which),
         grid_spec=pltpu.PrefetchScalarGridSpec(
             num_scalar_prefetch=1,
             grid=(turns,),
             in_specs=[
-                pl.BlockSpec((steps, lanes), wide),
-                pl.BlockSpec((steps, lanes), wide),
+                WHOLE,
+                WHOLE,
                 pl.BlockSpec((tails.shape[0], lanes), wide),
                 pl.BlockSpec((4, lanes), wide),
                 pl.BlockSpec((4, lanes), wide),
-                pl.BlockSpec((1, steps, group), lambda i, g: (g[0], 0, 0)),
-                pl.BlockSpec((1, steps, group), lambda i, g: (g[0], 0, 0)),
+                pl.BlockSpec((1, steps, group), lambda i, g: (g[GROUPS + which], 0, 0)),
+                pl.BlockSpec((1, steps, group), lambda i, g: (g[GROUPS + which], 0, 0)),
                 pl.BlockSpec((HB, chunks, CHUNK), per_head),
+                WHOLE,
             ],
             out_specs=[
-                pl.BlockSpec((HB, DK, 2 * DK), local),
-                pl.BlockSpec((HB, steps, 2 * DK), local),
-                pl.BlockSpec((HB, steps, 2 * DK), local),
-                pl.BlockSpec((HB, 3 * DK, 2 * DK), local),
-                pl.BlockSpec((HB, 3 * DK, 2 * DK), local),
+                WHOLE,
+                WHOLE,
+                WHOLE,
+                WHOLE,
+                WHOLE,
+                WHOLE,
             ],
             scratch_shapes=[pltpu.VMEM((steps + 16, lanes), BF16)] * 2,
         ),
         out_shape=(
-            jax.ShapeDtypeStruct((group, DK, 2 * DK), F32),
-            jax.ShapeDtypeStruct((group, steps, 2 * DK), BF16),
-            jax.ShapeDtypeStruct((group, steps, 2 * DK), BF16),
-            jax.ShapeDtypeStruct((group, 3 * DK, 2 * DK), BF16),
-            jax.ShapeDtypeStruct((group, 3 * DK, 2 * DK), BF16),
+            pltpu.VMEM((group, DK, 2 * DK), F32),
+            pltpu.VMEM((group, steps, 2 * DK), BF16),
+            pltpu.VMEM((group, steps, 2 * DK), BF16),
+            pltpu.VMEM((group, 3 * DK, 2 * DK), BF16),
+            pltpu.VMEM((group, 3 * DK, 2 * DK), BF16),
+            TOKEN,
         ),
         compiler_params=pltpu.CompilerParams(vmem_limit_bytes=VMEM),
         name="maps",
-    )(which, key_rows, value_rows, tails, key_kernel, value_kernel, rate_cols, cum_cols, chunk_rows)
+    )(flags, key_rows, value_rows, tails, key_kernel, value_kernel, rate_cols, cum_cols, chunk_rows, held(token))
 
 
 def reads_kernel(
-    group_ref,
+    which,
+    flags_ref,
     query_ref,
     tail_ref,
     query_kernel_ref,
@@ -364,21 +410,25 @@
     wl_ref,
     mh_ref,
     ml_ref,
+    token_ref,
     qh_out,
     ql_out,
     own_out,
+    token_out,
     scratch,
     key_scratch,
 ):
+    hand_on(token_ref, token_out)
     tokens = query_ref.shape[0]
     window = CHUNK // NH
     chunks = tokens // window
     at = pl.program_id(0)
-    load_rows(scratch, query_ref, tail_ref[0:3, :])
+    lanes = lanes_at(flags_ref, which, at, read_ref.shape[2])
+    load_rows(scratch, query_ref, lanes, tail_ref[0:3, :])
     shifts = shifter()
     queries = conv(shifts, scratch, query_kernel_ref, 0, tokens)
     queries = jnp.concatenate([unit(queries[:, h * DK : (h + 1) * DK]) for h in range(HB)], axis=1)
-    load_rows(key_scratch, key_ref, tail_ref[3:6, :])
+    load_rows(key_scratch, key_ref, lanes, tail_ref[3:6, :])
     keys = conv(shifts, key_scratch, key_kernel_ref, 0, NH * tokens)
     group = read_ref.shape[2]
     reads = read_ref[0]
@@ -406,7 +456,7 @@
     ]
     starts = {}
     for h in range(HB):
-        kept = [(mh_ref[h, i * DK : (i + 1) * DK, :], ml_ref[h, i * DK : (i + 1) * DK, :]) for i in range(3)]
+        kept = [tuple(x[at * HB + h, i * DK : (i + 1) * DK, :] for x in (mh_ref, ml_ref)) for i in range(3)]
         first, two, third = kept
         three = mm3(tuple(x[:, :DK] for x in third), two)
         late = third[0][:, DK:].astype(F32) + third[1][:, DK:].astype(F32)
@@ -416,17 +466,18 @@
     for (h, c), x in zip(items, scores):
         spread = columns[h][tokens_of(c)] - row_ref[h, c : c + 1, :]
         inner.append(split(jnp.where(visible, jnp.exp(jnp.where(visible, spread, 0.0)) * x, 0.0)))
-    got = [mm3(x, (wh_ref[h, steps_of(c), :], wl_ref[h, steps_of(c), :])) for (h, c), x in zip(items, inner)]
+    solved = [tuple(x[at * HB + h, steps_of(c), :] for x in (wh_ref, wl_ref)) for h, c in items]
+    got = [mm3(x, y) for x, y in zip(inner, solved)]
     eff = [lifted[h][tokens_of(c)] - x[:, :DK] for (h, c), x in zip(items, got)]
     eff_pieces = [split(x) for x in eff]
     taken = [None if c == 0 else mm3(x, starts[h][c]) for (h, c), x in zip(items, eff_pieces)]
     for (h, c), x, y, z in zip(items, eff_pieces, got, taken):
-        at_out = (tokens_of(c), slice(h * DK, (h + 1) * DK))
+        at_out = (at * HB + h, tokens_of(c))
         qh_out[at_out], ql_out[at_out] = x if c == 0 else split(z[:, :DK])
         own_out[at_out] = y[:, DK:] if c == 0 else y[:, DK:] + z[:, DK:]
 
 
-def group_reads(which, query_rows, key_rows, tails, query_kernel, key_kernel, scalars, kept):
+def group_reads(flags, token, which, query_rows, key_rows, tails, query_kernel, key_kernel, scalars, kept):
     _, _, chunk_rows, read_cols = scalars
     tokens, width = query_rows.shape
     steps = tokens * NH
@@ -437,64 +488,61 @@
     chunks = steps // CHUNK
 
     def wide(i, g):
-        return (0, g[0] * turns + i)
-
-    def here(i, g):
-        return (0, i)
-
-    def local(i, g):
-        return (i, 0, 0)
+        return (0, g[GROUPS + which] * turns + i)
 
     return pl.pallas_call(
-        reads_kernel,
+        functools.partial(reads_kernel, which),
         grid_spec=pltpu.PrefetchScalarGridSpec(
             num_scalar_prefetch=1,
             grid=(turns,),
             in_specs=[
-                pl.BlockSpec((tokens, lanes), wide),
+                WHOLE,
                 pl.BlockSpec((tails.shape[0], lanes), wide),
                 pl.BlockSpec((4, lanes), wide),
-                pl.BlockSpec((steps, lanes), wide),
+                WHOLE,
                 pl.BlockSpec((4, lanes), wide),
-                pl.BlockSpec((1, tokens, group), lambda i, g: (g[0], 0, 0)),
-                pl.BlockSpec((HB, chunks, CHUNK), lambda i, g: (g[0] * turns + i, 0, 0)),
-                pl.BlockSpec((HB, steps, 2 * DK), local),
-                pl.BlockSpec((HB, steps, 2 * DK), local),
-                pl.BlockSpec((HB, 3 * DK, 2 * DK), local),
-                pl.BlockSpec((HB, 3 * DK, 2 * DK), local),
+                pl.BlockSpec((1, tokens, group), lambda i, g: (g[GROUPS + which], 0, 0)),
+                pl.BlockSpec((HB, chunks, CHUNK), lambda i, g: (g[GROUPS + which] * turns + i, 0, 0)),
+                WHOLE,
+                WHOLE,
+                WHOLE,
+                WHOLE,
+                WHOLE,
             ],
-            out_specs=[
-                pl.BlockSpec((tokens, lanes), here),
-                pl.BlockSpec((tokens, lanes), here),
-                pl.BlockSpec((tokens, lanes), here),
-            ],
+            out_specs=[WHOLE] * 4,
             scratch_shapes=[pltpu.VMEM((tokens + 16, lanes), BF16), pltpu.VMEM((steps + 16, lanes), BF16)],
         ),
         out_shape=(
-            jax.ShapeDtypeStruct((tokens, group * DK), BF16),
-            jax.ShapeDtypeStruct((tokens, group * DK), BF16),
-            jax.ShapeDtypeStruct((tokens, group * DK), F32),
+            pltpu.VMEM((group, tokens, DK), BF16),
+            pltpu.VMEM((group, tokens, DK), BF16),
+            pltpu.VMEM((group, tokens, DK), F32),
+            TOKEN,
         ),
         compiler_params=pltpu.CompilerParams(vmem_limit_bytes=VMEM),
         name="reads",
-    )(which, query_rows, tails, query_kernel, key_rows, key_kernel, read_cols, chunk_rows, *kept)
-
-
-def small(kernel, flags, operands, outs, name):
+    )(flags, query_rows, tails, query_kernel, key_rows, key_kernel, read_cols, chunk_rows, *map(held, kept), held(token))
+
+
+def small(kernel, flags, token, operands, outs, name):
     def whole(shape):
-        return pl.BlockSpec(shape, lambda i, *_: (0,) * len(shape))
+        return pl.BlockSpec(shape, lambda i, f: (0,) * len(shape))
+
+    def body(flags_ref, token_ref, *refs):
+        hand_on(token_ref, refs[-1])
+        kernel(flags_ref, *refs[:-1])
 
     return pl.pallas_call(
-        kernel,
+        body,
         grid_spec=pltpu.PrefetchScalarGridSpec(
-            num_scalar_prefetch=len(flags),
+            num_scalar_prefetch=1,
             grid=(1,),
-            in_specs=[whole(x.shape) for x in operands],
-            out_specs=[whole(shape) for shape in outs],
+            in_specs=[WHOLE] + [whole(x.shape) for x in operands],
+            out_specs=[whole(shape) for shape in outs] + [WHOLE],
         ),
-        out_shape=[jax.ShapeDtypeStruct(shape, F32) for shape in outs],
+        out_shape=[jax.ShapeDtypeStruct(shape, F32) for shape in outs] + [TOKEN],
+        compiler_params=SMALL,
         name=name,
-    )(*flags, *operands)
+    )(flags, held(token), *operands)
 
 
 def after(first, mine, other):
@@ -504,42 +552,42 @@
     return jnp.concatenate([both[:, :DK], both[:, DK:] + late[:, DK:]], axis=1)
 
 
-def compose_kernel(core_ref, mine_ref, other_ref, out_ref):
+def compose_kernel(flags_ref, mine_ref, other_ref, out_ref):
     heads = range(mine_ref.shape[0])
-    for h, x in enumerate([after(core_ref[0] == 0, mine_ref[h], other_ref[h]) for h in heads]):
+    for h, x in enumerate([after(flags_ref[CORE] == 0, mine_ref[h], other_ref[h]) for h in heads]):
         out_ref[h] = x
 
 
-def composed(core, mine, other):
-    return small(compose_kernel, [core], [mine, other], [mine.shape], "compose")[0]
-
-
-def plane_kernel(core_ref, chip_ref, mine_ref, pair_ref, other_ref, chip_out, plane_out, offset_out):
+def composed(flags, token, mine, other):
+    return small(compose_kernel, flags, token, [mine, other], [mine.shape], "compose")
+
+
+def plane_kernel(flags_ref, mine_ref, pair_ref, other_ref, chip_out, plane_out, offset_out):
     heads = range(mine_ref.shape[0])
-    chips = [after(core_ref[0] == 0, mine_ref[h], pair_ref[h]) for h in heads]
-    planes = [after(chip_ref[0] == 0, chips[h], other_ref[h]) for h in heads]
+    chips = [after(flags_ref[CORE] == 0, mine_ref[h], pair_ref[h]) for h in heads]
+    planes = [after(flags_ref[CHIP] == 0, chips[h], other_ref[h]) for h in heads]
     for h in heads:
         chip_out[h] = chips[h]
         plane_out[h] = planes[h]
         offset_out[h] = planes[h][:, DK:]
 
 
-def plane_composed(core, chip, mine, pair, other):
+def plane_composed(flags, token, mine, pair, other):
     heads = mine.shape[0]
     return small(
-        plane_kernel, [core, chip], [mine, pair, other], [mine.shape, mine.shape, (heads, DK, DK)], "plane"
+        plane_kernel, flags, token, [mine, pair, other], [mine.shape, mine.shape, (heads, DK, DK)], "plane"
     )
 
 
-def apply_kernel(map_ref, state_ref, out_ref):
+def apply_kernel(flags_ref, map_ref, state_ref, out_ref):
     heads = range(map_ref.shape[0])
     got = [mm3(split(map_ref[h, :, :DK]), split(state_ref[h])) for h in heads]
     for h in heads:
         out_ref[h] = got[h] + map_ref[h, :, DK:]
 
 
-def applied(maps, state):
-    return small(apply_kernel, [], [maps, state], [state.shape], "apply")[0]
+def applied(flags, token, maps, state):
+    return small(apply_kernel, flags, token, [maps, state], [state.shape], "apply")
 
 
 def branches(first, mine, other, entry):
@@ -550,53 +598,46 @@
     return own, [jnp.where(first, later[h], entry[h]) for h in heads]
 
 
-def branch_kernel(core_ref, mine_ref, other_ref, entry_ref, keep_out, send_out):
+def branch_kernel(flags_ref, mine_ref, other_ref, entry_ref, keep_out, send_out):
     refs = (mine_ref, other_ref, entry_ref)
-    own, send = branches(core_ref[0] == 0, *([x[h] for h in range(x.shape[0])] for x in refs))
+    own, send = branches(flags_ref[CORE] == 0, *([x[h] for h in range(x.shape[0])] for x in refs))
     for h in range(len(own)):
         keep_out[h] = own[h]
         send_out[h] = send[h]
 
 
-def branched(core, mine, other, entry):
-    return small(branch_kernel, [core], [mine, other, entry], [entry.shape] * 2, "branch")
-
-
-def fork_kernel(core_ref, chip_ref, chip_map_ref, from_chip_ref, map_ref, pair_ref, entry_ref, *outs):
+def branched(flags, token, mine, other, entry):
+    return small(branch_kernel, flags, token, [mine, other, entry], [entry.shape] * 2, "branch")
+
+
+def fork_kernel(flags_ref, chip_map_ref, from_chip_ref, map_ref, pair_ref, entry_ref, *outs):
     refs = (chip_map_ref, from_chip_ref, map_ref, pair_ref, entry_ref)
     chip_map, from_chip, mine, pair, entry = ([x[h] for h in range(x.shape[0])] for x in refs)
-    own, across = branches(chip_ref[0] == 0, chip_map, from_chip, entry)
-    for out_ref, states in zip(outs, (across, *branches(core_ref[0] == 0, mine, pair, own))):
+    own, across = branches(flags_ref[CHIP] == 0, chip_map, from_chip, entry)
+    for out_ref, states in zip(outs, (across, *branches(flags_ref[CORE] == 0, mine, pair, own))):
         for h, state in enumerate(states):
             out_ref[h] = state
 
 
-def forked(core, chip, chip_map, from_chip, mine, pair, entry):
+def forked(flags, token, chip_map, from_chip, mine, pair, entry):
     operands = [chip_map, from_chip, mine, pair, entry]
-    return small(fork_kernel, [core, chip], operands, [entry.shape] * 3, "fork")
-
-
-def finish_kernel(group_ref, *refs):
-    out_ref = refs[-1]
-    count = (len(refs) - 1) // 4
-    for turn in range(count):
-        qh_ref, ql_ref, own_ref, entry_ref = refs[4 * turn : 4 * turn + 4]
-
-        @pl.when(pl.program_id(0) == turn)
-        def _():
-            for h in range(entry_ref.shape[0]):
-                lanes = slice(h * DK, (h + 1) * DK)
-                got = mm3((qh_ref[:, lanes], ql_ref[:, lanes]), split(entry_ref[h]))
-                out_ref[:, lanes] = (own_ref[:, lanes] + got).astype(BF16)
-
-
-def finished(order, reads, entries, out, width):
-    tokens, lanes = reads[0][0].shape
-    operands, specs = [], []
-    for (qh, ql, own), entry in zip(reads, entries):
-        operands += [qh, ql, own, entry]
-        specs += [pl.BlockSpec((tokens, lanes), lambda i, g: (0, 0))] * 3
-        specs += [pl.BlockSpec(entry.shape, lambda i, g: (0, 0, 0))]
+    return small(fork_kernel, flags, token, operands, [entry.shape] * 3, "fork")
+
+
+def finish_kernel(flags_ref, token_ref, qh_ref, ql_ref, own_ref, entry_ref, *refs):
+    out_ref, token_out = refs[-2:]
+    hand_on(token_ref, token_out)
+    for h in range(entry_ref.shape[0]):
+        lanes = slice(h * DK, (h + 1) * DK)
+        got = mm3((qh_ref[h], ql_ref[h]), split(entry_ref[h]))
+        out_ref[:, lanes] = (own_ref[h] + got).astype(BF16)
+
+
+def finished(flags, token, which, read, entry, out, width):
+    qh, ql, own, _ = read
+    group, tokens, _ = qh.shape
+    operands = [held(token), held(qh), held(ql), held(own), entry]
+    specs = [WHOLE] * 4 + [pl.BlockSpec(entry.shape, lambda i, g: (0, 0, 0))]
     if out is not None:
         operands.append(out)
         specs.append(pl.BlockSpec(memory_space=pl.ANY))
@@ -604,14 +645,15 @@
         finish_kernel,
         grid_spec=pltpu.PrefetchScalarGridSpec(
             num_scalar_prefetch=1,
-            grid=(len(reads),),
+            grid=(1,),
             in_specs=specs,
-            out_specs=pl.BlockSpec((tokens, lanes), lambda i, g: (0, g[i])),
+            out_specs=[pl.BlockSpec((tokens, group * DK), lambda i, g: (0, g[GROUPS + which])), WHOLE],
         ),
-        out_shape=jax.ShapeDtypeStruct((tokens, width), BF16),
+        out_shape=[jax.ShapeDtypeStruct((tokens, width), BF16), TOKEN],
         input_output_aliases={} if out is None else {len(operands): 0},
+        compiler_params=SMALL,
         name="finish",
-    )(order, *operands)
+    )(flags, *operands)
 
 
 def moved(x, pairs):
@@ -631,48 +673,51 @@
     value_kernel,
 ):
     tails = moved(last_rows(query_rows, key_rows, value_rows), [(s, s + 1) for s in range(count - 1)])
-    scalars = prep(write_rate, log_gate, keep_mask)
-    place = lax.axis_index("seq") % PLANE
-    core = (place % 2)[None]
-    chip = (place // 2)[None]
+    query_rows, key_rows, value_rows = held(query_rows), held(key_rows), held(value_rows)
+    query_kernel, key_kernel, value_kernel = held(query_kernel), held(key_kernel), held(value_kernel)
+    *scalars, flags, token = prep(lax.axis_index("seq")[None], write_rate, log_gate, keep_mask)
     pair = [(s, s ^ 1) for s in range(count)]
     across = [(s, s ^ 2) for s in range(count)]
     onward = [(s, s + PLANE) for s in range(count - PLANE)]
-    groups = [(place ^ x)[None] for x in (3, 1, 2, 0)]
-    made = [group_maps(g, key_rows, value_rows, tails, key_kernel, value_kernel, scalars) for g in groups]
+    made, from_pair = [], []
+    for i in range(PLANE):
+        *one, token = group_maps(flags, token, i, key_rows, value_rows, tails, key_kernel, value_kernel, scalars)
+        made.append(one)
+        if i < 2:
+            from_pair.append(moved(one[0], pair))
+        if i == 2:
+            next_map, token = composed(flags, token, one[0], from_pair[0])
+            from_chip = moved(next_map, across)
     maps = [m[0] for m in made]
-    from_pair = [moved(m, pair) for m in maps[:2]]
-    next_map = composed(core, maps[2], from_pair[0])
-    from_chip = moved(next_map, across)
-    chip_map, plane_map, offset = plane_composed(core, chip, maps[3], from_pair[1], from_chip)
-    plane_map, offset, kept = lax.optimization_barrier((plane_map, offset, [m[1:] for m in made]))
-
-    def read(i):
+    chip_map, plane_map, offset, token = plane_composed(flags, token, maps[3], from_pair[1], from_chip)
+
+    def read(token, i):
         return group_reads(
-            groups[i], query_rows, key_rows, tails, query_kernel, key_kernel, scalars, kept[i]
+            flags, token, i, query_rows, key_rows, tails, query_kernel, key_kernel, scalars, made[i][1:]
         )
 
     reads = []
     entry = moved(offset, onward)
     for i in range(count // PLANE - 1):
         if i > 0:
-            entry = moved(applied(plane_map, entry), onward)
+            exit_state, token = applied(flags, token, plane_map, entry)
+            entry = moved(exit_state, onward)
         if len(reads) < PLANE - 1:
-            reads.append(read(i))
-            entry, reads[-1] = lax.optimization_barrier((entry, reads[-1]))
-    send, own_entry, own_send = forked(core, chip, chip_map, from_chip, maps[3], from_pair[1], entry)
+            reads.append(read(token, i))
+            token = reads[-1][-1]
+    send, own_entry, own_send, token = forked(flags, token, chip_map, from_chip, maps[3], from_pair[1], entry)
     theirs = moved(send, across)
     far_own = moved(own_send, pair)
-    reads += [read(i) for i in range(len(reads), PLANE)]
+    for i in range(len(reads), PLANE):
+        reads.append(read(token, i))
+        token = reads[-1][-1]
     width = query_rows.shape[1]
-    out = finished(groups[3], reads[3:], [own_entry], None, width)
-    out = finished(groups[1], reads[1:2], [far_own], out, width)
-    theirs, out = lax.optimization_barrier((theirs, out))
-    next_entry, next_send = branched(core, maps[2], from_pair[0], theirs)
+    out, token = finished(flags, token, 3, reads[3], own_entry, None, width)
+    out, token = finished(flags, token, 1, reads[1], far_own, out, width)
+    next_entry, next_send, token = branched(flags, token, maps[2], from_pair[0], theirs)
     far_next = moved(next_send, pair)
-    out = finished(groups[2], reads[2:3], [next_entry], out, width)
-    far_next, out = lax.optimization_barrier((far_next, out))
-    return finished(groups[0], reads[:1], [far_next], out, width)
+    out, token = finished(flags, token, 2, reads[2], next_entry, out, width)
+    return finished(flags, token, 0, reads[0], far_next, out, width)[0]
 
 
 def solution(mesh):

time: 114 us -> 94.2 us (0.83); the launches traced: 112 us -> 94 us
  Pallas kernels: 91.1 us -> 64.5 us
  waiting for transfers between devices: 2.01 us -> 6.42 us
  starting transfers between devices: 19 us -> 21.1 us
  local copies, waits for them, and re-layouts: 0 us -> 1.62 us
    pallas_call x14, Pallas kernels: 77.2 us -> 55.2 us  [the longest x4 34.6 us: group_maps(): pl.pallas_call(functools.partial(maps_kernel, which), grid_spec=pltpu.Pre...]
    ppermute x10, waiting for transfers between devices: 2.01 us -> 6.42 us  [moved(): lax.ppermute(x, 'seq', pairs)]
    pallas_call x4, Pallas kernels: 9.2 us -> 6.47 us  [finished(): pl.pallas_call(finish_kernel, grid_spec=pltpu.PrefetchScalarGridSpec(num_...]
    ppermute x10, starting transfers between devices: 19 us -> 21.1 us  [moved(): lax.ppermute(x, 'seq', pairs)]
    unnamed x0 -> x18, local copies, waits for them, and re-layouts: none -> 1.62 us
    pallas_call x1, Pallas kernels: 3.15 us -> 1.77 us  [prep(): pl.pallas_call(prep_kernel, out_shape=(jax.ShapeDtypeStruct((PLANE, steps...]
  transfers between devices with their start and end apart: 10 -> 10, of which waited for: 1 -> 4; matrix products, arithmetic and copies ran while one was open for 0% -> 0% of each run, Pallas kernels for 59% -> 52%
where the time goes in v3:
time: 94.2 us; the launch traced here: 94 us
  Pallas kernels  64.5 us (68%)
  starting transfers between devices  21.1 us (22%)
  waiting for transfers between devices  6.42 us (7%)
  local copies, waits for them, and re-layouts  1.62 us (2%)
    pallas_call x4, Pallas kernels, group_maps(): pl.pallas_call(functools.partial(maps_kernel, which), grid_spec=pltpu.Pre...  34.6 us
    ppermute x10, starting transfers between devices, moved(): lax.ppermute(x, 'seq', pairs)  21.1 us
    pallas_call x4, Pallas kernels, group_reads(): pl.pallas_call(functools.partial(reads_kernel, which), grid_spec=pltpu.Pr...  15.1 us
    pallas_call x4, Pallas kernels, finished(): pl.pallas_call(finish_kernel, grid_spec=pltpu.PrefetchScalarGridSpec(num_...  6.47 us
    ppermute x10, waiting for transfers between devices, moved(): lax.ppermute(x, 'seq', pairs)  6.42 us
    pallas_call x6, Pallas kernels, small(): pl.pallas_call(body, grid_spec=pltpu.PrefetchScalarGridSpec(num_scalar_pr...  5.49 us
  transfers between devices with their start and end apart: 10, of which 4 were waited for; matrix products, arithmetic and copies ran while one was open for 0% of the time, Pallas kernels for 52%

profile of v3, /device:TPU:9, one launch (start us, length us, event | category | flops | bytes accessed | tf_op | source)
XLA Modules:
  0.0 94.0 jit_solution(6567246044896138839)
XLA Ops:
  0.0 1.1 %last_rows.1 = bf16[9,2048]{1,0:T(8,128)(2,1)S(1)} custom-call(bf16[256,2048]{1,0:T(8,128)(2,1)} %query_ref.9, bf16[512,2048]{1,0:T(8,128)(2,1)} %key_ref.17, bf16[512,2048]{1,0:T(8,128)(2,1)} %value_ref.9), custom_call_target="tpu_custom_call" | custom-call | tf_op jit(solution)/shard_map/last_rows/pallas_call | solution.py:172
  1.1 3.7 %collective-permute-start = (bf16[9,2048]{1,0:T(8,128)(2,1)S(1)}, bf16[9,2048]{1,0:T(8,128)(2,1)S(1)}, u32[]{:S(2)}, u32[]{:S(2)}) collective-permute-start(bf16[9,2048]{1,0:T(8,128)(2,1)S(1)} %last_rows.1), channel_id=1, source_target_pairs={{0,1},{1,2},{2,3},{3,4},{4,5},{5,6},{6,7},{7,8},{8,9},{9,10},{10,1... | collective-permute-start | bytes 110600 | tf_op jit(solution)/shard_map/ppermute | solution.py:660
  4.8 0.0 copy-done.8
  4.8 0.0 copy-done.7
  4.9 0.0 copy-done.6
  4.9 1.8 %prep.1 = (f32[4,512,4]{2,1,0:T(8,128)S(1)}, f32[4,512,4]{2,1,0:T(8,128)S(1)}, f32[16,4,128]{2,1,0:T(4,128)S(1)}, f32[4,256,4]{2,1,0:T(8,128)S(1)}, s32[8]{0:T(128)S(1)}, /*index=5*/s32[8,128]{1,0:T(8,128)S(1)}) custom-call(s32[1]{0:T(128)} %bitcast.at_ref, f32[16,512]{1,0:T(8,128)S(1)} %bitcast.4, f32[16,256]{1,0:T(8,128)S(1)} %bitcast.5, s32[4,8]{1,0:T(4,128)S(1)} %bitcast.6), custom_call_target="tpu_custom_call" | custom-call | tf_op jit(solution)/shard_map/prep/pallas_call | solution.py:187
  6.6 0.0 collective-permute-done.tail_ref
  6.7 0.0 copy-start.1
  6.7 1.6 %copy-done.1 = bf16[512,2048]{1,0:T(8,128)(2,1)S(1)} copy-done((bf16[512,2048]{1,0:T(8,128)(2,1)S(1)}, bf16[512,2048]{1,0:T(8,128)(2,1)}, u32[]{:S(2)}) %copy-start.1) | copy-done | bytes 2097176
  8.3 8.6 %maps.4 = (f32[4,128,256]{2,1,0:T(8,128)S(1)}, bf16[4,512,256]{2,1,0:T(8,128)(2,1)S(1)}, bf16[4,512,256]{2,1,0:T(8,128)(2,1)S(1)}, bf16[4,384,256]{2,1,0:T(8,128...) custom-call(s32[8]{0:T(128)S(1)} %get-tuple-element.75.flags_ref, bf16[512,2048]{1,0:T(8,128)(2,1)S(1)} %copy-done, ...), custom_call_target="tpu_custom_call" | custom-call | tf_op jit(solution)/shard_map/maps/pallas_call | solution.py:360
  16.9 1.6 %collective-permute-start.1 = (f32[4,128,256]{2,1,0:T(8,128)S(1)}, f32[4,128,256]{2,1,0:T(8,128)S(1)}, u32[]{:S(2)}, u32[]{:S(2)}) collective-permute-start(f32[4,128,256]{2,1,0:T(8,128)S(1)} %get-tuple-element.85), channel_id=1, source_target_pairs={{0,1},{1,0},{2,3},{3,2},{4,5},{5,4},{6,7},{7,6},{8,9},{9,8},{10,11... | collective-permute-start | bytes 1572872 | tf_op jit(solution)/shard_map/ppermute | solution.py:660
  18.5 8.6 %maps.5 = (f32[4,128,256]{2,1,0:T(8,128)S(1)}, bf16[4,512,256]{2,1,0:T(8,128)(2,1)S(1)}, bf16[4,512,256]{2,1,0:T(8,128)(2,1)S(1)}, bf16[4,384,256]{2,1,0:T(8,128...) custom-call(s32[8]{0:T(128)S(1)} %get-tuple-element.75.flags_ref, bf16[512,2048]{1,0:T(8,128)(2,1)S(1)} %copy-done, ...), custom_call_target="tpu_custom_call" | custom-call | tf_op jit(solution)/shard_map/maps/pallas_call | solution.py:360
  27.2 0.1 collective-permute-start.2
  27.2 8.8 %maps.6 = (f32[4,128,256]{2,1,0:T(8,128)S(1)}, bf16[4,512,256]{2,1,0:T(8,128)(2,1)S(1)}, bf16[4,512,256]{2,1,0:T(8,128)(2,1)S(1)}, bf16[4,384,256]{2,1,0:T(8,128...) custom-call(s32[8]{0:T(128)S(1)} %get-tuple-element.75.flags_ref, bf16[512,2048]{1,0:T(8,128)(2,1)S(1)} %copy-done, ...), custom_call_target="tpu_custom_call" | custom-call | tf_op jit(solution)/shard_map/maps/pallas_call | solution.py:360
  36.0 0.0 collective-permute-done.1.refs_1_
  36.0 0.9 compose.1
  37.0 0.4 collective-permute-start.3
  37.4 8.6 %maps.7 = (f32[4,128,256]{2,1,0:T(8,128)S(1)}, bf16[4,512,256]{2,1,0:T(8,128)(2,1)S(1)}, bf16[4,512,256]{2,1,0:T(8,128)(2,1)S(1)}, bf16[4,384,256]{2,1,0:T(8,128...) custom-call(s32[8]{0:T(128)S(1)} %get-tuple-element.75.flags_ref, bf16[512,2048]{1,0:T(8,128)(2,1)S(1)} %copy-done, ...), custom_call_target="tpu_custom_call" | custom-call | tf_op jit(solution)/shard_map/maps/pallas_call | solution.py:360
  46.0 0.0 copy-start.2
  46.0 0.0 collective-permute-done.2.refs_1_.refs_3_
  46.0 4.0 %collective-permute-done.3.refs_2_.refs_1_ = f32[4,128,256]{2,1,0:T(8,128)S(1)} collective-permute-done((f32[4,128,256]{2,1,0:T(8,128)S(1)}, f32[4,128,256]{2,1,0:T(8,128)S(1)}, u32[]{:S(2)}, u32[]{:S(2)}) %collective-permute-start.3) | collective-permute-done | bytes 524320 | tf_op jit(solution)/shard_map/ppermute | solution.py:660
  50.0 1.1 %plane.1 = (f32[4,128,256]{2,1,0:T(8,128)S(1)}, f32[4,128,256]{2,1,0:T(8,128)S(1)}, f32[4,128,128]{2,1,0:T(8,128)S(1)}, s32[8,128]{1,0:T(8,128)S(1)}) custom-call(s32[8]{0:T(128)S(1)} %get-tuple-element.75.flags_ref, s32[8,128]{1,0:T(8,128)S(1)} %get-tuple-element.103.token_ref, f32[4,128,256]{2,1,0:T(8,128)S(1)} %get-tuple-element.104.refs_0_.refs_2_, ...), custom_call_target="tpu_custom_call" | custom-call | tf_op jit(solution)/shard_map/plane/pallas_call | solution.py:534
  51.1 3.2 %collective-permute-start.4 = (f32[4,128,128]{2,1,0:T(8,128)S(1)}, f32[4,128,128]{2,1,0:T(8,128)S(1)}, u32[]{:S(2)}, u32[]{:S(2)}) collective-permute-start(f32[4,128,128]{2,1,0:T(8,128)S(1)} %get-tuple-element.110), channel_id=1, source_target_pairs={{0,4},{1,5},{2,6},{3,7},{4,8},{5,9},{6,10},{7,11},{8,12},{9,13},{1... | collective-permute-start | bytes 786440 | tf_op jit(solution)/shard_map/ppermute | solution.py:660
  54.4 0.0 copy-done.5
  54.4 0.0 copy-done.2
  54.4 3.7 %reads.4 = (bf16[4,256,128]{2,1,0:T(8,128)(2,1)S(1)}, bf16[4,256,128]{2,1,0:T(8,128)(2,1)S(1)}, f32[4,256,128]{2,1,0:T(8,128)S(1)}, s32[8,128]{1,0:T(8,128)S(1)}) custom-call(s32[8]{0:T(128)S(1)} %get-tuple-element.75.flags_ref, bf16[256,2048]{1,0:T(8,128)(2,1)S(1)} %copy-done.2, bf16[9,2048]{1,0:T(8,128)(2,1)S(1)} %collective-permute-done.tail_ref, ...), custom_call_target="tpu_custom_call" | custom-call | tf_op jit(solution)/shard_map/reads/pallas_call | solution.py:493
  58.1 1.4 %collective-permute-done.4.refs_1_ = f32[4,128,128]{2,1,0:T(8,128)S(1)} collective-permute-done((f32[4,128,128]{2,1,0:T(8,128)S(1)}, f32[4,128,128]{2,1,0:T(8,128)S(1)}, u32[]{:S(2)}, u32[]{:S(2)}) %collective-permute-start.4) | collective-permute-done | bytes 262176 | tf_op jit(solution)/shard_map/ppermute | solution.py:660
  59.5 0.8 apply.2
  60.3 3.2 %collective-permute-start.5 = (f32[4,128,128]{2,1,0:T(8,128)S(1)}, f32[4,128,128]{2,1,0:T(8,128)S(1)}, u32[]{:S(2)}, u32[]{:S(2)}) collective-permute-start(f32[4,128,128]{2,1,0:T(8,128)S(1)} %get-tuple-element.113), channel_id=1, source_target_pairs={{0,4},{1,5},{2,6},{3,7},{4,8},{5,9},{6,10},{7,11},{8,12},{9,13},{1... | collective-permute-start | bytes 786440 | tf_op jit(solution)/shard_map/ppermute | solution.py:660
  63.5 3.7 %reads.5 = (bf16[4,256,128]{2,1,0:T(8,128)(2,1)S(1)}, bf16[4,256,128]{2,1,0:T(8,128)(2,1)S(1)}, f32[4,256,128]{2,1,0:T(8,128)S(1)}, s32[8,128]{1,0:T(8,128)S(1)}) custom-call(s32[8]{0:T(128)S(1)} %get-tuple-element.75.flags_ref, bf16[256,2048]{1,0:T(8,128)(2,1)S(1)} %copy-done.2, bf16[9,2048]{1,0:T(8,128)(2,1)S(1)} %collective-permute-done.tail_ref, ...), custom_call_target="tpu_custom_call" | custom-call | tf_op jit(solution)/shard_map/reads/pallas_call | solution.py:493
  67.2 0.5 collective-permute-done.5.refs_1_
  67.7 0.8 apply.3
  68.5 3.2 %collective-permute-start.6 = (f32[4,128,128]{2,1,0:T(8,128)S(1)}, f32[4,128,128]{2,1,0:T(8,128)S(1)}, u32[]{:S(2)}, u32[]{:S(2)}) collective-permute-start(f32[4,128,128]{2,1,0:T(8,128)S(1)} %get-tuple-element.117), channel_id=1, source_target_pairs={{0,4},{1,5},{2,6},{3,7},{4,8},{5,9},{6,10},{7,11},{8,12},{9,13},{1... | collective-permute-start | bytes 786440 | tf_op jit(solution)/shard_map/ppermute | solution.py:660
  71.7 3.9 %reads.6 = (bf16[4,256,128]{2,1,0:T(8,128)(2,1)S(1)}, bf16[4,256,128]{2,1,0:T(8,128)(2,1)S(1)}, f32[4,256,128]{2,1,0:T(8,128)S(1)}, s32[8,128]{1,0:T(8,128)S(1)}) custom-call(s32[8]{0:T(128)S(1)} %get-tuple-element.75.flags_ref, bf16[256,2048]{1,0:T(8,128)(2,1)S(1)} %copy-done.2, bf16[9,2048]{1,0:T(8,128)(2,1)S(1)} %collective-permute-done.tail_ref, ...), custom_call_target="tpu_custom_call" | custom-call | tf_op jit(solution)/shard_map/reads/pallas_call | solution.py:493
  75.7 0.0 collective-permute-done.6.refs_4_
  75.7 1.0 %fork.1 = (f32[4,128,128]{2,1,0:T(8,128)S(1)}, f32[4,128,128]{2,1,0:T(8,128)S(1)}, f32[4,128,128]{2,1,0:T(8,128)S(1)}, s32[8,128]{1,0:T(8,128)S(1)}) custom-call(s32[8]{0:T(128)S(1)} %get-tuple-element.75.flags_ref, s32[8,128]{1,0:T(8,128)S(1)} %get-tuple-element.115.token_ref, f32[4,128,256]{2,1,0:T(8,128)S(1)} %get-tuple-element.116.refs_0_, ...), custom_call_target="tpu_custom_call" | custom-call | tf_op jit(solution)/shard_map/fork/pallas_call | solution.py:534
  76.7 4.4 %collective-permute-start.7 = (f32[4,128,128]{2,1,0:T(8,128)S(1)}, f32[4,128,128]{2,1,0:T(8,128)S(1)}, u32[]{:S(2)}, u32[]{:S(2)}) collective-permute-start(f32[4,128,128]{2,1,0:T(8,128)S(1)} %get-tuple-element.128), channel_id=1, source_target_pairs={{0,1},{1,0},{2,3},{3,2},{4,5},{5,4},{6,7},{7,6},{8,9},{9,8},{10,11... | collective-permute-start | bytes 786440 | tf_op jit(solution)/shard_map/ppermute | solution.py:660
  81.1 0.4 collective-permute-start.8
  81.5 3.7 %reads.7 = (bf16[4,256,128]{2,1,0:T(8,128)(2,1)S(1)}, bf16[4,256,128]{2,1,0:T(8,128)(2,1)S(1)}, f32[4,256,128]{2,1,0:T(8,128)S(1)}, s32[8,128]{1,0:T(8,128)S(1)}) custom-call(s32[8]{0:T(128)S(1)} %get-tuple-element.75.flags_ref, bf16[256,2048]{1,0:T(8,128)(2,1)S(1)} %copy-done.2, bf16[9,2048]{1,0:T(8,128)(2,1)S(1)} %collective-permute-done.tail_ref, ...), custom_call_target="tpu_custom_call" | custom-call | tf_op jit(solution)/shard_map/reads/pallas_call | solution.py:493
  85.2 1.6 %finish.4 = (bf16[256,2048]{1,0:T(8,128)(2,1)}, s32[8,128]{1,0:T(8,128)S(1)}) custom-call(s32[8]{0:T(128)S(1)} %get-tuple-element.75.flags_ref, s32[8,128]{1,0:T(8,128)S(1)} %get-tuple-element.119.token_ref, bf16[4,256,128]{2,1,0:T(8,128)(2,1)S(1)} %get-tuple-element.120.qh_ref, bf16[4,256,128]{2,1,0:T(8,128)(2,1)S(1)} %get-tuple-element.121.ql_ref, ...), custom_call_target="tpu_custom_call" | custom-call | tf_op jit(solution)/shard_map/finish/pallas_call | solution.py:644
  86.8 0.0 collective-permute-done.7.entry_ref
  86.8 1.6 %finish.5 = (bf16[256,2048]{1,0:T(8,128)(2,1)}, s32[8,128]{1,0:T(8,128)S(1)}) custom-call(s32[8]{0:T(128)S(1)} %get-tuple-element.75.flags_ref, s32[8,128]{1,0:T(8,128)S(1)} %get-tuple-element.124.token_ref, bf16[4,256,128]{2,1,0:T(8,128)(2,1)S(1)} %get-tuple-element.125.qh_ref, ...), custom_call_target="tpu_custom_call", output_to_operand_aliasing={{0}: (6, {})} | custom-call | tf_op jit(solution)/shard_map/finish/pallas_call | solution.py:644
  88.4 0.6 collective-permute-done.8.refs_2_
  89.0 0.8 branch.1
  89.8 0.9 collective-permute-start.9
  90.7 1.6 %finish.6 = (bf16[256,2048]{1,0:T(8,128)(2,1)}, s32[8,128]{1,0:T(8,128)S(1)}) custom-call(s32[8]{0:T(128)S(1)} %get-tuple-element.75.flags_ref, s32[8,128]{1,0:T(8,128)S(1)} %get-tuple-element.132.token_ref, bf16[4,256,128]{2,1,0:T(8,128)(2,1)S(1)} %get-tuple-element.133.qh_ref, ...), custom_call_target="tpu_custom_call", output_to_operand_aliasing={{0}: (6, {})} | custom-call | tf_op jit(solution)/shard_map/finish/pallas_call | solution.py:644
  92.3 0.0 collective-permute-done.9.entry_ref
  92.3 1.6 %finish.7 = (bf16[256,2048]{1,0:T(8,128)(2,1)}, s32[8,128]{1,0:T(8,128)}) custom-call(s32[8]{0:T(128)S(1)} %get-tuple-element.75.flags_ref, s32[8,128]{1,0:T(8,128)S(1)} %get-tuple-element.138.token_ref, bf16[4,256,128]{2,1,0:T(8,128)(2,1)S(1)} %get-tuple-element.139.qh_ref, ...), custom_call_target="tpu_custom_call", output_to_operand_aliasing={{0}: (6, {})} | custom-call | tf_op jit(solution)/shard_map/finish/pallas_call | solution.py:644
  (10 shorter events, 0.0 us)
Async XLA Ops:
  0.0 6.7 %copy-start = (bf16[512,2048]{1,0:T(8,128)(2,1)S(1)}, bf16[512,2048]{1,0:T(8,128)(2,1)}, u32[]{:S(2)}) copy-start(bf16[512,2048]{1,0:T(8,128)(2,1)} %key_ref.17) | copy-start | bytes 6291460
  0.0 4.8 %copy-start.8 = (s32[8,4]{0,1:T(4,128)S(1)}, s32[8,4]{0,1:T(4,128)}, u32[]{:S(2)}) copy-start(s32[8,4]{0,1:T(4,128)} %param.14) | copy-start | bytes 388
  0.0 4.8 %copy-start.7 = (f32[256,16]{0,1:T(8,128)S(1)}, f32[256,16]{0,1:T(8,128)}, u32[]{:S(2)}) copy-start(f32[256,16]{0,1:T(8,128)} %param.13) | copy-start | bytes 49156
  0.0 4.8 %copy-start.6 = (f32[512,16]{0,1:T(8,128)S(1)}, f32[512,16]{0,1:T(8,128)}, u32[]{:S(2)}) copy-start(f32[512,16]{0,1:T(8,128)} %param.12) | copy-start | bytes 98308
  0.0 6.6 %copy-start.3 = (f32[4,2048]{1,0:T(4,128)S(1)}, f32[4,2048]{1,0:T(4,128)}, u32[]{:S(2)}) copy-start(f32[4,2048]{1,0:T(4,128)} %key_kernel_ref.15) | copy-start | bytes 98308
  0.0 6.6 %copy-start.4 = (f32[4,2048]{1,0:T(4,128)S(1)}, f32[4,2048]{1,0:T(4,128)}, u32[]{:S(2)}) copy-start(f32[4,2048]{1,0:T(4,128)} %value_kernel_ref.7) | copy-start | bytes 98308
  1.1 5.5 %collective-permute-start = (bf16[9,2048]{1,0:T(8,128)(2,1)S(1)}, bf16[9,2048]{1,0:T(8,128)(2,1)S(1)}, u32[]{:S(2)}, u32[]{:S(2)}) collective-permute-start(bf16[9,2048]{1,0:T(8,128)(2,1)S(1)} %last_rows.1), channel_id=1, source_target_pairs={{0,1},{1,2},{2,3},{3,4},{4,5},{5,6},{6,7},{7,8},{8,9},{9,10},{10,1... | collective-permute-start | bytes 110600 | tf_op jit(solution)/shard_map/ppermute | solution.py:660
  6.7 1.6 %copy-start.1 = (bf16[512,2048]{1,0:T(8,128)(2,1)S(1)}, bf16[512,2048]{1,0:T(8,128)(2,1)}, u32[]{:S(2)}) copy-start(bf16[512,2048]{1,0:T(8,128)(2,1)} %value_ref.9) | copy-start | bytes 6291460
  16.9 19.1 %collective-permute-start.1 = (f32[4,128,256]{2,1,0:T(8,128)S(1)}, f32[4,128,256]{2,1,0:T(8,128)S(1)}, u32[]{:S(2)}, u32[]{:S(2)}) collective-permute-start(f32[4,128,256]{2,1,0:T(8,128)S(1)} %get-tuple-element.85), channel_id=1, source_target_pairs={{0,1},{1,0},{2,3},{3,2},{4,5},{5,4},{6,7},{7,6},{8,9},{9,8},{10,11... | collective-permute-start | bytes 1572872 | tf_op jit(solution)/shard_map/ppermute | solution.py:660
  27.2 18.8 %collective-permute-start.2 = (f32[4,128,256]{2,1,0:T(8,128)S(1)}, f32[4,128,256]{2,1,0:T(8,128)S(1)}, u32[]{:S(2)}, u32[]{:S(2)}) collective-permute-start(f32[4,128,256]{2,1,0:T(8,128)S(1)} %get-tuple-element.105), channel_id=1, source_target_pairs={{0,1},{1,0},{2,3},{3,2},{4,5},{5,4},{6,7},{7,6},{8,9},{9,8},{10,11... | collective-permute-start | bytes 1572872 | tf_op jit(solution)/shard_map/ppermute | solution.py:660
  37.0 13.0 %collective-permute-start.3 = (f32[4,128,256]{2,1,0:T(8,128)S(1)}, f32[4,128,256]{2,1,0:T(8,128)S(1)}, u32[]{:S(2)}, u32[]{:S(2)}) collective-permute-start(f32[4,128,256]{2,1,0:T(8,128)S(1)} %get-tuple-element.106), channel_id=1, source_target_pairs={{0,2},{1,3},{2,0},{3,1},{4,6},{5,7},{6,4},{7,5},{8,10},{9,11},{10,... | collective-permute-start | bytes 1572872 | tf_op jit(solution)/shard_map/ppermute | solution.py:660
  37.4 17.0 %copy-start.5 = (f32[4,2048]{1,0:T(4,128)S(1)}, f32[4,2048]{1,0:T(4,128)}, u32[]{:S(2)}) copy-start(f32[4,2048]{1,0:T(4,128)} %query_kernel_ref.7) | copy-start | bytes 98308
  46.0 8.4 %copy-start.2 = (bf16[256,2048]{1,0:T(8,128)(2,1)S(1)}, bf16[256,2048]{1,0:T(8,128)(2,1)}, u32[]{:S(2)}) copy-start(bf16[256,2048]{1,0:T(8,128)(2,1)} %query_ref.9) | copy-start | bytes 3145732
  51.1 8.3 %collective-permute-start.4 = (f32[4,128,128]{2,1,0:T(8,128)S(1)}, f32[4,128,128]{2,1,0:T(8,128)S(1)}, u32[]{:S(2)}, u32[]{:S(2)}) collective-permute-start(f32[4,128,128]{2,1,0:T(8,128)S(1)} %get-tuple-element.110), channel_id=1, source_target_pairs={{0,4},{1,5},{2,6},{3,7},{4,8},{5,9},{6,10},{7,11},{8,12},{9,13},{1... | collective-permute-start | bytes 786440 | tf_op jit(solution)/shard_map/ppermute | solution.py:660
  60.3 7.4 %collective-permute-start.5 = (f32[4,128,128]{2,1,0:T(8,128)S(1)}, f32[4,128,128]{2,1,0:T(8,128)S(1)}, u32[]{:S(2)}, u32[]{:S(2)}) collective-permute-start(f32[4,128,128]{2,1,0:T(8,128)S(1)} %get-tuple-element.113), channel_id=1, source_target_pairs={{0,4},{1,5},{2,6},{3,7},{4,8},{5,9},{6,10},{7,11},{8,12},{9,13},{1... | collective-permute-start | bytes 786440 | tf_op jit(solution)/shard_map/ppermute | solution.py:660
  68.5 7.2 %collective-permute-start.6 = (f32[4,128,128]{2,1,0:T(8,128)S(1)}, f32[4,128,128]{2,1,0:T(8,128)S(1)}, u32[]{:S(2)}, u32[]{:S(2)}) collective-permute-start(f32[4,128,128]{2,1,0:T(8,128)S(1)} %get-tuple-element.117), channel_id=1, source_target_pairs={{0,4},{1,5},{2,6},{3,7},{4,8},{5,9},{6,10},{7,11},{8,12},{9,13},{1... | collective-permute-start | bytes 786440 | tf_op jit(solution)/shard_map/ppermute | solution.py:660
  76.7 10.1 %collective-permute-start.7 = (f32[4,128,128]{2,1,0:T(8,128)S(1)}, f32[4,128,128]{2,1,0:T(8,128)S(1)}, u32[]{:S(2)}, u32[]{:S(2)}) collective-permute-start(f32[4,128,128]{2,1,0:T(8,128)S(1)} %get-tuple-element.128), channel_id=1, source_target_pairs={{0,1},{1,0},{2,3},{3,2},{4,5},{5,4},{6,7},{7,6},{8,9},{9,8},{10,11... | collective-permute-start | bytes 786440 | tf_op jit(solution)/shard_map/ppermute | solution.py:660
  81.1 7.9 %collective-permute-start.8 = (f32[4,128,128]{2,1,0:T(8,128)S(1)}, f32[4,128,128]{2,1,0:T(8,128)S(1)}, u32[]{:S(2)}, u32[]{:S(2)}) collective-permute-start(f32[4,128,128]{2,1,0:T(8,128)S(1)} %get-tuple-element.131), channel_id=1, source_target_pairs={{0,2},{1,3},{2,0},{3,1},{4,6},{5,7},{6,4},{7,5},{8,10},{9,11},{10,... | collective-permute-start | bytes 786440 | tf_op jit(solution)/shard_map/ppermute | solution.py:660
  89.8 2.5 %collective-permute-start.9 = (f32[4,128,128]{2,1,0:T(8,128)S(1)}, f32[4,128,128]{2,1,0:T(8,128)S(1)}, u32[]{:S(2)}, u32[]{:S(2)}) collective-permute-start(f32[4,128,128]{2,1,0:T(8,128)S(1)} %get-tuple-element.142), channel_id=1, source_target_pairs={{0,1},{1,0},{2,3},{3,2},{4,5},{5,4},{6,7},{7,6},{8,9},{9,8},{10,11... | collective-permute-start | bytes 786440 | tf_op jit(solution)/shard_map/ppermute | solution.py:660

commit v4 on v3

--- a/solution.py
+++ b/solution.py
@@ -14,6 +14,7 @@
 CHUNK = 128
 HALF = 64
 PLANE = 4
+PARTS = 2
 HB = 2
 VMEM = 24 << 20
 SMALL = pltpu.CompilerParams(vmem_limit_bytes=8 << 20)
@@ -562,32 +563,38 @@
     return small(compose_kernel, flags, token, [mine, other], [mine.shape], "compose")
 
 
-def plane_kernel(flags_ref, mine_ref, pair_ref, other_ref, chip_out, plane_out, offset_out):
+def plane_kernel(flags_ref, mine_ref, pair_ref, other_ref, chip_out, *outs):
+    parts = len(outs) // 3
+    for zero_out in outs[2 * parts :]:
+        zero_out[...] = jnp.zeros_like(zero_out)
     heads = range(mine_ref.shape[0])
     chips = [after(flags_ref[CORE] == 0, mine_ref[h], pair_ref[h]) for h in heads]
     planes = [after(flags_ref[CHIP] == 0, chips[h], other_ref[h]) for h in heads]
     for h in heads:
         chip_out[h] = chips[h]
-        plane_out[h] = planes[h]
-        offset_out[h] = planes[h][:, DK:]
+        part, at = h * parts // len(heads), h % (len(heads) // parts)
+        outs[part][at] = planes[h]
+        outs[parts + part][at] = planes[h][:, DK:]
 
 
 def plane_composed(flags, token, mine, pair, other):
-    heads = mine.shape[0]
-    return small(
-        plane_kernel, flags, token, [mine, pair, other], [mine.shape, mine.shape, (heads, DK, DK)], "plane"
-    )
-
-
-def apply_kernel(flags_ref, map_ref, state_ref, out_ref):
+    part = mine.shape[0] // PARTS
+    shapes = [(part, DK, 2 * DK)] * PARTS + [(part, DK, DK)] * (2 * PARTS)
+    chip_map, *outs, token = small(plane_kernel, flags, token, [mine, pair, other], [mine.shape] + shapes, "plane")
+    return chip_map, outs[:PARTS], outs[PARTS : 2 * PARTS], outs[2 * PARTS :], token
+
+
+def apply_kernel(flags_ref, map_ref, held_ref, come_ref, state_out, exit_out):
     heads = range(map_ref.shape[0])
-    got = [mm3(split(map_ref[h, :, :DK]), split(state_ref[h])) for h in heads]
+    state = [held_ref[h] + come_ref[h] for h in heads]
+    got = [mm3(split(map_ref[h, :, :DK]), split(state[h])) for h in heads]
     for h in heads:
-        out_ref[h] = got[h] + map_ref[h, :, DK:]
-
-
-def applied(flags, token, maps, state):
-    return small(apply_kernel, flags, token, [maps, state], [state.shape], "apply")
+        state_out[h] = state[h]
+        exit_out[h] = got[h] + map_ref[h, :, DK:]
+
+
+def applied(flags, token, maps, state, come):
+    return small(apply_kernel, flags, token, [maps, state, come], [state.shape] * 2, "apply")
 
 
 def branches(first, mine, other, entry):
@@ -610,18 +617,21 @@
     return small(branch_kernel, flags, token, [mine, other, entry], [entry.shape] * 2, "branch")
 
 
-def fork_kernel(flags_ref, chip_map_ref, from_chip_ref, map_ref, pair_ref, entry_ref, *outs):
-    refs = (chip_map_ref, from_chip_ref, map_ref, pair_ref, entry_ref)
-    chip_map, from_chip, mine, pair, entry = ([x[h] for h in range(x.shape[0])] for x in refs)
+def fork_kernel(flags_ref, chip_map_ref, from_chip_ref, map_ref, pair_ref, *refs):
+    maps = (chip_map_ref, from_chip_ref, map_ref, pair_ref)
+    chip_map, from_chip, mine, pair = ([x[h] for h in range(x.shape[0])] for x in maps)
+    states, outs = refs[: 2 * PARTS], refs[2 * PARTS :]
+    state, come = ([x[h] for x in part for h in range(x.shape[0])] for part in (states[:PARTS], states[PARTS:]))
+    entry = [x + y for x, y in zip(state, come)]
     own, across = branches(flags_ref[CHIP] == 0, chip_map, from_chip, entry)
     for out_ref, states in zip(outs, (across, *branches(flags_ref[CORE] == 0, mine, pair, own))):
         for h, state in enumerate(states):
             out_ref[h] = state
 
 
-def forked(flags, token, chip_map, from_chip, mine, pair, entry):
-    operands = [chip_map, from_chip, mine, pair, entry]
-    return small(fork_kernel, flags, token, operands, [entry.shape] * 3, "fork")
+def forked(flags, token, chip_map, from_chip, mine, pair, state, come):
+    operands = [chip_map, from_chip, mine, pair, *state, *come]
+    return small(fork_kernel, flags, token, operands, [(mine.shape[0], DK, DK)] * 3, "fork")
 
 
 def finish_kernel(flags_ref, token_ref, qh_ref, ql_ref, own_ref, entry_ref, *refs):
@@ -678,18 +688,17 @@
     *scalars, flags, token = prep(lax.axis_index("seq")[None], write_rate, log_gate, keep_mask)
     pair = [(s, s ^ 1) for s in range(count)]
     across = [(s, s ^ 2) for s in range(count)]
-    onward = [(s, s + PLANE) for s in range(count - PLANE)]
-    made, from_pair = [], []
-    for i in range(PLANE):
+    made, from_pair = {}, {}
+    for i in (0, 2, 1, 3):
         *one, token = group_maps(flags, token, i, key_rows, value_rows, tails, key_kernel, value_kernel, scalars)
-        made.append(one)
+        made[i] = one
         if i < 2:
-            from_pair.append(moved(one[0], pair))
+            from_pair[i] = moved(one[0], pair)
         if i == 2:
             next_map, token = composed(flags, token, one[0], from_pair[0])
             from_chip = moved(next_map, across)
-    maps = [m[0] for m in made]
-    chip_map, plane_map, offset, token = plane_composed(flags, token, maps[3], from_pair[1], from_chip)
+    maps = [made[i][0] for i in range(PLANE)]
+    chip_map, plane_maps, offset, state, token = plane_composed(flags, token, maps[3], from_pair[1], from_chip)
 
     def read(token, i):
         return group_reads(
@@ -697,15 +706,17 @@
         )
 
     reads = []
-    entry = moved(offset, onward)
     for i in range(count // PLANE - 1):
         if i > 0:
-            exit_state, token = applied(flags, token, plane_map, entry)
-            entry = moved(exit_state, onward)
+            offset = []
+            for part in range(PARTS):
+                state[part], part_offset, token = applied(flags, token, plane_maps[part], state[part], come[part])
+                offset.append(part_offset)
+        come = [moved(x, [(s, s + PLANE) for s in range(i * PLANE, (i + 1) * PLANE)]) for x in offset]
         if len(reads) < PLANE - 1:
             reads.append(read(token, i))
             token = reads[-1][-1]
-    send, own_entry, own_send, token = forked(flags, token, chip_map, from_chip, maps[3], from_pair[1], entry)
+    send, own_entry, own_send, token = forked(flags, token, chip_map, from_chip, maps[3], from_pair[1], state, come)
     theirs = moved(send, across)
     far_own = moved(own_send, pair)
     for i in range(len(reads), PLANE):

time: 94.2 us -> 84.9 us (0.901)
  waiting for transfers between devices: 6.42 us -> 0.87 us
  starting transfers between devices: 21.1 us -> 15.9 us
  Pallas kernels: 64.5 us -> 65.9 us
    ppermute x10 -> x13, waiting for transfers between devices: 6.42 us -> 0.87 us  [moved(): lax.ppermute(x, 'seq', pairs)]
    ppermute x10 -> x13, starting transfers between devices: 21.1 us -> 15.9 us  [moved(): lax.ppermute(x, 'seq', pairs)]
    pallas_call x6 -> x8, Pallas kernels: 5.49 us -> 6.86 us  [small(): pl.pallas_call(body, grid_spec=pltpu.PrefetchScalarGridSpec(num_scalar_pr...]
  transfers between devices with their start and end apart: 10 -> 13, of which waited for: 4 -> 2; matrix products, arithmetic and copies ran while one was open for 0% -> 0% of each run, Pallas kernels for 52% -> 60%
where the time goes in v4:
time: 84.9 us; the launch traced here: 84.7 us
  Pallas kernels  65.9 us (78%)
  starting transfers between devices  15.9 us (19%)
  local copies, waits for them, and re-layouts  1.62 us (2%)
  waiting for transfers between devices  0.87 us (1%)
    pallas_call x4, Pallas kernels, group_maps(): pl.pallas_call(functools.partial(maps_kernel, which), grid_spec=pltpu.Pre...  34.6 us
    ppermute x13, starting transfers between devices, moved(): lax.ppermute(x, 'seq', pairs)  15.9 us
    pallas_call x4, Pallas kernels, group_reads(): pl.pallas_call(functools.partial(reads_kernel, which), grid_spec=pltpu.Pr...  15.1 us
    pallas_call x8, Pallas kernels, small(): pl.pallas_call(body, grid_spec=pltpu.PrefetchScalarGridSpec(num_scalar_pr...  6.86 us
    pallas_call x4, Pallas kernels, finished(): pl.pallas_call(finish_kernel, grid_spec=pltpu.PrefetchScalarGridSpec(num_...  6.47 us
    pallas_call x1, Pallas kernels, prep(): pl.pallas_call(prep_kernel, out_shape=(jax.ShapeDtypeStruct((PLANE, steps...  1.77 us
  transfers between devices with their start and end apart: 13, of which 2 were waited for; matrix products, arithmetic and copies ran while one was open for 0% of the time, Pallas kernels for 60%

profile of v4, /device:TPU:9, one launch (start us, length us, event | category | flops | bytes accessed | tf_op | source)
XLA Modules:
  0.0 84.7 jit_solution(16451585587117266955)
XLA Ops:
  0.0 1.1 %last_rows.1 = bf16[9,2048]{1,0:T(8,128)(2,1)S(1)} custom-call(bf16[256,2048]{1,0:T(8,128)(2,1)} %query_ref.9, bf16[512,2048]{1,0:T(8,128)(2,1)} %key_ref.17, bf16[512,2048]{1,0:T(8,128)(2,1)} %value_ref.9), custom_call_target="tpu_custom_call" | custom-call | tf_op jit(solution)/shard_map/last_rows/pallas_call | solution.py:173
  1.1 3.7 %collective-permute-start = (bf16[9,2048]{1,0:T(8,128)(2,1)S(1)}, bf16[9,2048]{1,0:T(8,128)(2,1)S(1)}, u32[]{:S(2)}, u32[]{:S(2)}) collective-permute-start(bf16[9,2048]{1,0:T(8,128)(2,1)S(1)} %last_rows.1), channel_id=1, source_target_pairs={{0,1},{1,2},{2,3},{3,4},{4,5},{5,6},{6,7},{7,8},{8,9},{9,10},{10,1... | collective-permute-start | bytes 110600 | tf_op jit(solution)/shard_map/ppermute | solution.py:670
  4.9 1.8 %prep.1 = (f32[4,512,4]{2,1,0:T(8,128)S(1)}, f32[4,512,4]{2,1,0:T(8,128)S(1)}, f32[16,4,128]{2,1,0:T(4,128)S(1)}, f32[4,256,4]{2,1,0:T(8,128)S(1)}, s32[8]{0:T(128)S(1)}, /*index=5*/s32[8,128]{1,0:T(8,128)S(1)}) custom-call(s32[1]{0:T(128)} %bitcast.at_ref, f32[16,512]{1,0:T(8,128)S(1)} %bitcast.4, f32[16,256]{1,0:T(8,128)S(1)} %bitcast.5, s32[4,8]{1,0:T(4,128)S(1)} %bitcast.6), custom_call_target="tpu_custom_call" | custom-call | tf_op jit(solution)/shard_map/prep/pallas_call | solution.py:188
  6.6 0.0 collective-permute-done.tail_ref
  6.7 0.0 copy-start.1
  6.7 1.6 %copy-done.1 = bf16[512,2048]{1,0:T(8,128)(2,1)S(1)} copy-done((bf16[512,2048]{1,0:T(8,128)(2,1)S(1)}, bf16[512,2048]{1,0:T(8,128)(2,1)}, u32[]{:S(2)}) %copy-start.1) | copy-done | bytes 2097176
  8.3 8.6 %maps.4 = (f32[4,128,256]{2,1,0:T(8,128)S(1)}, bf16[4,512,256]{2,1,0:T(8,128)(2,1)S(1)}, bf16[4,512,256]{2,1,0:T(8,128)(2,1)S(1)}, bf16[4,384,256]{2,1,0:T(8,128...) custom-call(s32[8]{0:T(128)S(1)} %get-tuple-element.87.flags_ref, bf16[512,2048]{1,0:T(8,128)(2,1)S(1)} %copy-done, ...), custom_call_target="tpu_custom_call" | custom-call | tf_op jit(solution)/shard_map/maps/pallas_call | solution.py:361
  16.9 1.6 %collective-permute-start.1 = (f32[4,128,256]{2,1,0:T(8,128)S(1)}, f32[4,128,256]{2,1,0:T(8,128)S(1)}, u32[]{:S(2)}, u32[]{:S(2)}) collective-permute-start(f32[4,128,256]{2,1,0:T(8,128)S(1)} %get-tuple-element.96), channel_id=1, source_target_pairs={{0,1},{1,0},{2,3},{3,2},{4,5},{5,4},{6,7},{7,6},{8,9},{9,8},{10,11... | collective-permute-start | bytes 1572872 | tf_op jit(solution)/shard_map/ppermute | solution.py:670
  18.5 8.6 %maps.5 = (f32[4,128,256]{2,1,0:T(8,128)S(1)}, bf16[4,512,256]{2,1,0:T(8,128)(2,1)S(1)}, bf16[4,512,256]{2,1,0:T(8,128)(2,1)S(1)}, bf16[4,384,256]{2,1,0:T(8,128...) custom-call(s32[8]{0:T(128)S(1)} %get-tuple-element.87.flags_ref, bf16[512,2048]{1,0:T(8,128)(2,1)S(1)} %copy-done, ...), custom_call_target="tpu_custom_call" | custom-call | tf_op jit(solution)/shard_map/maps/pallas_call | solution.py:361
  27.2 0.0 collective-permute-done.1.refs_1_
  27.2 0.9 %compose.1 = (f32[4,128,256]{2,1,0:T(8,128)S(1)}, s32[8,128]{1,0:T(8,128)S(1)}) custom-call(s32[8]{0:T(128)S(1)} %get-tuple-element.87.flags_ref, s32[8,128]{1,0:T(8,128)S(1)} %get-tuple-element.94.token_ref, f32[4,128,256]{2,1,0:T(8,128)S(1)} %get-tuple-element.95.refs_0_, f32[4,128,256]{2,1,0:T(8,128)S(1)} %collective-permute-done.1.refs_1_), custom_call_target="tpu_custom_call" | custom-call | tf_op jit(solution)/shard_map/compose/pallas_call | solution.py:535
  28.1 0.4 collective-permute-start.3
  28.5 8.8 %maps.6 = (f32[4,128,256]{2,1,0:T(8,128)S(1)}, bf16[4,512,256]{2,1,0:T(8,128)(2,1)S(1)}, bf16[4,512,256]{2,1,0:T(8,128)(2,1)S(1)}, bf16[4,384,256]{2,1,0:T(8,128...) custom-call(s32[8]{0:T(128)S(1)} %get-tuple-element.87.flags_ref, bf16[512,2048]{1,0:T(8,128)(2,1)S(1)} %copy-done, ...), custom_call_target="tpu_custom_call" | custom-call | tf_op jit(solution)/shard_map/maps/pallas_call | solution.py:361
  37.3 0.4 collective-permute-start.2
  37.6 8.6 %maps.7 = (f32[4,128,256]{2,1,0:T(8,128)S(1)}, bf16[4,512,256]{2,1,0:T(8,128)(2,1)S(1)}, bf16[4,512,256]{2,1,0:T(8,128)(2,1)S(1)}, bf16[4,384,256]{2,1,0:T(8,128...) custom-call(s32[8]{0:T(128)S(1)} %get-tuple-element.87.flags_ref, bf16[512,2048]{1,0:T(8,128)(2,1)S(1)} %copy-done, ...), custom_call_target="tpu_custom_call" | custom-call | tf_op jit(solution)/shard_map/maps/pallas_call | solution.py:361
  46.3 0.0 copy-start.2
  46.3 0.0 collective-permute-done.3.refs_2_.refs_1_
  46.3 0.0 collective-permute-done.2.refs_1_.refs_3_
  46.3 1.1 %plane.1 = (f32[4,128,256]{2,1,0:T(8,128)S(1)}, f32[2,128,256]{2,1,0:T(8,128)S(1)}, f32[2,128,256]{2,1,0:T(8,128)S(1)}, f32[2,128,128]{2,1,0:T(8,128)S(1)}, f32[...) custom-call(s32[8]{0:T(128)S(1)} %get-tuple-element.87.flags_ref, ...), custom_call_target="tpu_custom_call" | custom-call | tf_op jit(solution)/shard_map/plane/pallas_call | solution.py:535
  47.4 1.3 %collective-permute-start.4 = (f32[2,128,128]{2,1,0:T(8,128)S(1)}, f32[2,128,128]{2,1,0:T(8,128)S(1)}, u32[]{:S(2)}, u32[]{:S(2)}) collective-permute-start(f32[2,128,128]{2,1,0:T(8,128)S(1)} %get-tuple-element.123), channel_id=1, source_target_pairs={{0,4},{1,5},{2,6},{3,7},{16,20},{17,21},{18,22},{19,23}} | collective-permute-start | bytes 393224 | tf_op jit(solution)/shard_map/ppermute | solution.py:670
  48.7 1.3 %collective-permute-start.5 = (f32[2,128,128]{2,1,0:T(8,128)S(1)}, f32[2,128,128]{2,1,0:T(8,128)S(1)}, u32[]{:S(2)}, u32[]{:S(2)}) collective-permute-start(f32[2,128,128]{2,1,0:T(8,128)S(1)} %get-tuple-element.127), channel_id=1, source_target_pairs={{0,4},{1,5},{2,6},{3,7},{16,20},{17,21},{18,22},{19,23}} | collective-permute-start | bytes 393224 | tf_op jit(solution)/shard_map/ppermute | solution.py:670
  50.1 3.7 %reads.4 = (bf16[4,256,128]{2,1,0:T(8,128)(2,1)S(1)}, bf16[4,256,128]{2,1,0:T(8,128)(2,1)S(1)}, f32[4,256,128]{2,1,0:T(8,128)S(1)}, s32[8,128]{1,0:T(8,128)S(1)}) custom-call(s32[8]{0:T(128)S(1)} %get-tuple-element.87.flags_ref, bf16[256,2048]{1,0:T(8,128)(2,1)S(1)} %copy-done.2, bf16[9,2048]{1,0:T(8,128)(2,1)S(1)} %collective-permute-done.tail_ref, ...), custom_call_target="tpu_custom_call" | custom-call | tf_op jit(solution)/shard_map/reads/pallas_call | solution.py:494
  53.8 0.4 collective-permute-done.4.refs_2_
  54.2 0.7 apply.4
  54.9 1.6 %collective-permute-start.6 = (f32[2,128,128]{2,1,0:T(8,128)S(1)}, f32[2,128,128]{2,1,0:T(8,128)S(1)}, u32[]{:S(2)}, u32[]{:S(2)}) collective-permute-start(f32[2,128,128]{2,1,0:T(8,128)S(1)} %get-tuple-element.131), channel_id=1, source_target_pairs={{4,8},{5,9},{6,10},{7,11},{20,24},{21,25},{22,26},{23,27}} | collective-permute-start | bytes 393224 | tf_op jit(solution)/shard_map/ppermute | solution.py:670
  56.5 0.5 collective-permute-done.5.refs_2_
  57.0 0.7 apply.5
  57.7 1.3 %collective-permute-start.7 = (f32[2,128,128]{2,1,0:T(8,128)S(1)}, f32[2,128,128]{2,1,0:T(8,128)S(1)}, u32[]{:S(2)}, u32[]{:S(2)}) collective-permute-start(f32[2,128,128]{2,1,0:T(8,128)S(1)} %get-tuple-element.134), channel_id=1, source_target_pairs={{4,8},{5,9},{6,10},{7,11},{20,24},{21,25},{22,26},{23,27}} | collective-permute-start | bytes 393224 | tf_op jit(solution)/shard_map/ppermute | solution.py:670
  59.1 3.7 %reads.5 = (bf16[4,256,128]{2,1,0:T(8,128)(2,1)S(1)}, bf16[4,256,128]{2,1,0:T(8,128)(2,1)S(1)}, f32[4,256,128]{2,1,0:T(8,128)S(1)}, s32[8,128]{1,0:T(8,128)S(1)}) custom-call(s32[8]{0:T(128)S(1)} %get-tuple-element.87.flags_ref, bf16[256,2048]{1,0:T(8,128)(2,1)S(1)} %copy-done.2, bf16[9,2048]{1,0:T(8,128)(2,1)S(1)} %collective-permute-done.tail_ref, ...), custom_call_target="tpu_custom_call" | custom-call | tf_op jit(solution)/shard_map/reads/pallas_call | solution.py:494
  62.8 0.0 collective-permute-done.6.refs_2_
  62.8 0.8 apply.6
  63.5 0.7 collective-permute-start.8
  64.2 0.0 collective-permute-done.7.refs_2_
  64.2 0.8 apply.7
  65.0 0.7 collective-permute-start.9
  65.7 3.9 %reads.6 = (bf16[4,256,128]{2,1,0:T(8,128)(2,1)S(1)}, bf16[4,256,128]{2,1,0:T(8,128)(2,1)S(1)}, f32[4,256,128]{2,1,0:T(8,128)S(1)}, s32[8,128]{1,0:T(8,128)S(1)}) custom-call(s32[8]{0:T(128)S(1)} %get-tuple-element.87.flags_ref, bf16[256,2048]{1,0:T(8,128)(2,1)S(1)} %copy-done.2, bf16[9,2048]{1,0:T(8,128)(2,1)S(1)} %collective-permute-done.tail_ref, ...), custom_call_target="tpu_custom_call" | custom-call | tf_op jit(solution)/shard_map/reads/pallas_call | solution.py:494
  69.6 0.0 collective-permute-done.8.refs_6_
  69.6 1.0 %fork.1 = (f32[4,128,128]{2,1,0:T(8,128)S(1)}, f32[4,128,128]{2,1,0:T(8,128)S(1)}, f32[4,128,128]{2,1,0:T(8,128)S(1)}, s32[8,128]{1,0:T(8,128)S(1)}) custom-call(s32[8]{0:T(128)S(1)} %get-tuple-element.87.flags_ref, s32[8,128]{1,0:T(8,128)S(1)} %get-tuple-element.136.token_ref, f32[4,128,256]{2,1,0:T(8,128)S(1)} %get-tuple-element.137.refs_0_, ...), custom_call_target="tpu_custom_call" | custom-call | tf_op jit(solution)/shard_map/fork/pallas_call | solution.py:535
  70.7 1.1 %collective-permute-start.10 = (f32[4,128,128]{2,1,0:T(8,128)S(1)}, f32[4,128,128]{2,1,0:T(8,128)S(1)}, u32[]{:S(2)}, u32[]{:S(2)}) collective-permute-start(f32[4,128,128]{2,1,0:T(8,128)S(1)} %get-tuple-element.152), channel_id=1, source_target_pairs={{0,1},{1,0},{2,3},{3,2},{4,5},{5,4},{6,7},{7,6},{8,9},{9,8},{10,11... | collective-permute-start | bytes 786440 | tf_op jit(solution)/shard_map/ppermute | solution.py:670
  71.8 1.1 %collective-permute-start.11 = (f32[4,128,128]{2,1,0:T(8,128)S(1)}, f32[4,128,128]{2,1,0:T(8,128)S(1)}, u32[]{:S(2)}, u32[]{:S(2)}) collective-permute-start(f32[4,128,128]{2,1,0:T(8,128)S(1)} %get-tuple-element.155), channel_id=1, source_target_pairs={{0,2},{1,3},{2,0},{3,1},{4,6},{5,7},{6,4},{7,5},{8,10},{9,11},{10,... | collective-permute-start | bytes 786440 | tf_op jit(solution)/shard_map/ppermute | solution.py:670
  72.9 3.7 %reads.7 = (bf16[4,256,128]{2,1,0:T(8,128)(2,1)S(1)}, bf16[4,256,128]{2,1,0:T(8,128)(2,1)S(1)}, f32[4,256,128]{2,1,0:T(8,128)S(1)}, s32[8,128]{1,0:T(8,128)S(1)}) custom-call(s32[8]{0:T(128)S(1)} %get-tuple-element.87.flags_ref, bf16[256,2048]{1,0:T(8,128)(2,1)S(1)} %copy-done.2, bf16[9,2048]{1,0:T(8,128)(2,1)S(1)} %collective-permute-done.tail_ref, ...), custom_call_target="tpu_custom_call" | custom-call | tf_op jit(solution)/shard_map/reads/pallas_call | solution.py:494
  76.6 1.6 %finish.4 = (bf16[256,2048]{1,0:T(8,128)(2,1)}, s32[8,128]{1,0:T(8,128)S(1)}) custom-call(s32[8]{0:T(128)S(1)} %get-tuple-element.87.flags_ref, s32[8,128]{1,0:T(8,128)S(1)} %get-tuple-element.143.token_ref, bf16[4,256,128]{2,1,0:T(8,128)(2,1)S(1)} %get-tuple-element.144.qh_ref, bf16[4,256,128]{2,1,0:T(8,128)(2,1)S(1)} %get-tuple-element.145.ql_ref, ...), custom_call_target="tpu_custom_call" | custom-call | tf_op jit(solution)/shard_map/finish/pallas_call | solution.py:654
  78.3 1.6 %finish.5 = (bf16[256,2048]{1,0:T(8,128)(2,1)}, s32[8,128]{1,0:T(8,128)S(1)}) custom-call(s32[8]{0:T(128)S(1)} %get-tuple-element.87.flags_ref, s32[8,128]{1,0:T(8,128)S(1)} %get-tuple-element.148.token_ref, bf16[4,256,128]{2,1,0:T(8,128)(2,1)S(1)} %get-tuple-element.149.qh_ref, ...), custom_call_target="tpu_custom_call", output_to_operand_aliasing={{0}: (6, {})} | custom-call | tf_op jit(solution)/shard_map/finish/pallas_call | solution.py:654
  79.9 0.8 branch.1
  80.7 0.7 collective-permute-start.12
  81.4 1.6 %finish.6 = (bf16[256,2048]{1,0:T(8,128)(2,1)}, s32[8,128]{1,0:T(8,128)S(1)}) custom-call(s32[8]{0:T(128)S(1)} %get-tuple-element.87.flags_ref, s32[8,128]{1,0:T(8,128)S(1)} %get-tuple-element.156.token_ref, bf16[4,256,128]{2,1,0:T(8,128)(2,1)S(1)} %get-tuple-element.157.qh_ref, ...), custom_call_target="tpu_custom_call", output_to_operand_aliasing={{0}: (6, {})} | custom-call | tf_op jit(solution)/shard_map/finish/pallas_call | solution.py:654
  83.0 0.0 collective-permute-done.12.entry_ref
  83.0 1.6 %finish.7 = (bf16[256,2048]{1,0:T(8,128)(2,1)}, s32[8,128]{1,0:T(8,128)}) custom-call(s32[8]{0:T(128)S(1)} %get-tuple-element.87.flags_ref, s32[8,128]{1,0:T(8,128)S(1)} %get-tuple-element.162.token_ref, bf16[4,256,128]{2,1,0:T(8,128)(2,1)S(1)} %get-tuple-element.163.qh_ref, ...), custom_call_target="tpu_custom_call", output_to_operand_aliasing={{0}: (6, {})} | custom-call | tf_op jit(solution)/shard_map/finish/pallas_call | solution.py:654
  (18 shorter events, 0.0 us)
Async XLA Ops:
  0.0 6.7 %copy-start = (bf16[512,2048]{1,0:T(8,128)(2,1)S(1)}, bf16[512,2048]{1,0:T(8,128)(2,1)}, u32[]{:S(2)}) copy-start(bf16[512,2048]{1,0:T(8,128)(2,1)} %key_ref.17) | copy-start | bytes 6291460
  0.0 4.8 %copy-start.8 = (s32[8,4]{0,1:T(4,128)S(1)}, s32[8,4]{0,1:T(4,128)}, u32[]{:S(2)}) copy-start(s32[8,4]{0,1:T(4,128)} %param.14) | copy-start | bytes 388
  0.0 4.8 %copy-start.7 = (f32[256,16]{0,1:T(8,128)S(1)}, f32[256,16]{0,1:T(8,128)}, u32[]{:S(2)}) copy-start(f32[256,16]{0,1:T(8,128)} %param.13) | copy-start | bytes 49156
  0.0 4.8 %copy-start.6 = (f32[512,16]{0,1:T(8,128)S(1)}, f32[512,16]{0,1:T(8,128)}, u32[]{:S(2)}) copy-start(f32[512,16]{0,1:T(8,128)} %param.12) | copy-start | bytes 98308
  0.0 6.6 %copy-start.3 = (f32[4,2048]{1,0:T(4,128)S(1)}, f32[4,2048]{1,0:T(4,128)}, u32[]{:S(2)}) copy-start(f32[4,2048]{1,0:T(4,128)} %key_kernel_ref.15) | copy-start | bytes 98308
  0.0 6.6 %copy-start.4 = (f32[4,2048]{1,0:T(4,128)S(1)}, f32[4,2048]{1,0:T(4,128)}, u32[]{:S(2)}) copy-start(f32[4,2048]{1,0:T(4,128)} %value_kernel_ref.7) | copy-start | bytes 98308
  1.1 5.5 %collective-permute-start = (bf16[9,2048]{1,0:T(8,128)(2,1)S(1)}, bf16[9,2048]{1,0:T(8,128)(2,1)S(1)}, u32[]{:S(2)}, u32[]{:S(2)}) collective-permute-start(bf16[9,2048]{1,0:T(8,128)(2,1)S(1)} %last_rows.1), channel_id=1, source_target_pairs={{0,1},{1,2},{2,3},{3,4},{4,5},{5,6},{6,7},{7,8},{8,9},{9,10},{10,1... | collective-permute-start | bytes 110600 | tf_op jit(solution)/shard_map/ppermute | solution.py:670
  6.7 1.6 %copy-start.1 = (bf16[512,2048]{1,0:T(8,128)(2,1)S(1)}, bf16[512,2048]{1,0:T(8,128)(2,1)}, u32[]{:S(2)}) copy-start(bf16[512,2048]{1,0:T(8,128)(2,1)} %value_ref.9) | copy-start | bytes 6291460
  16.9 10.3 %collective-permute-start.1 = (f32[4,128,256]{2,1,0:T(8,128)S(1)}, f32[4,128,256]{2,1,0:T(8,128)S(1)}, u32[]{:S(2)}, u32[]{:S(2)}) collective-permute-start(f32[4,128,256]{2,1,0:T(8,128)S(1)} %get-tuple-element.96), channel_id=1, source_target_pairs={{0,1},{1,0},{2,3},{3,2},{4,5},{5,4},{6,7},{7,6},{8,9},{9,8},{10,11... | collective-permute-start | bytes 1572872 | tf_op jit(solution)/shard_map/ppermute | solution.py:670
  28.1 18.2 %collective-permute-start.3 = (f32[4,128,256]{2,1,0:T(8,128)S(1)}, f32[4,128,256]{2,1,0:T(8,128)S(1)}, u32[]{:S(2)}, u32[]{:S(2)}) collective-permute-start(f32[4,128,256]{2,1,0:T(8,128)S(1)} %get-tuple-element.118), channel_id=1, source_target_pairs={{0,2},{1,3},{2,0},{3,1},{4,6},{5,7},{6,4},{7,5},{8,10},{9,11},{10,... | collective-permute-start | bytes 1572872 | tf_op jit(solution)/shard_map/ppermute | solution.py:670
  37.3 9.0 %collective-permute-start.2 = (f32[4,128,256]{2,1,0:T(8,128)S(1)}, f32[4,128,256]{2,1,0:T(8,128)S(1)}, u32[]{:S(2)}, u32[]{:S(2)}) collective-permute-start(f32[4,128,256]{2,1,0:T(8,128)S(1)} %get-tuple-element.117), channel_id=1, source_target_pairs={{0,1},{1,0},{2,3},{3,2},{4,5},{5,4},{6,7},{7,6},{8,9},{9,8},{10,11... | collective-permute-start | bytes 1572872 | tf_op jit(solution)/shard_map/ppermute | solution.py:670
  37.6 12.4 %copy-start.5 = (f32[4,2048]{1,0:T(4,128)S(1)}, f32[4,2048]{1,0:T(4,128)}, u32[]{:S(2)}) copy-start(f32[4,2048]{1,0:T(4,128)} %query_kernel_ref.7) | copy-start | bytes 98308
  46.3 3.8 %copy-start.2 = (bf16[256,2048]{1,0:T(8,128)(2,1)S(1)}, bf16[256,2048]{1,0:T(8,128)(2,1)}, u32[]{:S(2)}) copy-start(bf16[256,2048]{1,0:T(8,128)(2,1)} %query_ref.9) | copy-start | bytes 3145732
  47.4 6.8 %collective-permute-start.4 = (f32[2,128,128]{2,1,0:T(8,128)S(1)}, f32[2,128,128]{2,1,0:T(8,128)S(1)}, u32[]{:S(2)}, u32[]{:S(2)}) collective-permute-start(f32[2,128,128]{2,1,0:T(8,128)S(1)} %get-tuple-element.123), channel_id=1, source_target_pairs={{0,4},{1,5},{2,6},{3,7},{16,20},{17,21},{18,22},{19,23}} | collective-permute-start | bytes 393224 | tf_op jit(solution)/shard_map/ppermute | solution.py:670
  48.7 8.3 %collective-permute-start.5 = (f32[2,128,128]{2,1,0:T(8,128)S(1)}, f32[2,128,128]{2,1,0:T(8,128)S(1)}, u32[]{:S(2)}, u32[]{:S(2)}) collective-permute-start(f32[2,128,128]{2,1,0:T(8,128)S(1)} %get-tuple-element.127), channel_id=1, source_target_pairs={{0,4},{1,5},{2,6},{3,7},{16,20},{17,21},{18,22},{19,23}} | collective-permute-start | bytes 393224 | tf_op jit(solution)/shard_map/ppermute | solution.py:670
  54.9 7.8 %collective-permute-start.6 = (f32[2,128,128]{2,1,0:T(8,128)S(1)}, f32[2,128,128]{2,1,0:T(8,128)S(1)}, u32[]{:S(2)}, u32[]{:S(2)}) collective-permute-start(f32[2,128,128]{2,1,0:T(8,128)S(1)} %get-tuple-element.131), channel_id=1, source_target_pairs={{4,8},{5,9},{6,10},{7,11},{20,24},{21,25},{22,26},{23,27}} | collective-permute-start | bytes 393224 | tf_op jit(solution)/shard_map/ppermute | solution.py:670
  57.7 6.5 %collective-permute-start.7 = (f32[2,128,128]{2,1,0:T(8,128)S(1)}, f32[2,128,128]{2,1,0:T(8,128)S(1)}, u32[]{:S(2)}, u32[]{:S(2)}) collective-permute-start(f32[2,128,128]{2,1,0:T(8,128)S(1)} %get-tuple-element.134), channel_id=1, source_target_pairs={{4,8},{5,9},{6,10},{7,11},{20,24},{21,25},{22,26},{23,27}} | collective-permute-start | bytes 393224 | tf_op jit(solution)/shard_map/ppermute | solution.py:670
  63.5 6.1 %collective-permute-start.8 = (f32[2,128,128]{2,1,0:T(8,128)S(1)}, f32[2,128,128]{2,1,0:T(8,128)S(1)}, u32[]{:S(2)}, u32[]{:S(2)}) collective-permute-start(f32[2,128,128]{2,1,0:T(8,128)S(1)} %get-tuple-element.140), channel_id=1, source_target_pairs={{8,12},{9,13},{10,14},{11,15},{24,28},{25,29},{26,30},{27,31}} | collective-permute-start | bytes 393224 | tf_op jit(solution)/shard_map/ppermute | solution.py:670
  65.0 4.6 %collective-permute-start.9 = (f32[2,128,128]{2,1,0:T(8,128)S(1)}, f32[2,128,128]{2,1,0:T(8,128)S(1)}, u32[]{:S(2)}, u32[]{:S(2)}) collective-permute-start(f32[2,128,128]{2,1,0:T(8,128)S(1)} %get-tuple-element.141), channel_id=1, source_target_pairs={{8,12},{9,13},{10,14},{11,15},{24,28},{25,29},{26,30},{27,31}} | collective-permute-start | bytes 393224 | tf_op jit(solution)/shard_map/ppermute | solution.py:670
  70.7 7.6 %collective-permute-start.10 = (f32[4,128,128]{2,1,0:T(8,128)S(1)}, f32[4,128,128]{2,1,0:T(8,128)S(1)}, u32[]{:S(2)}, u32[]{:S(2)}) collective-permute-start(f32[4,128,128]{2,1,0:T(8,128)S(1)} %get-tuple-element.152), channel_id=1, source_target_pairs={{0,1},{1,0},{2,3},{3,2},{4,5},{5,4},{6,7},{7,6},{8,9},{9,8},{10,11... | collective-permute-start | bytes 786440 | tf_op jit(solution)/shard_map/ppermute | solution.py:670
  71.8 8.1 %collective-permute-start.11 = (f32[4,128,128]{2,1,0:T(8,128)S(1)}, f32[4,128,128]{2,1,0:T(8,128)S(1)}, u32[]{:S(2)}, u32[]{:S(2)}) collective-permute-start(f32[4,128,128]{2,1,0:T(8,128)S(1)} %get-tuple-element.155), channel_id=1, source_target_pairs={{0,2},{1,3},{2,0},{3,1},{4,6},{5,7},{6,4},{7,5},{8,10},{9,11},{10,... | collective-permute-start | bytes 786440 | tf_op jit(solution)/shard_map/ppermute | solution.py:670
  80.7 2.3 %collective-permute-start.12 = (f32[4,128,128]{2,1,0:T(8,128)S(1)}, f32[4,128,128]{2,1,0:T(8,128)S(1)}, u32[]{:S(2)}, u32[]{:S(2)}) collective-permute-start(f32[4,128,128]{2,1,0:T(8,128)S(1)} %get-tuple-element.166), channel_id=1, source_target_pairs={{0,1},{1,0},{2,3},{3,2},{4,5},{5,4},{6,7},{7,6},{8,9},{9,8},{10,11... | collective-permute-start | bytes 786440 | tf_op jit(solution)/shard_map/ppermute | solution.py:670
